TPU v7x, 512 devices: a whole 4x4x16 slice. The times are simulated.
512 devices in a mesh: sub: 32 (over y, x, core), node: 16 (over z).
Axes of the slice: x: 4, y: 4, z: 16, core: 2. Of those that a mesh axis runs over, the one named last changes fastest.
Arguments:
- node_tensor: bfloat16 [32, 16, 128, 128, 128], P('sub', 'node'), may hold values from -0.046875 to 0.046875
- outer_env: bfloat16 [32, 16, 2, 1, 128, 128], P('sub', 'node'), may hold values from -6 to 6
- upper_env: bfloat16 [32, 16, 1, 128, 128], P('sub', 'node'), may hold values from -6 to 6
- role_map: int32 [32, 16], P('sub'), may hold values from 0 to 15, each once within a row
- child_slots: int32 [32, 16], P('sub'), may hold values from -1 to 3, as said below
Outputs:
- mean_field: bfloat16 [32, 16, 1, 128, 128], P('sub', 'node')
Inputs may be any that keep to these rules, and one draw needn't show every extreme that they name: `role_map`: each group's row is a permutation of the roles 0 to 15. `child_slots`: each group's row names every lower node 0 to 3 exactly once; all other entries are -1.
All inputs are finite; a program needn't handle non-finite values.
Results may differ from a plain program's by a relative error of at most 0.012.
Values may be sent and summed in bfloat16 or wider, within the bound.
A program may use at most 64 MiB of HBM per device.

v0:
```python
import jax
import jax.numpy as jnp
from jax import lax
from jax.sharding import PartitionSpec as P

TERMS = 1


def from_behind(block, axis, distance):
    devices = range(lax.axis_size(axis))
    route = [((i - distance) % len(devices), i) for i in devices]
    return lax.ppermute(block, axis, route)


def node_up(tensor_here, left_env, right_env):
    first = jnp.einsum(
        "xa,abp->xbp", left_env, tensor_here, preferred_element_type=jnp.float32
    ).astype(jnp.bfloat16)
    second = jnp.einsum("yb,xbp->xyp", right_env, first, preferred_element_type=jnp.float32).astype(
        jnp.bfloat16
    )
    return jnp.einsum(
        "xyq,xyp->qp", tensor_here, second, preferred_element_type=jnp.float32
    ).astype(jnp.bfloat16)


def node_down(tensor_here, left_env, right_env, upper_here):
    weighted = jnp.einsum(
        "qp,abp->abq", upper_here, tensor_here, preferred_element_type=jnp.float32
    ).astype(jnp.bfloat16)
    right_part = jnp.einsum(
        "xyq,yb->xbq", tensor_here, right_env, preferred_element_type=jnp.float32
    ).astype(jnp.bfloat16)
    left_part = jnp.einsum(
        "xyq,xa->ayq", tensor_here, left_env, preferred_element_type=jnp.float32
    ).astype(jnp.bfloat16)
    first_child = jnp.einsum(
        "xbq,abq->xa", right_part, weighted, preferred_element_type=jnp.float32
    ).astype(jnp.bfloat16)
    second_child = jnp.einsum(
        "ayq,abq->yb", left_part, weighted, preferred_element_type=jnp.float32
    ).astype(jnp.bfloat16)
    return (first_child, second_child)


def placements(group_roles):
    group_size = group_roles.shape[0]
    spots = jnp.arange(group_size, dtype=jnp.int32)
    return jnp.sum(jnp.where(group_roles[None, :] == spots[:, None], spots[None, :], 0), axis=1)


def local(node_tensor, outer_env, upper_env, role_map, child_slots):
    tensor_here = node_tensor[0, 0]
    outer_envs = outer_env[0, 0]
    upper_envs = upper_env[0, 0]
    group_roles = role_map[0]
    child_links = child_slots[0]
    group_size = lax.axis_size("node")
    top_count = group_size // 4
    mid_count = 2 * top_count
    bond_size = tensor_here.shape[0]
    role_spot = placements(group_roles)
    position = lax.axis_index("node")
    my_role = group_roles[position]
    is_top = my_role < top_count
    is_mid = jnp.logical_and(my_role >= top_count, my_role < top_count + mid_count)
    is_leaf = my_role >= top_count + mid_count
    zero_envs = jnp.zeros((TERMS, bond_size, bond_size), jnp.bfloat16)

    def leaf_work():
        return jnp.stack([node_up(tensor_here, outer_envs[0, 0], outer_envs[1, 0])])

    leaf_up = lax.cond(is_leaf, leaf_work, lambda: zero_envs)
    leaf_spots = role_spot[top_count + mid_count :]
    every_leaf = lax.all_gather(leaf_up[None], "node", axis=0, tiled=True)
    leaf_table = jnp.take(every_leaf, leaf_spots, axis=0)
    mid_index = jnp.clip(my_role - top_count, 0, mid_count - 1)

    def mid_work():
        child_envs = []
        for branch in range(2):
            slot_link = child_links[2 * mid_index + branch]
            leaf_pick = leaf_table[jnp.maximum(slot_link, 0)]
            child_envs.append(jnp.where(slot_link >= 0, leaf_pick, outer_envs[branch]))
        return jnp.stack([node_up(tensor_here, child_envs[0][0], child_envs[1][0])])

    mid_up = lax.cond(is_mid, mid_work, lambda: zero_envs)
    mid_spots = role_spot[top_count : top_count + mid_count]
    every_mid = lax.all_gather(mid_up[None], "node", axis=0, tiled=True)
    mid_table = jnp.take(every_mid, mid_spots, axis=0)
    top_index = jnp.clip(my_role, 0, top_count - 1)
    next_half = from_behind(mid_table[top_count:], "sub", -1)
    right_envs = next_half[top_index]

    def top_work():
        left_env = mid_table[top_index]
        results = [node_down(tensor_here, left_env[0], right_envs[0], upper_envs[0])]
        return jnp.stack([jnp.stack([r[0] for r in results]), jnp.stack([r[1] for r in results])])

    top_down = lax.cond(
        is_top, top_work, lambda: jnp.zeros((2, TERMS, bond_size, bond_size), jnp.bfloat16)
    )
    top_spots = role_spot[:top_count]
    every_top = lax.all_gather(top_down[None], "node", axis=0, tiled=True)
    top_table = jnp.take(every_top, top_spots, axis=0)
    own_field = top_table[jnp.clip(mid_index, 0, top_count - 1), 0]
    from_before = from_behind(top_table[:, 1], "sub", 1)
    other_field = from_before[jnp.clip(mid_index - top_count, 0, top_count - 1)]
    mid_field = jnp.where(mid_index < top_count, own_field, other_field)
    result = jnp.where(is_mid, mid_field, jnp.where(is_leaf, leaf_up, zero_envs))
    return result[None, None]


def solution(mesh):
    return jax.shard_map(
        local,
        mesh=mesh,
        in_specs=(
            P("sub", "node", None, None, None),
            P("sub", "node", None, None, None, None),
            P("sub", "node", None, None, None),
            P("sub", None),
            P("sub", None),
        ),
        out_specs=P("sub", "node", None, None, None),
        check_vma=False,
    )
```

profile of v0, /device:TPU:24, one launch (start us, length us, event | category | flops | bytes accessed | tf_op | source)
XLA Modules:
  0.0 245.7 jit_solution(16495266926667430249)
XLA Ops:
  6.5 0.0 all-gather.5.cloned.1.call-start
  6.5 1.2 constant_dynamic-slice_fusion.2
  9.1 0.0 copy-start.6
  9.1 4.9 %copy.130 = bf16[1,1,128,128,128]{4,2,3,1,0:T(8,128)(2,1)S(1)} copy(bf16[1,1,128,128,128]{4,3,2,1,0:T(8,128)(2,1)} %param.11) | data formatting | bytes 8388608 | tf_op args[0]
  14.0 0.0 copy-start
  14.0 0.0 copy-done.6
  14.0 0.0 copy-start.9
  14.0 0.0 copy-start.8
  14.1 1.9 copy-done
  16.0 17.7 %conditional.3 = (bf16[1,128,128]{2,1,0:T(8,128)(2,1)S(1)}) conditional(s32[]{:T(128)} %convert_element_type.75, () %tuple.35, (bf16[2,1,128,128]{3,2,1,0:T(8,128)(2,1)S(1)}, bf16[128,128,128]{2,0,1:T(8,128)(2,1)S(1)}) %tuple.65), branch_computations={%region_1.2_spmd, %region_2.3_spmd} | conditional | flops 1614823424 | bytes 33718308 | solution.py:73
  16.1 0.0 copy-start.1
  16.1 2.0 copy-done.1
  18.1 3.2 %convolution_convert_fusion = bf16[128,128,128]{2,0,1:T(8,128)(2,1)} fusion(bf16[128,128,128]{2,0,1:T(8,128)(2,1)S(1)} %get-tuple-element.182, bf16[2,1,128,128]{3,2,1,0:T(8,128)(2,1)S(1)} %get-tuple-element.140), kind=kOutput, calls=%fused_computation.9 | convolution fusion | flops 538968064 | bytes 8421376 | tf_op jit(solution)/shard_map/cond/branch_1_fun/xa,abp->xbp/dot_general | solution.py:16
  21.3 12.2 %fusion.24 = bf16[1,128,128]{1,2,0:T(8,128)(2,1)S(1)} fusion(bf16[128,128,128]{2,0,1:T(8,128)(2,1)} %copy-done.1, bf16[128,128,128]{2,0,1:T(8,128)(2,1)} %convolution_convert_fusion, bf16[2,1,128,128]{3,2,1,0:T(8,128)(2,1)S(1)} %get-tuple-element.140), kind=kOutput, calls=%fused_computation.12 | convolution fusion | flops 1075855360 | bytes 8454144 | tf_op jit(solution)/shard_map/cond/branch_1_fun/xyq,xyp->qp/dot_general | solution.py:22
  33.5 0.1 copy.56
  33.6 37.7 %all-gather = bf16[16,128,128]{2,1,0:T(8,128)(2,1)S(1)} all-gather(bf16[1,128,128]{2,1,0:T(8,128)(2,1)S(1)} %get-tuple-element.195), channel_id=2, replica_groups=mesh['sub'=32,'node'=16] {'node'}, dimensions={0}, use_global_device_ids=true | all-gather | bytes 557056 | tf_op jit(solution)/shard_map/all_gather | solution.py:75
  72.0 0.0 copy-done.9
  72.0 0.1 select_reduce_fusion
  72.8 0.1 compare_and_fusion.1
  72.9 0.0 copy-done.8
  72.9 0.0 copy-start.7
  72.9 0.2 conditional.4
  73.1 0.1 copy.51
  73.2 50.7 %all-gather.1 = bf16[16,128,128]{2,1,0:T(8,128)(2,1)S(1)} all-gather(bf16[1,128,128]{2,1,0:T(8,128)(2,1)S(1)} %copy.51), channel_id=3, replica_groups=mesh['sub'=32,'node'=16] {'node'}, dimensions={0}, use_global_device_ids=true | all-gather | bytes 557056 | tf_op jit(solution)/shard_map/all_gather | solution.py:89
  123.9 0.6 gather_fusion.1
  124.5 0.1 bitcast_select_fusion.2
  124.6 1.9 collective-permute-start
  127.2 1.9 collective-permute-done
  129.1 0.0 copy-done.7
  129.1 1.3 conditional.5
  130.4 0.0 copy-start.5
  130.4 0.6 copy-done.5
  131.0 0.0 all-gather.5.cloned.1.call-update
  131.1 96.3 %all-gather.5.cloned.1.call-done = bf16[32,1,128,128]{3,2,1,0:T(8,128)(2,1)} async-done(((bf16[2,1,128,128]{3,2,1,0:T(8,128)(2,1)}), bf16[32,1,128,128]{3,2,1,0:T(8,128)(2,1)}) %all-gather.5.cloned.1.call-update) | async-done | bytes 1048592 | tf_op jit(solution)/shard_map/all_gather | solution.py:104
  227.4 1.8 gather_fusion.2
  229.2 0.1 bitcast_select_fusion.1
  229.3 1.9 collective-permute-start.1
  231.3 6.5 %collective-permute-done.1 = bf16[4,1,128,128]{3,2,0,1:T(8,128)(2,1)S(1)} collective-permute-done((bf16[4,1,128,128]{3,2,0,1:T(8,128)(2,1)S(1)}, bf16[4,1,128,128]{3,2,0,1:T(8,128)(2,1)S(1)}, u32[]{:S(2)}, u32[]{:S(2)}) %collective-permute-start.1) | collective-permute-done | bytes 131104 | tf_op jit(solution)/shard_map/ppermute | solution.py:12
  237.7 0.6 fusion.132
  (8 shorter events, 0.1 us)
Async XLA Ops:
  6.5 220.9 %all-gather.5.cloned.1.call-start = ((), (), s32[]{:S(2)}) async-start(), calls=%async_computation | async-start | bytes 1114112 | tf_op jit(solution)/shard_map/all_gather | solution.py:104
  9.1 4.9 %copy-start.6 = (bf16[1,1,2,1,128,128]{5,4,3,2,1,0:T(8,128)(2,1)S(1)}, bf16[1,1,2,1,128,128]{5,4,3,2,1,0:T(8,128)(2,1)}, u32[]{:S(2)}) copy-start(bf16[1,1,2,1,128,128]{5,4,3,2,1,0:T(8,128)(2,1)} %param.12) | copy-start | bytes 196612
  14.0 1.9 copy-start
  14.0 58.0 %copy-start.9 = (s32[1,16]{1,0:T(1,128)S(1)}, s32[1,16]{1,0:T(1,128)}, u32[]{:S(2)}) copy-start(s32[1,16]{1,0:T(1,128)} %param.14) | copy-start | bytes 196
  14.0 58.8 %copy-start.8 = (s32[1,16]{1,0:T(1,128)S(1)}, s32[1,16]{1,0:T(1,128)}, u32[]{:S(2)}) copy-start(s32[1,16]{1,0:T(1,128)} %param.15) | copy-start | bytes 196
  16.1 2.0 copy-start.1
  72.9 56.2 %copy-start.7 = (bf16[1,1,1,128,128]{4,3,2,1,0:T(8,128)(2,1)S(1)}, bf16[1,1,1,128,128]{4,3,2,1,0:T(8,128)(2,1)}, u32[]{:S(2)}) copy-start(bf16[1,1,1,128,128]{4,3,2,1,0:T(8,128)(2,1)} %param.13) | copy-start | bytes 98308
  124.6 4.4 %collective-permute-start = (bf16[4,1,128,128]{3,2,0,1:T(8,128)(2,1)S(1)}, bf16[4,1,128,128]{3,2,0,1:T(8,128)(2,1)S(1)}, u32[]{:S(2)}, u32[]{:S(2)}) collective-permute-start(bf16[4,1,128,128]{3,2,0,1:T(8,128)(2,1)S(1)} %slice.43), channel_id=1, source_target_pairs={{16,0},{32,16},{48,32},{64,48},{80,64},{96,80},{112,96},{128,112},... | collective-permute-start | bytes 393224 | tf_op jit(solution)/shard_map/ppermute | solution.py:12
  130.4 0.6 copy-start.5
  229.3 8.4 %collective-permute-start.1 = (bf16[4,1,128,128]{3,2,0,1:T(8,128)(2,1)S(1)}, bf16[4,1,128,128]{3,2,0,1:T(8,128)(2,1)S(1)}, u32[]{:S(2)}, u32[]{:S(2)}) collective-permute-start(bf16[4,1,128,128]{3,2,0,1:T(8,128)(2,1)S(1)} %slice_bitcast_fusion), channel_id=1, source_target_pairs={{496,0},{0,16},{16,32},{32,48},{48,64},{64,80},{80,96},{96,112},{1... | collective-permute-start | bytes 393224 | tf_op jit(solution)/shard_map/ppermute | solution.py:12
Sparse Core Ops, SparseCore 0:
  131.2 96.1 all-gather.4
where the time goes:
time: 250 us; the launch traced here: 246 us
  waiting for transfers between devices  105 us (42%)
  blocking collectives  88.4 us (35%)
  between operations  17.3 us (7%)
  matrix products  15.4 us (6%)
  local copies, waits for them, and re-layouts  13.4 us (5%)
  starting transfers between devices  3.84 us (2%)
    all_gather x1, waiting for transfers between devices, local(): every_top = lax.all_gather(top_down[None], 'node', axis=0, tiled=True)  96.3 us
    all_gather x1, blocking collectives, local(): every_mid = lax.all_gather(mid_up[None], 'node', axis=0, tiled=True)  50.7 us
    all_gather x1, blocking collectives, local(): every_leaf = lax.all_gather(leaf_up[None], 'node', axis=0, tiled=True)  37.7 us
    dot_general x1, matrix products, node_up(): jnp.einsum('xyq,xyp->qp', tensor_here, second, preferred_element_type=jnp...  12.2 us
    ppermute x2, waiting for transfers between devices, from_behind(): return lax.ppermute(block, axis, route)  8.3 us
    unnamed x13, local copies, waits for them, and re-layouts  7.46 us
  transfers between devices with their start and end apart: 3, of which 3 were waited for; matrix products, arithmetic and copies ran while one was open for 0% of the time, Pallas kernels for 0%

commit v1 on v0

--- a/solution.py
+++ b/solution.py
@@ -1,15 +1,71 @@
+import functools
+
 import jax
 import jax.numpy as jnp
 from jax import lax
+from jax.experimental import pallas as pl
+from jax.experimental.pallas import tpu as pltpu
 from jax.sharding import PartitionSpec as P
 
 TERMS = 1
+MESH = pl.DeviceIdType.MESH
 
 
 def from_behind(block, axis, distance):
     devices = range(lax.axis_size(axis))
     route = [((i - distance) % len(devices), i) for i in devices]
     return lax.ppermute(block, axis, route)
+
+
+def gather_kernel(n, x_ref, out_ref, send_sem, recv_sem, own_sem):
+    me = lax.axis_index("node")
+    group = lax.axis_index("sub")
+    barrier = pltpu.get_barrier_semaphore()
+    for d in range(1, n):
+        pl.semaphore_signal(barrier, inc=1, device_id=(group, lax.rem(me + d, n)), device_id_type=MESH)
+    pl.semaphore_wait(barrier, n - 1)
+    own = pltpu.make_async_copy(x_ref, out_ref.at[me], own_sem)
+    own.start()
+    copies = []
+    for d in range(1, n):
+        copy = pltpu.make_async_remote_copy(
+            src_ref=x_ref,
+            dst_ref=out_ref.at[me],
+            send_sem=send_sem.at[d - 1],
+            recv_sem=recv_sem.at[d - 1],
+            device_id=(group, lax.rem(me + d, n)),
+            device_id_type=MESH,
+        )
+        copy.start()
+        copies.append(copy)
+    for copy in copies:
+        copy.wait_send()
+    for d in range(1, n):
+        pltpu.make_async_remote_copy(
+            src_ref=x_ref,
+            dst_ref=out_ref.at[lax.rem(me + n - d, n)],
+            send_sem=send_sem.at[d - 1],
+            recv_sem=recv_sem.at[d - 1],
+            device_id=(group, lax.rem(me + n - d, n)),
+            device_id_type=MESH,
+        ).wait_recv()
+    own.wait()
+
+
+def node_gather(block, collective_id):
+    n = lax.axis_size("node")
+    return pl.pallas_call(
+        functools.partial(gather_kernel, n),
+        out_shape=jax.ShapeDtypeStruct((n,) + block.shape, block.dtype),
+        in_specs=[pl.BlockSpec(memory_space=pl.ANY)],
+        out_specs=pl.BlockSpec(memory_space=pl.ANY),
+        scratch_shapes=[
+            pltpu.SemaphoreType.DMA((n - 1,)),
+            pltpu.SemaphoreType.DMA((n - 1,)),
+            pltpu.SemaphoreType.DMA,
+        ],
+        compiler_params=pltpu.CompilerParams(collective_id=collective_id, has_side_effects=True),
+    )(block)
 
 
 def node_up(tensor_here, left_env, right_env):
@@ -72,7 +128,7 @@
 
     leaf_up = lax.cond(is_leaf, leaf_work, lambda: zero_envs)
     leaf_spots = role_spot[top_count + mid_count :]
-    every_leaf = lax.all_gather(leaf_up[None], "node", axis=0, tiled=True)
+    every_leaf = node_gather(leaf_up, 0)
     leaf_table = jnp.take(every_leaf, leaf_spots, axis=0)
     mid_index = jnp.clip(my_role - top_count, 0, mid_count - 1)
 
@@ -86,7 +142,7 @@
 
     mid_up = lax.cond(is_mid, mid_work, lambda: zero_envs)
     mid_spots = role_spot[top_count : top_count + mid_count]
-    every_mid = lax.all_gather(mid_up[None], "node", axis=0, tiled=True)
+    every_mid = node_gather(mid_up, 1)
     mid_table = jnp.take(every_mid, mid_spots, axis=0)
     top_index = jnp.clip(my_role, 0, top_count - 1)
     next_half = from_behind(mid_table[top_count:], "sub", -1)
@@ -101,7 +157,7 @@
         is_top, top_work, lambda: jnp.zeros((2, TERMS, bond_size, bond_size), jnp.bfloat16)
     )
     top_spots = role_spot[:top_count]
-    every_top = lax.all_gather(top_down[None], "node", axis=0, tiled=True)
+    every_top = node_gather(top_down, 2)
     top_table = jnp.take(every_top, top_spots, axis=0)
     own_field = top_table[jnp.clip(mid_index, 0, top_count - 1), 0]
     from_before = from_behind(top_table[:, 1], "sub", 1)

time: 250 us -> 207 us (0.83)
  the two profiles are of different devices: /device:TPU:24 before, /device:TPU:64 now
where the time goes in v1:
time: 207 us
  Pallas kernels  160 us (77%)
  matrix products  17 us (8%)
  starting transfers between devices  9.91 us (5%)
  waiting for transfers between devices  9.48 us (5%)
  local copies, waits for them, and re-layouts  5.45 us (3%)
  between operations  2.94 us (1%)
    pallas_call x3, Pallas kernels, node_gather(): pl.pallas_call(functools.partial(gather_kernel, n), out_shape=jax.ShapeDt...  160 us
    ppermute x2, starting transfers between devices, from_behind(): return lax.ppermute(block, axis, route)  9.91 us
    ppermute x2, waiting for transfers between devices, from_behind(): return lax.ppermute(block, axis, route)  9.48 us
    dot_general x1, matrix products, node_down(): jnp.einsum('xyq,xa->ayq', tensor_here, left_env, preferred_element_type=j...  5.72 us
    dot_general x1, matrix products, node_down(): jnp.einsum('xbq,abq->xa', right_part, weighted, preferred_element_type=jn...  4.65 us
  transfers between devices with their start and end apart: 2, of which 2 were waited for; matrix products, arithmetic and copies ran while one was open for 0% of the time, Pallas kernels for 0%

profile of v1, /device:TPU:64, one launch (start us, length us, event | category | flops | bytes accessed | tf_op | source)
XLA Modules:
  0.0 206.8 jit_solution(4182748271715362292)
XLA Ops:
  0.0 1.2 constant_dynamic-slice_fusion.2
  2.3 0.0 copy-start.5
  2.3 0.0 copy-start.4
  2.4 53.2 %shard_map.57 = bf16[16,1,128,128]{3,2,1,0:T(8,128)(2,1)S(1)} custom-call(bf16[1,128,128]{2,1,0:T(8,128)(2,1)S(1)} %get-tuple-element.172.x_ref), custom_call_target="tpu_custom_call" | custom-call | tf_op jit(solution)/shard_map/pallas_call | solution.py:57
  56.2 0.0 copy-done.5
  56.2 0.1 select_reduce_fusion
  56.9 0.1 compare_and_fusion.1
  56.9 0.0 copy-done.4
  56.9 0.0 copy-start.3
  56.9 0.2 conditional.4
  57.2 0.7 copy.18.x_ref
  57.9 50.8 %shard_map.58 = bf16[16,1,128,128]{3,2,1,0:T(8,128)(2,1)} custom-call(bf16[1,128,128]{2,1,0:T(8,128)(2,1)} %copy.18.x_ref), custom_call_target="tpu_custom_call" | custom-call | tf_op jit(solution)/shard_map/pallas_call | solution.py:57
  108.7 1.6 gather_fusion.1
  110.4 0.1 bitcast_select_fusion.2
  110.5 7.9 %collective-permute-start = (bf16[4,1,128,128]{3,2,0,1:T(8,128)(2,1)S(1)}, bf16[4,1,128,128]{3,2,0,1:T(8,128)(2,1)S(1)}, u32[]{:S(2)}, u32[]{:S(2)}) collective-permute-start(bf16[4,1,128,128]{3,2,0,1:T(8,128)(2,1)S(1)} %slice.45), channel_id=1, source_target_pairs={{16,0},{32,16},{48,32},{64,48},{80,64},{96,80},{112,96},{128,112},... | collective-permute-start | bytes 393224 | tf_op jit(solution)/shard_map/ppermute | solution.py:17
  119.0 1.9 collective-permute-done
  120.9 0.0 copy-done.3
  120.9 17.7 %conditional.5 = (bf16[2,1,128,128]{3,2,1,0:T(8,128)(2,1)S(1)}) conditional(s32[]{:T(128)} %convert_element_type.73, () %tuple.33, (s32[]{:T(128)}, bf16[4,1,128,128]{3,2,0,1:T(8,128)(2,1)S(1)}, bf16[128,128,128]{2,1,0:T(8,128)(2,1)}, bf16[1,1,1,128,128]{4,3,2,1,0:T(8,128)(2,1)S(1)}, bf16[8,1,128,128]{3,2,0,1:T(8,128)(2,1)S(1)}) %tuple.59), branch_computations={%region_5.6_spmd, %region_6.7_spmd} | conditional | flops 2686517248 | bytes 59015236 | solution.py:156
  121.5 0.0 copy-start
  121.5 5.7 %fusion.19 = bf16[128,128,128]{2,0,1:T(8,128)(2,1)S(1)} fusion(bf16[128,128,128]{2,1,0:T(8,128)(2,1)} %get-tuple-element.151, bf16[8,1,128,128]{3,2,1,0:T(8,128)(2,1)S(1)} %bitcast.143, s32[]{:T(128)S(6)} %min.10), kind=kOutput, calls=%fused_computation.20 | convolution fusion | flops 536870912 | bytes 8421380 | tf_op jit(solution)/shard_map/cond/branch_1_fun/xyq,xa->ayq/dot_general | solution.py:90
  127.2 0.0 copy-done
  127.2 1.2 convolution_convert_fusion
  128.5 4.1 %fusion.34 = bf16[1,1,128,128]{3,2,1,0:T(8,128)(2,1)S(1)} fusion(bf16[128,128,128]{2,1,0:T(8,128)(2,1)S(1)} %convolution_convert_fusion, bf16[128,128,128]{2,0,1:T(8,128)(2,1)S(1)} %fusion.19), kind=kOutput, calls=%fused_computation.28 | convolution fusion | flops 536887296 | bytes 8421376 | tf_op jit(solution)/shard_map/cond/branch_1_fun/ayq,abq->yb/dot_general | solution.py:96
  132.6 1.3 fusion.42
  133.9 4.6 %fusion.35 = bf16[1,1,128,128]{3,2,1,0:T(8,128)(2,1)S(1)} fusion(bf16[128,128,128]{2,1,0:T(8,128)(2,1)S(1)} %convolution_convert_fusion, bf16[128,128,128]{2,0,1:T(8,128)(2,1)S(1)} %fusion.42), kind=kOutput, calls=%fused_computation.29 | convolution fusion | flops 536887296 | bytes 8421376 | tf_op jit(solution)/shard_map/cond/branch_1_fun/xbq,abq->xa/dot_general | solution.py:93
  138.6 56.0 %shard_map.59 = bf16[16,2,1,128,128]{4,3,2,1,0:T(8,128)(2,1)} custom-call(bf16[2,1,128,128]{3,2,1,0:T(8,128)(2,1)S(1)} %get-tuple-element.182.x_ref), custom_call_target="tpu_custom_call" | custom-call | tf_op jit(solution)/shard_map/pallas_call | solution.py:57
  194.6 1.8 gather_fusion.2
  196.4 0.1 bitcast_select_fusion.1
  196.5 2.0 collective-permute-start.1
  198.6 7.6 %collective-permute-done.1 = bf16[4,1,128,128]{3,2,0,1:T(8,128)(2,1)S(1)} collective-permute-done((bf16[4,1,128,128]{3,2,0,1:T(8,128)(2,1)S(1)}, bf16[4,1,128,128]{3,2,0,1:T(8,128)(2,1)S(1)}, u32[]{:S(2)}, u32[]{:S(2)}) %collective-permute-start.1) | collective-permute-done | bytes 131104 | tf_op jit(solution)/shard_map/ppermute | solution.py:17
  206.1 0.6 fusion.82
  (10 shorter events, 0.1 us)
Async XLA Ops:
  2.3 53.9 %copy-start.5 = (s32[1,16]{1,0:T(1,128)S(1)}, s32[1,16]{1,0:T(1,128)}, u32[]{:S(2)}) copy-start(s32[1,16]{1,0:T(1,128)} %param.14) | copy-start | bytes 196
  2.3 54.6 %copy-start.4 = (s32[1,16]{1,0:T(1,128)S(1)}, s32[1,16]{1,0:T(1,128)}, u32[]{:S(2)}) copy-start(s32[1,16]{1,0:T(1,128)} %param.15) | copy-start | bytes 196
  56.9 64.0 %copy-start.3 = (bf16[1,1,1,128,128]{4,3,2,1,0:T(8,128)(2,1)S(1)}, bf16[1,1,1,128,128]{4,3,2,1,0:T(8,128)(2,1)}, u32[]{:S(2)}) copy-start(bf16[1,1,1,128,128]{4,3,2,1,0:T(8,128)(2,1)} %param.13) | copy-start | bytes 98308
  110.5 10.4 %collective-permute-start = (bf16[4,1,128,128]{3,2,0,1:T(8,128)(2,1)S(1)}, bf16[4,1,128,128]{3,2,0,1:T(8,128)(2,1)S(1)}, u32[]{:S(2)}, u32[]{:S(2)}) collective-permute-start(bf16[4,1,128,128]{3,2,0,1:T(8,128)(2,1)S(1)} %slice.45), channel_id=1, source_target_pairs={{16,0},{32,16},{48,32},{64,48},{80,64},{96,80},{112,96},{128,112},... | collective-permute-start | bytes 393224 | tf_op jit(solution)/shard_map/ppermute | solution.py:17
  121.5 5.7 %copy-start = (bf16[128,128,128]{2,1,0:T(8,128)(2,1)S(1)}, bf16[128,128,128]{2,1,0:T(8,128)(2,1)}, u32[]{:S(2)}) copy-start(bf16[128,128,128]{2,1,0:T(8,128)(2,1)} %get-tuple-element.151) | copy-start | bytes 12582916 | tf_op jit(solution)/shard_map/cond
  196.5 9.6 %collective-permute-start.1 = (bf16[4,1,128,128]{3,2,0,1:T(8,128)(2,1)S(1)}, bf16[4,1,128,128]{3,2,0,1:T(8,128)(2,1)S(1)}, u32[]{:S(2)}, u32[]{:S(2)}) collective-permute-start(bf16[4,1,128,128]{3,2,0,1:T(8,128)(2,1)S(1)} %slice_bitcast_fusion.5), channel_id=1, source_target_pairs={{496,0},{0,16},{16,32},{32,48},{48,64},{64,80},{80,96},{96,112},{1... | collective-permute-start | bytes 393224 | tf_op jit(solution)/shard_map/ppermute | solution.py:17

commit v2 on v1

--- a/solution.py
+++ b/solution.py
@@ -20,35 +20,42 @@
 def gather_kernel(n, x_ref, out_ref, send_sem, recv_sem, own_sem):
     me = lax.axis_index("node")
     group = lax.axis_index("sub")
+    right = lax.rem(me + 1, n)
+    left = lax.rem(me + n - 1, n)
     barrier = pltpu.get_barrier_semaphore()
-    for d in range(1, n):
-        pl.semaphore_signal(barrier, inc=1, device_id=(group, lax.rem(me + d, n)), device_id_type=MESH)
-    pl.semaphore_wait(barrier, n - 1)
+    for neighbour in (left, right):
+        pl.semaphore_signal(barrier, inc=1, device_id=(group, neighbour), device_id_type=MESH)
+    pl.semaphore_wait(barrier, 2)
     own = pltpu.make_async_copy(x_ref, out_ref.at[me], own_sem)
     own.start()
-    copies = []
-    for d in range(1, n):
-        copy = pltpu.make_async_remote_copy(
-            src_ref=x_ref,
-            dst_ref=out_ref.at[me],
-            send_sem=send_sem.at[d - 1],
-            recv_sem=recv_sem.at[d - 1],
-            device_id=(group, lax.rem(me + d, n)),
+    ways = ((0, 1, right, n // 2), (1, -1, left, n - 1 - n // 2))
+
+    def hop(way, sign, target, step, origin):
+        return pltpu.make_async_remote_copy(
+            src_ref=x_ref if step == 0 else out_ref.at[origin],
+            dst_ref=out_ref.at[origin],
+            send_sem=send_sem.at[way, step],
+            recv_sem=recv_sem.at[way, step],
+            device_id=(group, target),
             device_id_type=MESH,
         )
-        copy.start()
-        copies.append(copy)
-    for copy in copies:
+
+    sent = []
+    for step in range(n // 2):
+        for way, sign, target, steps in ways:
+            if step >= steps:
+                continue
+            origin = lax.rem(me - sign * step + 2 * n, n)
+            if step > 0:
+                hop(way, sign, target, step - 1, origin).wait_recv()
+            copy = hop(way, sign, target, step, origin)
+            copy.start()
+            sent.append(copy)
+    for way, sign, target, steps in ways:
+        origin = lax.rem(me - sign * steps + 2 * n, n)
+        hop(way, sign, target, steps - 1, origin).wait_recv()
+    for copy in sent:
         copy.wait_send()
-    for d in range(1, n):
-        pltpu.make_async_remote_copy(
-            src_ref=x_ref,
-            dst_ref=out_ref.at[lax.rem(me + n - d, n)],
-            send_sem=send_sem.at[d - 1],
-            recv_sem=recv_sem.at[d - 1],
-            device_id=(group, lax.rem(me + n - d, n)),
-            device_id_type=MESH,
-        ).wait_recv()
     own.wait()
 
 
@@ -60,8 +67,8 @@
         in_specs=[pl.BlockSpec(memory_space=pl.ANY)],
         out_specs=pl.BlockSpec(memory_space=pl.ANY),
         scratch_shapes=[
-            pltpu.SemaphoreType.DMA((n - 1,)),
-            pltpu.SemaphoreType.DMA((n - 1,)),
+            pltpu.SemaphoreType.DMA((2, n // 2)),
+            pltpu.SemaphoreType.DMA((2, n // 2)),
             pltpu.SemaphoreType.DMA,
         ],
         compiler_params=pltpu.CompilerParams(collective_id=collective_id, has_side_effects=True),

time: 207 us -> 173 us (0.84)
  the two profiles are of different devices: /device:TPU:64 before, /device:TPU:24 now
where the time goes in v2:
time: 173 us; the launch traced here: 170 us
  Pallas kernels  132 us (76%)
  matrix products  16.5 us (10%)
  waiting for transfers between devices  8.38 us (5%)
  local copies, waits for them, and re-layouts  5.57 us (3%)
  starting transfers between devices  3.84 us (2%)
  between operations  2.94 us (2%)
    pallas_call x3, Pallas kernels, node_gather(): pl.pallas_call(functools.partial(gather_kernel, n), out_shape=jax.ShapeDt...  132 us
    dot_general x1, matrix products, node_up(): jnp.einsum('xyq,xyp->qp', tensor_here, second, preferred_element_type=jnp...  8.89 us
    ppermute x2, waiting for transfers between devices, from_behind(): return lax.ppermute(block, axis, route)  8.38 us
    dot_general x1, matrix products, node_up(): jnp.einsum('xa,abp->xbp', left_env, tensor_here, preferred_element_type=j...  7.6 us
    ppermute x2, starting transfers between devices, from_behind(): return lax.ppermute(block, axis, route)  3.84 us
  transfers between devices with their start and end apart: 2, of which 2 were waited for; matrix products, arithmetic and copies ran while one was open for 0% of the time, Pallas kernels for 0%

profile of v2, /device:TPU:24, one launch (start us, length us, event | category | flops | bytes accessed | tf_op | source)
XLA Modules:
  0.0 170.3 jit_solution(2694485670265288146)
XLA Ops:
  0.0 1.2 constant_dynamic-slice_fusion.2
  2.3 0.0 copy-start.5
  2.3 0.0 copy-start.4
  2.3 16.6 %conditional.3 = (bf16[1,128,128]{2,1,0:T(8,128)(2,1)S(1)}) conditional(s32[]{:T(128)} %convert_element_type.75, () %tuple.35, (bf16[2,1,128,128]{3,2,0,1:T(8,128)(2,1)}, bf16[128,128,128]{2,1,0:T(8,128)(2,1)}) %tuple.57), branch_computations={%region_1.2_spmd, %region_2.3_spmd} | conditional | flops 1612726272 | bytes 17203236 | solution.py:136
  2.4 0.0 copy-start.1
  2.4 7.6 %fusion.3 = bf16[128,128,128]{2,0,1:T(8,128)(2,1)} fusion(bf16[128,128,128]{2,1,0:T(8,128)(2,1)} %get-tuple-element.141, bf16[2,1,128,128]{3,2,1,0:T(8,128)(2,1)} %bitcast.146), kind=kOutput, calls=%fused_computation.7 | convolution fusion | flops 536870912 | bytes 8421376 | tf_op jit(solution)/shard_map/cond/branch_1_fun/xa,abp->xbp/dot_general | solution.py:79
  10.0 0.0 copy-done.1
  10.0 8.9 %fusion.12 = bf16[1,128,128]{1,2,0:T(8,128)(2,1)S(1)} fusion(bf16[128,128,128]{2,1,0:T(8,128)(2,1)} %get-tuple-element.141, bf16[128,128,128]{2,0,1:T(8,128)(2,1)} %fusion.3, bf16[2,1,128,128]{3,2,1,0:T(8,128)(2,1)S(1)} %bitcast.147), kind=kOutput, calls=%fused_computation.12 | convolution fusion | flops 1075855360 | bytes 8454144 | tf_op jit(solution)/shard_map/cond/branch_1_fun/xyq,xyp->qp/dot_general | solution.py:85
  18.9 0.1 copy.30
  19.0 35.0 %shard_map.57 = bf16[16,1,128,128]{3,2,1,0:T(8,128)(2,1)S(1)} custom-call(bf16[1,128,128]{2,1,0:T(8,128)(2,1)S(1)} %get-tuple-element.172.x_ref), custom_call_target="tpu_custom_call" | custom-call | tf_op jit(solution)/shard_map/pallas_call | solution.py:64
  54.6 0.0 copy-done.5
  54.6 0.1 select_reduce_fusion
  55.2 0.1 compare_and_fusion.1
  55.3 0.0 copy-done.4
  55.3 0.0 copy-start.3
  55.3 0.2 conditional.4
  55.6 0.7 copy.18.x_ref
  56.3 50.1 %shard_map.58 = bf16[16,1,128,128]{3,2,1,0:T(8,128)(2,1)} custom-call(bf16[1,128,128]{2,1,0:T(8,128)(2,1)} %copy.18.x_ref), custom_call_target="tpu_custom_call" | custom-call | tf_op jit(solution)/shard_map/pallas_call | solution.py:64
  106.4 1.6 gather_fusion.1
  108.0 0.1 bitcast_select_fusion.2
  108.2 1.9 %collective-permute-start = (bf16[4,1,128,128]{3,2,0,1:T(8,128)(2,1)S(1)}, bf16[4,1,128,128]{3,2,0,1:T(8,128)(2,1)S(1)}, u32[]{:S(2)}, u32[]{:S(2)}) collective-permute-start(bf16[4,1,128,128]{3,2,0,1:T(8,128)(2,1)S(1)} %slice.45), channel_id=1, source_target_pairs={{16,0},{32,16},{48,32},{64,48},{80,64},{96,80},{112,96},{128,112},... | collective-permute-start | bytes 393224 | tf_op jit(solution)/shard_map/ppermute | solution.py:17
  110.7 1.9 %collective-permute-done = bf16[4,1,128,128]{3,2,0,1:T(8,128)(2,1)S(1)} collective-permute-done((bf16[4,1,128,128]{3,2,0,1:T(8,128)(2,1)S(1)}, bf16[4,1,128,128]{3,2,0,1:T(8,128)(2,1)S(1)}, u32[]{:S(2)}, u32[]{:S(2)}) %collective-permute-start) | collective-permute-done | bytes 131104 | tf_op jit(solution)/shard_map/ppermute | solution.py:17
  112.6 0.0 copy-done.3
  112.6 46.7 %shard_map.59 = bf16[16,2,1,128,128]{4,3,2,1,0:T(8,128)(2,1)} custom-call(bf16[2,1,128,128]{3,2,1,0:T(8,128)(2,1)S(1)} %get-tuple-element.182.x_ref), custom_call_target="tpu_custom_call" | custom-call | tf_op jit(solution)/shard_map/pallas_call | solution.py:64
  159.3 1.8 %gather_fusion.2 = bf16[4,2,128,128]{3,2,1,0:T(8,128)(2,1)S(1)} fusion(bf16[16,2,128,128]{3,2,1,0:T(8,128)(2,1)} %bitcast.140, s32[1024]{0:T(1024)S(1)} %pad_clamp_fusion.1), kind=kCustom, calls=%fused_computation.2 | custom fusion | bytes 524304 | tf_op jit(solution)/shard_map/jit(_take)/gather | solution.py:168
  161.2 0.1 bitcast_select_fusion.1
  161.3 1.9 %collective-permute-start.1 = (bf16[4,1,128,128]{3,2,0,1:T(8,128)(2,1)S(1)}, bf16[4,1,128,128]{3,2,0,1:T(8,128)(2,1)S(1)}, u32[]{:S(2)}, u32[]{:S(2)}) collective-permute-start(bf16[4,1,128,128]{3,2,0,1:T(8,128)(2,1)S(1)} %slice_bitcast_fusion.5), channel_id=1, source_target_pairs={{496,0},{0,16},{16,32},{32,48},{48,64},{64,80},{80,96},{96,112},{1... | collective-permute-start | bytes 393224 | tf_op jit(solution)/shard_map/ppermute | solution.py:17
  163.2 6.5 %collective-permute-done.1 = bf16[4,1,128,128]{3,2,0,1:T(8,128)(2,1)S(1)} collective-permute-done((bf16[4,1,128,128]{3,2,0,1:T(8,128)(2,1)S(1)}, bf16[4,1,128,128]{3,2,0,1:T(8,128)(2,1)S(1)}, u32[]{:S(2)}, u32[]{:S(2)}) %collective-permute-start.1) | collective-permute-done | bytes 131104 | tf_op jit(solution)/shard_map/ppermute | solution.py:17
  169.7 0.6 fusion.82
  (9 shorter events, 0.1 us)
Async XLA Ops:
  2.3 52.2 %copy-start.5 = (s32[1,16]{1,0:T(1,128)S(1)}, s32[1,16]{1,0:T(1,128)}, u32[]{:S(2)}) copy-start(s32[1,16]{1,0:T(1,128)} %param.14) | copy-start | bytes 196
  2.3 53.0 %copy-start.4 = (s32[1,16]{1,0:T(1,128)S(1)}, s32[1,16]{1,0:T(1,128)}, u32[]{:S(2)}) copy-start(s32[1,16]{1,0:T(1,128)} %param.15) | copy-start | bytes 196
  2.4 7.6 %copy-start.1 = (bf16[2,1,128,128]{3,2,0,1:T(8,128)(2,1)S(1)}, bf16[2,1,128,128]{3,2,0,1:T(8,128)(2,1)}, u32[]{:S(2)}) copy-start(bf16[2,1,128,128]{3,2,0,1:T(8,128)(2,1)} %get-tuple-element.165) | copy-start | bytes 196612 | tf_op jit(solution)/shard_map/cond
  55.3 57.3 %copy-start.3 = (bf16[1,1,1,128,128]{4,3,2,1,0:T(8,128)(2,1)S(1)}, bf16[1,1,1,128,128]{4,3,2,1,0:T(8,128)(2,1)}, u32[]{:S(2)}) copy-start(bf16[1,1,1,128,128]{4,3,2,1,0:T(8,128)(2,1)} %param.13) | copy-start | bytes 98308
  108.2 4.4 %collective-permute-start = (bf16[4,1,128,128]{3,2,0,1:T(8,128)(2,1)S(1)}, bf16[4,1,128,128]{3,2,0,1:T(8,128)(2,1)S(1)}, u32[]{:S(2)}, u32[]{:S(2)}) collective-permute-start(bf16[4,1,128,128]{3,2,0,1:T(8,128)(2,1)S(1)} %slice.45), channel_id=1, source_target_pairs={{16,0},{32,16},{48,32},{64,48},{80,64},{96,80},{112,96},{128,112},... | collective-permute-start | bytes 393224 | tf_op jit(solution)/shard_map/ppermute | solution.py:17
  161.3 8.4 %collective-permute-start.1 = (bf16[4,1,128,128]{3,2,0,1:T(8,128)(2,1)S(1)}, bf16[4,1,128,128]{3,2,0,1:T(8,128)(2,1)S(1)}, u32[]{:S(2)}, u32[]{:S(2)}) collective-permute-start(bf16[4,1,128,128]{3,2,0,1:T(8,128)(2,1)S(1)} %slice_bitcast_fusion.5), channel_id=1, source_target_pairs={{496,0},{0,16},{16,32},{32,48},{48,64},{64,80},{80,96},{96,112},{1... | collective-permute-start | bytes 393224 | tf_op jit(solution)/shard_map/ppermute | solution.py:17

commit v3 on v2

--- a/solution.py
+++ b/solution.py
@@ -64,8 +64,8 @@
     return pl.pallas_call(
         functools.partial(gather_kernel, n),
         out_shape=jax.ShapeDtypeStruct((n,) + block.shape, block.dtype),
-        in_specs=[pl.BlockSpec(memory_space=pl.ANY)],
-        out_specs=pl.BlockSpec(memory_space=pl.ANY),
+        in_specs=[pl.BlockSpec(memory_space=pltpu.VMEM)],
+        out_specs=pl.BlockSpec(memory_space=pltpu.VMEM),
         scratch_shapes=[
             pltpu.SemaphoreType.DMA((2, n // 2)),
             pltpu.SemaphoreType.DMA((2, n // 2)),

time: 173 us -> 174 us (level)
  the two profiles are of different devices: /device:TPU:24 before, /device:TPU:16 now
where the time goes in v3:
time: 174 us; the launch traced here: 173 us
  Pallas kernels  131 us (75%)
  matrix products  16.3 us (9%)
  waiting for transfers between devices  8.38 us (5%)
  local copies, waits for them, and re-layouts  6.69 us (4%)
  starting transfers between devices  3.84 us (2%)
  between operations  2.94 us (2%)
  loops' own time  2.92 us (2%)
    pallas_call x3, Pallas kernels, node_gather(): pl.pallas_call(functools.partial(gather_kernel, n), out_shape=jax.ShapeDt...  131 us
    dot_general x1, matrix products, node_up(): jnp.einsum('xyq,xyp->qp', tensor_here, second, preferred_element_type=jnp...  8.78 us
    ppermute x2, waiting for transfers between devices, from_behind(): return lax.ppermute(block, axis, route)  8.38 us
    dot_general x1, matrix products, node_up(): jnp.einsum('xa,abp->xbp', left_env, tensor_here, preferred_element_type=j...  7.55 us
    ppermute x2, starting transfers between devices, from_behind(): return lax.ppermute(block, axis, route)  3.84 us
  transfers between devices with their start and end apart: 2, of which 2 were waited for; matrix products, arithmetic and copies ran while one was open for 0% of the time, Pallas kernels for 0%

profile of v3, /device:TPU:16, one launch (start us, length us, event | category | flops | bytes accessed | tf_op | source)
XLA Modules:
  0.0 173.4 jit_solution(8809602653632998422)
XLA Ops:
  0.0 1.2 constant_dynamic-slice_fusion.2
  2.3 0.0 copy-start.5
  2.3 0.0 copy-start.4
  2.4 51.9 %shard_map.57 = bf16[16,1,128,128]{3,2,1,0:T(8,128)(2,1)S(1)} custom-call(bf16[1,128,128]{2,1,0:T(8,128)(2,1)S(1)} %get-tuple-element.172.x_ref), custom_call_target="tpu_custom_call" | custom-call | tf_op jit(solution)/shard_map/pallas_call | solution.py:64
  54.8 0.0 copy-done.5
  54.8 0.1 select_reduce_fusion
  55.5 0.1 compare_and_fusion.1
  55.6 0.0 copy-done.4
  55.6 0.0 copy-start.3
  55.6 20.7 %conditional.4 = (bf16[1,128,128]{1,2,0:T(8,128)(2,1)S(1)}) conditional(s32[]{:T(128)} %convert_element_type.74, () %tuple.34, (s32[]{:T(128)}, s32[1,16]{1,0:T(1,128)S(1)}, s32[16]{0:T(128)S(1)}, s32[4]{0:T(128)S(1)}, bf16[16,1,128,128]{3,2,1,0:T(8,128)(2,1)S(1)}, /*index=5*/bf16[2,1,128,128]{3,2,0,1:T(8,128)(2,1)}, ...), branch_computations={%region_3.4_spmd, %region_4.5_spmd} | conditional | flops 1612825600 | bytes 17732928 | solution.py:150
  55.8 0.7 constant_dynamic-slice_fusion
  57.8 0.1 compare_select_fusion
  57.8 0.6 gather_fusion
  58.4 0.1 compare_and_fusion
  58.5 0.1 bitcast_select_fusion
  58.6 0.0 copy-start.2
  58.6 7.6 %fusion.51 = bf16[128,128,128]{2,0,1:T(8,128)(2,1)} fusion(bf16[128,128,128]{2,1,0:T(8,128)(2,1)} %get-tuple-element.148, bf16[2,1,128,128]{3,2,0,1:T(8,128)(2,1)} %get-tuple-element.147, bf16[4,1,128,128]{3,2,0,1:T(8,128)(2,1)S(1)} %bitcast_select_fusion, s32[]{:T(128)} %bitcast.12, pred[]{:T(512)} %bitcast.9), kind=kOutput, calls=%fused_computation.43 | convolution fusion | flops 536887296 | bytes 8455168 | tf_op jit(solution)/shard_map/cond/branch_1_fun/xa,abp->xbp/dot_general | solution.py:79
  67.5 0.0 copy-done.2
  67.5 8.8 %fusion.60 = bf16[1,128,128]{1,2,0:T(8,128)(2,1)S(1)} fusion(bf16[128,128,128]{2,1,0:T(8,128)(2,1)} %get-tuple-element.148, bf16[128,128,128]{2,0,1:T(8,128)(2,1)} %fusion.51, bf16[2,1,128,128]{3,2,0,1:T(8,128)(2,1)S(1)} %copy-done.2, bf16[4,1,128,128]{3,2,0,1:T(8,128)(2,1)S(1)} %bitcast_select_fusion, s32[]{:T(128)} %bitcast.16, pred[]{:T(512)} %bitcast.15), kind=kOutput, calls=%fused_computation.48 | convolution fusion | flops 1075871744 | bytes 8486917 | tf_op jit(solution)/shard_map/cond/branch_1_fun/xyq,xyp->qp/dot_general | solution.py:85
  76.3 0.7 copy.18.x_ref
  77.1 26.9 %shard_map.58 = bf16[16,1,128,128]{3,2,1,0:T(8,128)(2,1)} custom-call(bf16[1,128,128]{2,1,0:T(8,128)(2,1)} %copy.18.x_ref), custom_call_target="tpu_custom_call" | custom-call | tf_op jit(solution)/shard_map/pallas_call | solution.py:64
  104.0 1.6 gather_fusion.1
  105.7 0.1 bitcast_select_fusion.2
  105.8 1.9 %collective-permute-start = (bf16[4,1,128,128]{3,2,0,1:T(8,128)(2,1)S(1)}, bf16[4,1,128,128]{3,2,0,1:T(8,128)(2,1)S(1)}, u32[]{:S(2)}, u32[]{:S(2)}) collective-permute-start(bf16[4,1,128,128]{3,2,0,1:T(8,128)(2,1)S(1)} %slice.45), channel_id=1, source_target_pairs={{16,0},{32,16},{48,32},{64,48},{80,64},{96,80},{112,96},{128,112},... | collective-permute-start | bytes 393224 | tf_op jit(solution)/shard_map/ppermute | solution.py:17
  108.3 1.9 %collective-permute-done = bf16[4,1,128,128]{3,2,0,1:T(8,128)(2,1)S(1)} collective-permute-done((bf16[4,1,128,128]{3,2,0,1:T(8,128)(2,1)S(1)}, bf16[4,1,128,128]{3,2,0,1:T(8,128)(2,1)S(1)}, u32[]{:S(2)}, u32[]{:S(2)}) %collective-permute-start) | collective-permute-done | bytes 131104 | tf_op jit(solution)/shard_map/ppermute | solution.py:17
  110.2 0.0 copy-done.3
  110.2 52.2 %shard_map.59 = bf16[16,2,1,128,128]{4,3,2,1,0:T(8,128)(2,1)} custom-call(bf16[2,1,128,128]{3,2,1,0:T(8,128)(2,1)S(1)} %get-tuple-element.182.x_ref), custom_call_target="tpu_custom_call" | custom-call | tf_op jit(solution)/shard_map/pallas_call | solution.py:64
  162.4 1.8 %gather_fusion.2 = bf16[4,2,128,128]{3,2,1,0:T(8,128)(2,1)S(1)} fusion(bf16[16,2,128,128]{3,2,1,0:T(8,128)(2,1)} %bitcast.140, s32[1024]{0:T(1024)S(1)} %pad_clamp_fusion.1), kind=kCustom, calls=%fused_computation.2 | custom fusion | bytes 524304 | tf_op jit(solution)/shard_map/jit(_take)/gather | solution.py:168
  164.3 0.1 bitcast_select_fusion.1
  164.4 1.9 %collective-permute-start.1 = (bf16[4,1,128,128]{3,2,0,1:T(8,128)(2,1)S(1)}, bf16[4,1,128,128]{3,2,0,1:T(8,128)(2,1)S(1)}, u32[]{:S(2)}, u32[]{:S(2)}) collective-permute-start(bf16[4,1,128,128]{3,2,0,1:T(8,128)(2,1)S(1)} %slice_bitcast_fusion.5), channel_id=1, source_target_pairs={{496,0},{0,16},{16,32},{32,48},{48,64},{64,80},{80,96},{96,112},{1... | collective-permute-start | bytes 393224 | tf_op jit(solution)/shard_map/ppermute | solution.py:17
  166.3 6.5 %collective-permute-done.1 = bf16[4,1,128,128]{3,2,0,1:T(8,128)(2,1)S(1)} collective-permute-done((bf16[4,1,128,128]{3,2,0,1:T(8,128)(2,1)S(1)}, bf16[4,1,128,128]{3,2,0,1:T(8,128)(2,1)S(1)}, u32[]{:S(2)}, u32[]{:S(2)}) %collective-permute-start.1) | collective-permute-done | bytes 131104 | tf_op jit(solution)/shard_map/ppermute | solution.py:17
  172.8 0.6 fusion.82
  (11 shorter events, 0.1 us)
Async XLA Ops:
  2.3 52.5 %copy-start.5 = (s32[1,16]{1,0:T(1,128)S(1)}, s32[1,16]{1,0:T(1,128)}, u32[]{:S(2)}) copy-start(s32[1,16]{1,0:T(1,128)} %param.14) | copy-start | bytes 196
  2.3 53.3 %copy-start.4 = (s32[1,16]{1,0:T(1,128)S(1)}, s32[1,16]{1,0:T(1,128)}, u32[]{:S(2)}) copy-start(s32[1,16]{1,0:T(1,128)} %param.15) | copy-start | bytes 196
  55.6 54.6 %copy-start.3 = (bf16[1,1,1,128,128]{4,3,2,1,0:T(8,128)(2,1)S(1)}, bf16[1,1,1,128,128]{4,3,2,1,0:T(8,128)(2,1)}, u32[]{:S(2)}) copy-start(bf16[1,1,1,128,128]{4,3,2,1,0:T(8,128)(2,1)} %param.13) | copy-start | bytes 98308
  58.6 8.9 %copy-start.2 = (bf16[2,1,128,128]{3,2,0,1:T(8,128)(2,1)S(1)}, bf16[2,1,128,128]{3,2,0,1:T(8,128)(2,1)}, u32[]{:S(2)}) copy-start(bf16[2,1,128,128]{3,2,0,1:T(8,128)(2,1)} %get-tuple-element.147) | copy-start | bytes 196612 | tf_op jit(solution)/shard_map/cond
  105.8 4.4 %collective-permute-start = (bf16[4,1,128,128]{3,2,0,1:T(8,128)(2,1)S(1)}, bf16[4,1,128,128]{3,2,0,1:T(8,128)(2,1)S(1)}, u32[]{:S(2)}, u32[]{:S(2)}) collective-permute-start(bf16[4,1,128,128]{3,2,0,1:T(8,128)(2,1)S(1)} %slice.45), channel_id=1, source_target_pairs={{16,0},{32,16},{48,32},{64,48},{80,64},{96,80},{112,96},{128,112},... | collective-permute-start | bytes 393224 | tf_op jit(solution)/shard_map/ppermute | solution.py:17
  164.4 8.4 %collective-permute-start.1 = (bf16[4,1,128,128]{3,2,0,1:T(8,128)(2,1)S(1)}, bf16[4,1,128,128]{3,2,0,1:T(8,128)(2,1)S(1)}, u32[]{:S(2)}, u32[]{:S(2)}) collective-permute-start(bf16[4,1,128,128]{3,2,0,1:T(8,128)(2,1)S(1)} %slice_bitcast_fusion.5), channel_id=1, source_target_pairs={{496,0},{0,16},{16,32},{32,48},{48,64},{64,80},{80,96},{96,112},{1... | collective-permute-start | bytes 393224 | tf_op jit(solution)/shard_map/ppermute | solution.py:17

commit v4 on v3

--- a/solution.py
+++ b/solution.py
@@ -148,27 +148,27 @@
         return jnp.stack([node_up(tensor_here, child_envs[0][0], child_envs[1][0])])
 
     mid_up = lax.cond(is_mid, mid_work, lambda: zero_envs)
-    mid_spots = role_spot[top_count : top_count + mid_count]
-    every_mid = node_gather(mid_up, 1)
-    mid_table = jnp.take(every_mid, mid_spots, axis=0)
+    next_roles = from_behind(group_roles, "sub", -1)
+    prev_roles = from_behind(group_roles, "sub", 1)
+    mid_pair = jnp.stack([mid_up, from_behind(mid_up, "sub", -1)])
+    every_mid = node_gather(mid_pair, 1)
     top_index = jnp.clip(my_role, 0, top_count - 1)
-    next_half = from_behind(mid_table[top_count:], "sub", -1)
-    right_envs = next_half[top_index]
+    left_spot = role_spot[top_count + top_index]
+    right_spot = placements(next_roles)[top_count + top_count + top_index]
+    left_env = every_mid[left_spot, 0]
+    right_env = every_mid[right_spot, 1]
 
     def top_work():
-        left_env = mid_table[top_index]
-        results = [node_down(tensor_here, left_env[0], right_envs[0], upper_envs[0])]
+        results = [node_down(tensor_here, left_env[t], right_env[t], upper_envs[t]) for t in range(TERMS)]
         return jnp.stack([jnp.stack([r[0] for r in results]), jnp.stack([r[1] for r in results])])
 
     top_down = lax.cond(
         is_top, top_work, lambda: jnp.zeros((2, TERMS, bond_size, bond_size), jnp.bfloat16)
     )
-    top_spots = role_spot[:top_count]
-    every_top = node_gather(top_down, 2)
-    top_table = jnp.take(every_top, top_spots, axis=0)
-    own_field = top_table[jnp.clip(mid_index, 0, top_count - 1), 0]
-    from_before = from_behind(top_table[:, 1], "sub", 1)
-    other_field = from_before[jnp.clip(mid_index - top_count, 0, top_count - 1)]
+    top_pair = jnp.stack([top_down[0], from_behind(top_down[1], "sub", 1)])
+    every_top = node_gather(top_pair, 2)
+    own_field = every_top[role_spot[jnp.clip(mid_index, 0, top_count - 1)], 0]
+    other_field = every_top[placements(prev_roles)[jnp.clip(mid_index - top_count, 0, top_count - 1)], 1]
     mid_field = jnp.where(mid_index < top_count, own_field, other_field)
     result = jnp.where(is_mid, mid_field, jnp.where(is_leaf, leaf_up, zero_envs))
     return result[None, None]

time: 174 us -> 195 us (1.12)
  the two profiles are of different devices: /device:TPU:16 before, /device:TPU:8 now
where the time goes in v4:
time: 195 us; the launch traced here: 194 us
  Pallas kernels  122 us (63%)
  starting transfers between devices  27.1 us (14%)
  matrix products  19.6 us (10%)
  between operations  7.54 us (4%)
  local copies, waits for them, and re-layouts  7.27 us (4%)
  loops' own time  5.33 us (3%)
  other arithmetic  3.04 us (2%)
  waiting for transfers between devices  2.76 us (1%)
    pallas_call x3, Pallas kernels, node_gather(): pl.pallas_call(functools.partial(gather_kernel, n), out_shape=jax.ShapeDt...  122 us
    ppermute x4, starting transfers between devices, from_behind(): return lax.ppermute(block, axis, route)  27.1 us
    dot_general x1, matrix products, node_down(): jnp.einsum('xyq,xa->ayq', tensor_here, left_env, preferred_element_type=j...  5.72 us
    another operation x1, loops' own time, local(): lax.cond(is_top, top_work, lambda: jnp.zeros((2, TERMS, bond_size, bond_s...  5.3 us
    dot_general x1, matrix products, node_down(): jnp.einsum('xbq,abq->xa', right_part, weighted, preferred_element_type=jn...  4.64 us
    dot_general x1, matrix products, node_down(): jnp.einsum('ayq,abq->yb', left_part, weighted, preferred_element_type=jnp...  4.41 us
  transfers between devices with their start and end apart: 4, of which 1 were waited for; matrix products, arithmetic and copies ran while one was open for 12% of the time, Pallas kernels for 19%

profile of v4, /device:TPU:8, one launch (start us, length us, event | category | flops | bytes accessed | tf_op | source)
XLA Modules:
  0.0 194.2 jit_solution(6359563934309570795)
XLA Ops:
  0.0 1.3 constant_dynamic-slice_fusion.2
  2.7 0.0 copy-start.7
  2.7 0.0 copy-start.6
  2.8 49.1 %shard_map.57 = bf16[16,1,128,128]{3,2,1,0:T(8,128)(2,1)S(1)} custom-call(bf16[1,128,128]{2,1,0:T(8,128)(2,1)S(1)} %get-tuple-element.341.x_ref), custom_call_target="tpu_custom_call" | custom-call | tf_op jit(solution)/shard_map/pallas_call | solution.py:64
  52.6 0.0 copy-done.7
  52.6 0.1 select_reduce_fusion.2
  53.4 0.0 copy-done.6
  53.4 0.0 copy-start.5
  53.5 0.6 conditional.4
  53.5 0.6 broadcast_in_dim.50
  54.1 0.9 copy.11
  55.0 20.8 %collective-permute-start.1 = (bf16[1,128,128]{2,1,0:T(8,128)(2,1)S(1)}, bf16[1,128,128]{2,1,0:T(8,128)(2,1)S(1)}, u32[]{:S(2)}, u32[]{:S(2)}) collective-permute-start(bf16[1,128,128]{2,1,0:T(8,128)(2,1)S(1)} %copy.11), channel_id=1, source_target_pairs={{16,0},{32,16},{48,32},{64,48},{80,64},{96,80},{112,96},{128,112},... | collective-permute-start | bytes 98312 | tf_op jit(solution)/shard_map/ppermute | solution.py:17
  75.8 1.9 collective-permute-start
  77.7 2.4 %collective-permute-start.3 = (s32[16]{0:T(128)S(1)}, s32[16]{0:T(128)S(1)}, u32[]{:S(2)}, u32[]{:S(2)}) collective-permute-start(s32[16]{0:T(128)S(1)} %bitcast.140), channel_id=1, source_target_pairs={{496,0},{0,16},{16,32},{32,48},{48,64},{64,80},{80,96},{96,112},{1... | collective-permute-start | bytes 200 | tf_op jit(solution)/shard_map/ppermute | solution.py:17
  80.9 0.6 dynamic_slice.70
  83.4 0.0 collective-permute-done.1
  83.4 0.6 pad_maximum_fusion.1.x_ref
  84.0 37.3 %shard_map.58 = bf16[16,2,1,128,128]{4,3,2,1,0:T(8,128)(2,1)S(1)} custom-call(bf16[2,1,128,128]{3,2,1,0:T(8,128)(2,1)} %pad_maximum_fusion.1.x_ref), custom_call_target="tpu_custom_call" | custom-call | tf_op jit(solution)/shard_map/pallas_call | solution.py:64
  121.3 0.0 collective-permute-done
  121.3 0.0 copy-done.5
  121.4 28.3 %conditional.5 = (bf16[2,1,128,128]{3,2,1,0:T(8,128)(2,1)S(1)}) conditional(s32[]{:T(128)} %convert_element_type.86, () %tuple.62, (s32[16]{0:T(128)S(1)}, s32[16,16]{1,0:T(8,128)S(1)}, s32[16,16]{1,0:T(8,128)S(1)}, s32[16,16]{1,0:T(8,128)S(1)}, s32[]{:T(128)}, /*index=5*/bf16[16,2,1,128,128]{4,3,2,1,0:T(8,128)(2,1)S(1)}, ...), branch_computations={%region_5.6_spmd, %region_6.8_spmd} | conditional | flops 2686518016 | bytes 92573096 | solution.py:165
  122.4 0.1 select_reduce_fusion
  122.5 0.6 dynamic_slice.60
  125.0 0.0 copy-start
  125.0 3.6 %fusion.42 = bf16[128,128,128]{2,0,1:T(8,128)(2,1)S(1)} fusion(bf16[128,128,128]{2,1,0:T(8,128)(2,1)} %get-tuple-element.328, bf16[16,2,1,128,128]{4,3,2,1,0:T(8,128)(2,1)S(1)} %get-tuple-element.322, s32[]{:T(128)S(6)} %select_n.139), kind=kOutput, calls=%fused_computation.31 | convolution fusion | flops 536870912 | bytes 8421380 | tf_op jit(solution)/shard_map/cond/branch_1_fun/xyq,yb->xbq/dot_general | solution.py:94
  128.6 0.0 copy-done
  128.6 1.2 convolution_convert_fusion
  129.9 0.0 copy-start.1
  129.9 1.9 copy-done.1
  131.9 4.6 %fusion.35 = bf16[1,1,128,128]{3,2,1,0:T(8,128)(2,1)S(1)} fusion(bf16[128,128,128]{2,1,0:T(8,128)(2,1)S(1)} %convolution_convert_fusion, bf16[128,128,128]{2,0,1:T(8,128)(2,1)S(1)} %fusion.42), kind=kOutput, calls=%fused_computation.27 | convolution fusion | flops 536887296 | bytes 8421376 | tf_op jit(solution)/shard_map/cond/branch_1_fun/xbq,abq->xa/dot_general | solution.py:100
  136.5 0.7 dynamic_slice.62
  139.2 0.0 copy-start.2
  139.2 5.7 %fusion.19 = bf16[128,128,128]{2,0,1:T(8,128)(2,1)S(1)} fusion(bf16[128,128,128]{2,1,0:T(8,128)(2,1)} %get-tuple-element.328, bf16[16,2,1,128,128]{4,3,2,1,0:T(8,128)(2,1)S(1)} %get-tuple-element.322, s32[]{:T(128)S(6)} %select_n.141), kind=kOutput, calls=%fused_computation.18 | convolution fusion | flops 536870912 | bytes 8421380 | tf_op jit(solution)/shard_map/cond/branch_1_fun/xyq,xa->ayq/dot_general | solution.py:97
  144.9 0.0 copy-done.2
  145.0 4.4 %fusion.34 = bf16[1,1,128,128]{3,2,1,0:T(8,128)(2,1)S(1)} fusion(bf16[128,128,128]{2,1,0:T(8,128)(2,1)S(1)} %copy-done.2, bf16[128,128,128]{2,0,1:T(8,128)(2,1)S(1)} %fusion.19), kind=kOutput, calls=%fused_computation.26 | convolution fusion | flops 536887296 | bytes 8421376 | tf_op jit(solution)/shard_map/cond/branch_1_fun/ayq,abq->yb/dot_general | solution.py:103
  149.7 1.9 collective-permute-start.2
  151.6 0.0 collective-permute-done.3
  151.6 0.1 select_reduce_fusion.1
  151.7 0.6 dynamic_slice.72
  154.3 2.8 %collective-permute-done.2 = bf16[1,128,128]{2,1,0:T(8,128)(2,1)S(1)} collective-permute-done((bf16[1,128,128]{2,1,0:T(8,128)(2,1)S(1)}, bf16[1,128,128]{2,1,0:T(8,128)(2,1)S(1)}, u32[]{:S(2)}, u32[]{:S(2)}) %collective-permute-start.2) | collective-permute-done | bytes 32800 | tf_op jit(solution)/shard_map/ppermute | solution.py:17
  157.0 0.6 pad_maximum_fusion.2.x_ref
  157.7 35.1 %shard_map.59 = bf16[16,2,1,128,128]{4,3,2,1,0:T(8,128)(2,1)} custom-call(bf16[2,1,128,128]{3,2,1,0:T(8,128)(2,1)} %pad_maximum_fusion.2.x_ref), custom_call_target="tpu_custom_call" | custom-call | tf_op jit(solution)/shard_map/pallas_call | solution.py:64
  192.8 1.4 fusion.79
  (8 shorter events, 0.1 us)
Async XLA Ops:
  2.7 49.9 %copy-start.7 = (s32[1,16]{1,0:T(1,128)S(1)}, s32[1,16]{1,0:T(1,128)}, u32[]{:S(2)}) copy-start(s32[1,16]{1,0:T(1,128)} %param.14) | copy-start | bytes 196
  2.7 50.7 %copy-start.6 = (s32[1,16]{1,0:T(1,128)S(1)}, s32[1,16]{1,0:T(1,128)}, u32[]{:S(2)}) copy-start(s32[1,16]{1,0:T(1,128)} %param.15) | copy-start | bytes 196
  53.4 67.9 %copy-start.5 = (bf16[1,1,1,128,128]{4,3,2,1,0:T(8,128)(2,1)S(1)}, bf16[1,1,1,128,128]{4,3,2,1,0:T(8,128)(2,1)}, u32[]{:S(2)}) copy-start(bf16[1,1,1,128,128]{4,3,2,1,0:T(8,128)(2,1)} %param.13) | copy-start | bytes 98308
  55.0 28.4 %collective-permute-start.1 = (bf16[1,128,128]{2,1,0:T(8,128)(2,1)S(1)}, bf16[1,128,128]{2,1,0:T(8,128)(2,1)S(1)}, u32[]{:S(2)}, u32[]{:S(2)}) collective-permute-start(bf16[1,128,128]{2,1,0:T(8,128)(2,1)S(1)} %copy.11), channel_id=1, source_target_pairs={{16,0},{32,16},{48,32},{64,48},{80,64},{96,80},{112,96},{128,112},... | collective-permute-start | bytes 98312 | tf_op jit(solution)/shard_map/ppermute | solution.py:17
  75.8 45.5 %collective-permute-start = (s32[16]{0:T(128)S(1)}, s32[16]{0:T(128)S(1)}, u32[]{:S(2)}, u32[]{:S(2)}) collective-permute-start(s32[16]{0:T(128)S(1)} %bitcast.139), channel_id=1, source_target_pairs={{16,0},{32,16},{48,32},{64,48},{80,64},{96,80},{112,96},{128,112},... | collective-permute-start | bytes 200 | tf_op jit(solution)/shard_map/ppermute | solution.py:17
  77.7 73.9 %collective-permute-start.3 = (s32[16]{0:T(128)S(1)}, s32[16]{0:T(128)S(1)}, u32[]{:S(2)}, u32[]{:S(2)}) collective-permute-start(s32[16]{0:T(128)S(1)} %bitcast.140), channel_id=1, source_target_pairs={{496,0},{0,16},{16,32},{32,48},{48,64},{64,80},{80,96},{96,112},{1... | collective-permute-start | bytes 200 | tf_op jit(solution)/shard_map/ppermute | solution.py:17
  125.0 3.6 %copy-start = (bf16[128,128,128]{2,1,0:T(8,128)(2,1)S(1)}, bf16[128,128,128]{2,1,0:T(8,128)(2,1)}, u32[]{:S(2)}) copy-start(bf16[128,128,128]{2,1,0:T(8,128)(2,1)} %get-tuple-element.328) | copy-start | bytes 12582916 | tf_op jit(solution)/shard_map/cond
  129.9 2.0 %copy-start.1 = (bf16[128,128,128]{2,1,0:T(8,128)(2,1)}, bf16[128,128,128]{2,1,0:T(8,128)(2,1)S(1)}, u32[]{:S(2)}) copy-start(bf16[128,128,128]{2,1,0:T(8,128)(2,1)S(1)} %convolution_convert_fusion) | copy-start | bytes 12582916 | tf_op jit(solution)/shard_map/cond
  139.2 5.7 %copy-start.2 = (bf16[128,128,128]{2,1,0:T(8,128)(2,1)S(1)}, bf16[128,128,128]{2,1,0:T(8,128)(2,1)}, u32[]{:S(2)}) copy-start(bf16[128,128,128]{2,1,0:T(8,128)(2,1)} %copy-done.1) | copy-start | bytes 12582916 | tf_op jit(solution)/shard_map/cond
  149.7 7.3 %collective-permute-start.2 = (bf16[1,128,128]{2,1,0:T(8,128)(2,1)S(1)}, bf16[1,128,128]{2,1,0:T(8,128)(2,1)S(1)}, u32[]{:S(2)}, u32[]{:S(2)}) collective-permute-start(bf16[1,128,128]{2,1,0:T(8,128)(2,1)S(1)} %get-tuple-element.348), channel_id=1, source_target_pairs={{496,0},{0,16},{16,32},{32,48},{48,64},{64,80},{80,96},{96,112},{1... | collective-permute-start | bytes 98312 | tf_op jit(solution)/shard_map/ppermute | solution.py:17

commit v5 on v4

--- a/solution.py
+++ b/solution.py
@@ -17,22 +17,42 @@
     return lax.ppermute(block, axis, route)
 
 
-def gather_kernel(n, x_ref, out_ref, send_sem, recv_sem, own_sem):
+def gather_kernel(n, groups, shift, x_ref, out_ref, send_sem, recv_sem, own_sem, sub_sem):
     me = lax.axis_index("node")
     group = lax.axis_index("sub")
     right = lax.rem(me + 1, n)
     left = lax.rem(me + n - 1, n)
     barrier = pltpu.get_barrier_semaphore()
-    for neighbour in (left, right):
-        pl.semaphore_signal(barrier, inc=1, device_id=(group, neighbour), device_id_type=MESH)
-    pl.semaphore_wait(barrier, 2)
-    own = pltpu.make_async_copy(x_ref, out_ref.at[me], own_sem)
-    own.start()
+    peers = [(group, left), (group, right)]
+    if shift:
+        peers += [(lax.rem(group + shift + groups, groups), me), (lax.rem(group - shift + groups, groups), me)]
+    for peer in peers:
+        pl.semaphore_signal(barrier, inc=1, device_id=peer, device_id_type=MESH)
+    pl.semaphore_wait(barrier, len(peers))
+    if shift:
+        own = pltpu.make_async_copy(x_ref.at[0], out_ref.at[me, 0], own_sem)
+        own.start()
+        across = pltpu.make_async_remote_copy(
+            src_ref=x_ref.at[1],
+            dst_ref=out_ref.at[me, 1],
+            send_sem=sub_sem.at[0],
+            recv_sem=sub_sem.at[1],
+            device_id=peers[2],
+            device_id_type=MESH,
+        )
+        across.start()
+        own.wait()
+        across.wait_recv()
+        first_src = out_ref.at[me]
+    else:
+        own = pltpu.make_async_copy(x_ref, out_ref.at[me], own_sem)
+        own.start()
+        first_src = x_ref
     ways = ((0, 1, right, n // 2), (1, -1, left, n - 1 - n // 2))
 
-    def hop(way, sign, target, step, origin):
+    def hop(way, target, step, origin):
         return pltpu.make_async_remote_copy(
-            src_ref=x_ref if step == 0 else out_ref.at[origin],
+            src_ref=first_src if step == 0 else out_ref.at[origin],
             dst_ref=out_ref.at[origin],
             send_sem=send_sem.at[way, step],
             recv_sem=recv_sem.at[way, step],
@@ -47,22 +67,26 @@
                 continue
             origin = lax.rem(me - sign * step + 2 * n, n)
             if step > 0:
-                hop(way, sign, target, step - 1, origin).wait_recv()
-            copy = hop(way, sign, target, step, origin)
+                hop(way, target, step - 1, origin).wait_recv()
+            copy = hop(way, target, step, origin)
             copy.start()
             sent.append(copy)
     for way, sign, target, steps in ways:
         origin = lax.rem(me - sign * steps + 2 * n, n)
-        hop(way, sign, target, steps - 1, origin).wait_recv()
+        hop(way, target, steps - 1, origin).wait_recv()
     for copy in sent:
         copy.wait_send()
-    own.wait()
-
-
-def node_gather(block, collective_id):
+    if shift:
+        across.wait_send()
+    else:
+        own.wait()
+
+
+def node_gather(block, collective_id, shift=0):
     n = lax.axis_size("node")
+    groups = lax.axis_size("sub")
     return pl.pallas_call(
-        functools.partial(gather_kernel, n),
+        functools.partial(gather_kernel, n, groups, shift),
         out_shape=jax.ShapeDtypeStruct((n,) + block.shape, block.dtype),
         in_specs=[pl.BlockSpec(memory_space=pltpu.VMEM)],
         out_specs=pl.BlockSpec(memory_space=pltpu.VMEM),
@@ -70,6 +94,7 @@
             pltpu.SemaphoreType.DMA((2, n // 2)),
             pltpu.SemaphoreType.DMA((2, n // 2)),
             pltpu.SemaphoreType.DMA,
+            pltpu.SemaphoreType.DMA((2,)),
         ],
         compiler_params=pltpu.CompilerParams(collective_id=collective_id, has_side_effects=True),
     )(block)
@@ -150,8 +175,7 @@
     mid_up = lax.cond(is_mid, mid_work, lambda: zero_envs)
     next_roles = from_behind(group_roles, "sub", -1)
     prev_roles = from_behind(group_roles, "sub", 1)
-    mid_pair = jnp.stack([mid_up, from_behind(mid_up, "sub", -1)])
-    every_mid = node_gather(mid_pair, 1)
+    every_mid = node_gather(jnp.stack([mid_up, mid_up]), 1, -1)
     top_index = jnp.clip(my_role, 0, top_count - 1)
     left_spot = role_spot[top_count + top_index]
     right_spot = placements(next_roles)[top_count + top_count + top_index]
@@ -165,8 +189,7 @@
     top_down = lax.cond(
         is_top, top_work, lambda: jnp.zeros((2, TERMS, bond_size, bond_size), jnp.bfloat16)
     )
-    top_pair = jnp.stack([top_down[0], from_behind(top_down[1], "sub", 1)])
-    every_top = node_gather(top_pair, 2)
+    every_top = node_gather(top_down, 2, 1)
     own_field = every_top[role_spot[jnp.clip(mid_index, 0, top_count - 1)], 0]
     other_field = every_top[placements(prev_roles)[jnp.clip(mid_index - top_count, 0, top_count - 1)], 1]
     mid_field = jnp.where(mid_index < top_count, own_field, other_field)

time: 195 us -> 189 us (0.969)
  the two profiles are of different devices: /device:TPU:8 before, /device:TPU:32 now
where the time goes in v5:
time: 189 us; the launch traced here: 188 us
  Pallas kernels  146 us (77%)
  matrix products  16.3 us (9%)
  starting transfers between devices  8.47 us (4%)
  between operations  7.15 us (4%)
  local copies, waits for them, and re-layouts  3.83 us (2%)
  other arithmetic  3.11 us (2%)
  loops' own time  3.11 us (2%)
    pallas_call x3, Pallas kernels, node_gather(): pl.pallas_call(functools.partial(gather_kernel, n, groups, shift), out_sh...  146 us
    dot_general x1, matrix products, node_up(): jnp.einsum('xyq,xyp->qp', tensor_here, second, preferred_element_type=jnp...  8.79 us
    ppermute x2, starting transfers between devices, from_behind(): return lax.ppermute(block, axis, route)  8.47 us
    dot_general x1, matrix products, node_up(): jnp.einsum('xa,abp->xbp', left_env, tensor_here, preferred_element_type=j...  7.54 us
  transfers between devices with their start and end apart: 2, of which 0 were waited for; matrix products, arithmetic and copies ran while one was open for 12% of the time, Pallas kernels for 41%

profile of v5, /device:TPU:32, one launch (start us, length us, event | category | flops | bytes accessed | tf_op | source)
XLA Modules:
  0.0 188.3 jit_solution(1740528004447311192)
XLA Ops:
  0.0 6.5 %collective-permute-start = (s32[16]{0:T(128)}, s32[16]{0:T(128)S(1)}, u32[]{:S(2)}, u32[]{:S(2)}) collective-permute-start(s32[16]{0:T(128)} %bitcast.137), channel_id=1, source_target_pairs={{16,0},{32,16},{48,32},{64,48},{80,64},{96,80},{112,96},{128,112},... | collective-permute-start | bytes 200 | tf_op jit(solution)/shard_map/ppermute | solution.py:17
  6.6 1.9 %collective-permute-start.1 = (s32[16]{0:T(128)}, s32[16]{0:T(128)S(1)}, u32[]{:S(2)}, u32[]{:S(2)}) collective-permute-start(s32[16]{0:T(128)} %bitcast.138), channel_id=1, source_target_pairs={{496,0},{0,16},{16,32},{32,48},{48,64},{64,80},{80,96},{96,112},{1... | collective-permute-start | bytes 200 | tf_op jit(solution)/shard_map/ppermute | solution.py:17
  8.5 0.8 select_reduce_fusion.2
  9.3 1.2 constant_dynamic-slice_fusion.2
  13.7 0.6 dynamic_slice.70
  15.6 0.0 copy-start.6
  15.7 49.5 %shard_map.57 = bf16[16,1,128,128]{3,2,1,0:T(8,128)(2,1)S(1)} custom-call(bf16[1,128,128]{2,1,0:T(8,128)(2,1)S(1)} %get-tuple-element.338.x_ref), custom_call_target="tpu_custom_call" | custom-call | tf_op jit(solution)/shard_map/pallas_call | solution.py:88
  65.2 0.0 copy-done.6
  65.2 0.0 copy-start.5
  65.2 20.5 %conditional.4 = (bf16[1,128,128]{1,2,0:T(8,128)(2,1)S(1)}) conditional(s32[]{:T(128)} %convert_element_type.87, () %tuple.59, (s32[]{:T(128)}, s32[1,16]{1,0:T(1,128)S(1)}, s32[16]{0:T(128)S(1)}, bf16[16,1,128,128]{3,2,1,0:T(8,128)(2,1)S(1)}, bf16[2,1,128,128]{3,2,0,1:T(8,128)(2,1)}, /*index=5*/bf16[128,128,128]{2,1,0:T(8,128)(2,1)}) %tuple.81), branch_computations={%region_3.4_spmd, %region_4.5_spmd} | conditional | flops 1612825600 | bytes 17732880 | solution.py:175
  65.4 0.7 constant_dynamic-slice_fusion
  67.5 0.1 compare_and_fusion
  67.6 0.6 gather_fusion
  68.1 0.1 bitcast_select_fusion
  68.2 0.0 copy-start.4
  68.2 7.5 %fusion.52 = bf16[128,128,128]{2,0,1:T(8,128)(2,1)} fusion(bf16[128,128,128]{2,1,0:T(8,128)(2,1)} %get-tuple-element.322, bf16[2,1,128,128]{3,2,0,1:T(8,128)(2,1)} %get-tuple-element.321, bf16[4,1,128,128]{3,2,0,1:T(8,128)(2,1)S(1)} %bitcast_select_fusion, s32[]{:T(128)} %bitcast.12, pred[]{:T(512)} %bitcast.9), kind=kOutput, calls=%fused_computation.43 | convolution fusion | flops 536887296 | bytes 8455168 | tf_op jit(solution)/shard_map/cond/branch_1_fun/xa,abp->xbp/dot_general | solution.py:104
  76.9 0.0 copy-done.4
  77.0 8.8 %fusion.61 = bf16[1,128,128]{1,2,0:T(8,128)(2,1)S(1)} fusion(bf16[128,128,128]{2,1,0:T(8,128)(2,1)} %get-tuple-element.322, bf16[128,128,128]{2,0,1:T(8,128)(2,1)} %fusion.52, bf16[2,1,128,128]{3,2,0,1:T(8,128)(2,1)S(1)} %copy-done.4, bf16[4,1,128,128]{3,2,0,1:T(8,128)(2,1)S(1)} %bitcast_select_fusion, s32[]{:T(128)} %bitcast.16, pred[]{:T(512)} %bitcast.15), kind=kOutput, calls=%fused_computation.48 | convolution fusion | flops 1075871744 | bytes 8486917 | tf_op jit(solution)/shard_map/cond/branch_1_fun/xyq,xyp->qp/dot_general | solution.py:110
  85.7 0.1 copy.11
  85.9 0.6 pad_maximum_fusion.1.x_ref
  86.5 28.5 %shard_map.58 = bf16[16,2,1,128,128]{4,3,2,1,0:T(8,128)(2,1)S(1)} custom-call(bf16[2,1,128,128]{3,2,1,0:T(8,128)(2,1)} %pad_maximum_fusion.1.x_ref), custom_call_target="tpu_custom_call" | custom-call | tf_op jit(solution)/shard_map/pallas_call | solution.py:88
  115.6 0.0 collective-permute-done.1
  115.6 0.1 select_reduce_fusion.1
  115.7 0.6 dynamic_slice.72
  117.6 0.0 collective-permute-done
  117.6 0.0 copy-done.5
  117.6 0.3 conditional.5
  118.0 68.3 %shard_map.59 = bf16[16,2,1,128,128]{4,3,2,1,0:T(8,128)(2,1)} custom-call(bf16[2,1,128,128]{3,2,1,0:T(8,128)(2,1)S(1)} %get-tuple-element.346.x_ref), custom_call_target="tpu_custom_call" | custom-call | tf_op jit(solution)/shard_map/pallas_call | solution.py:88
  186.9 1.4 fusion.82
  (7 shorter events, 0.1 us)
Async XLA Ops:
  0.0 117.6 %collective-permute-start = (s32[16]{0:T(128)}, s32[16]{0:T(128)S(1)}, u32[]{:S(2)}, u32[]{:S(2)}) collective-permute-start(s32[16]{0:T(128)} %bitcast.137), channel_id=1, source_target_pairs={{16,0},{32,16},{48,32},{64,48},{80,64},{96,80},{112,96},{128,112},... | collective-permute-start | bytes 200 | tf_op jit(solution)/shard_map/ppermute | solution.py:17
  6.6 109.1 %collective-permute-start.1 = (s32[16]{0:T(128)}, s32[16]{0:T(128)S(1)}, u32[]{:S(2)}, u32[]{:S(2)}) collective-permute-start(s32[16]{0:T(128)} %bitcast.138), channel_id=1, source_target_pairs={{496,0},{0,16},{16,32},{32,48},{48,64},{64,80},{80,96},{96,112},{1... | collective-permute-start | bytes 200 | tf_op jit(solution)/shard_map/ppermute | solution.py:17
  15.6 49.6 %copy-start.6 = (s32[1,16]{1,0:T(1,128)S(1)}, s32[1,16]{1,0:T(1,128)}, u32[]{:S(2)}) copy-start(s32[1,16]{1,0:T(1,128)} %param.15) | copy-start | bytes 196
  65.2 52.4 %copy-start.5 = (bf16[1,1,1,128,128]{4,3,2,1,0:T(8,128)(2,1)S(1)}, bf16[1,1,1,128,128]{4,3,2,1,0:T(8,128)(2,1)}, u32[]{:S(2)}) copy-start(bf16[1,1,1,128,128]{4,3,2,1,0:T(8,128)(2,1)} %param.13) | copy-start | bytes 98308
  68.2 8.7 %copy-start.4 = (bf16[2,1,128,128]{3,2,0,1:T(8,128)(2,1)S(1)}, bf16[2,1,128,128]{3,2,0,1:T(8,128)(2,1)}, u32[]{:S(2)}) copy-start(bf16[2,1,128,128]{3,2,0,1:T(8,128)(2,1)} %get-tuple-element.321) | copy-start | bytes 196612 | tf_op jit(solution)/shard_map/cond

commit v6 on v5

--- a/solution.py
+++ b/solution.py
@@ -173,22 +173,22 @@
         return jnp.stack([node_up(tensor_here, child_envs[0][0], child_envs[1][0])])
 
     mid_up = lax.cond(is_mid, mid_work, lambda: zero_envs)
-    next_roles = from_behind(group_roles, "sub", -1)
-    prev_roles = from_behind(group_roles, "sub", 1)
-    every_mid = node_gather(jnp.stack([mid_up, mid_up]), 1, -1)
+    mid_spots = role_spot[top_count : top_count + mid_count]
+    every_mid = node_gather(mid_up, 1)
+    mid_table = jnp.take(every_mid, mid_spots, axis=0)
     top_index = jnp.clip(my_role, 0, top_count - 1)
-    left_spot = role_spot[top_count + top_index]
-    right_spot = placements(next_roles)[top_count + top_count + top_index]
-    left_env = every_mid[left_spot, 0]
-    right_env = every_mid[right_spot, 1]
+    next_half = from_behind(mid_table[top_count:], "sub", -1)
+    right_envs = next_half[top_index]
 
     def top_work():
-        results = [node_down(tensor_here, left_env[t], right_env[t], upper_envs[t]) for t in range(TERMS)]
+        left_env = mid_table[top_index]
+        results = [node_down(tensor_here, left_env[0], right_envs[0], upper_envs[0])]
         return jnp.stack([jnp.stack([r[0] for r in results]), jnp.stack([r[1] for r in results])])
 
     top_down = lax.cond(
         is_top, top_work, lambda: jnp.zeros((2, TERMS, bond_size, bond_size), jnp.bfloat16)
     )
+    prev_roles = from_behind(group_roles, "sub", 1)
     every_top = node_gather(top_down, 2, 1)
     own_field = every_top[role_spot[jnp.clip(mid_index, 0, top_count - 1)], 0]
     other_field = every_top[placements(prev_roles)[jnp.clip(mid_index - top_count, 0, top_count - 1)], 1]

time: 189 us -> 175 us (0.926)
  Pallas kernels: 146 us -> 132 us
  waiting for transfers between devices: 0.01 us -> 4.39 us
  starting transfers between devices: 8.47 us -> 4.33 us
  local copies, waits for them, and re-layouts: 3.83 us -> 6.19 us
    pallas_call x3, Pallas kernels: 146 us -> 132 us  [node_gather(): pl.pallas_call(functools.partial(gather_kernel, n, groups, shift), out_sh...]
    ppermute x2, waiting for transfers between devices: 0.01 us -> 4.39 us  [from_behind(): return lax.ppermute(block, axis, route)]
    ppermute x2, starting transfers between devices: 8.47 us -> 4.33 us  [from_behind(): return lax.ppermute(block, axis, route)]
  transfers between devices with their start and end apart: 2 -> 2, of which waited for: 0 -> 1; matrix products, arithmetic and copies ran while one was open for 12% -> 1% of each run, Pallas kernels for 41% -> 0%
where the time goes in v6:
time: 175 us
  Pallas kernels  132 us (75%)
  matrix products  16.3 us (9%)
  between operations  6.8 us (4%)
  local copies, waits for them, and re-layouts  6.19 us (4%)
  waiting for transfers between devices  4.39 us (3%)
  starting transfers between devices  4.33 us (2%)
  loops' own time  2.9 us (2%)
  other arithmetic  1.97 us (1%)
    pallas_call x3, Pallas kernels, node_gather(): pl.pallas_call(functools.partial(gather_kernel, n, groups, shift), out_sh...  132 us
    dot_general x1, matrix products, node_up(): jnp.einsum('xyq,xyp->qp', tensor_here, second, preferred_element_type=jnp...  8.78 us
    dot_general x1, matrix products, node_up(): jnp.einsum('xa,abp->xbp', left_env, tensor_here, preferred_element_type=j...  7.56 us
    ppermute x2, waiting for transfers between devices, from_behind(): return lax.ppermute(block, axis, route)  4.39 us
    ppermute x2, starting transfers between devices, from_behind(): return lax.ppermute(block, axis, route)  4.33 us
  transfers between devices with their start and end apart: 2, of which 1 were waited for; matrix products, arithmetic and copies ran while one was open for 1% of the time, Pallas kernels for 0%

profile of v6, /device:TPU:32, one launch (start us, length us, event | category | flops | bytes accessed | tf_op | source)
XLA Modules:
  0.0 174.9 jit_solution(2737585451093116074)
XLA Ops:
  0.0 1.2 constant_dynamic-slice_fusion.2
  2.4 0.0 copy-start.5
  2.4 0.0 copy-start.4
  2.5 50.8 %shard_map.57 = bf16[16,1,128,128]{3,2,1,0:T(8,128)(2,1)S(1)} custom-call(bf16[1,128,128]{2,1,0:T(8,128)(2,1)S(1)} %get-tuple-element.171.x_ref), custom_call_target="tpu_custom_call" | custom-call | tf_op jit(solution)/shard_map/pallas_call | solution.py:88
  53.9 0.0 copy-done.5
  53.9 0.1 select_reduce_fusion.1
  54.6 0.1 compare_and_fusion.1
  54.7 0.0 copy-done.4
  54.7 0.0 copy-start.3
  54.7 20.6 %conditional.4 = (bf16[1,128,128]{1,2,0:T(8,128)(2,1)S(1)}) conditional(s32[]{:T(128)} %convert_element_type.74, () %tuple.34, (s32[]{:T(128)}, s32[1,16]{1,0:T(1,128)S(1)}, s32[16]{0:T(128)S(1)}, bf16[16,1,128,128]{3,2,1,0:T(8,128)(2,1)S(1)}, bf16[2,1,128,128]{3,2,0,1:T(8,128)(2,1)}, /*index=5*/bf16[128,128,128]{2,1,0:T(8,128)(2,1)}) %tuple.60), branch_computations={%region_3.4_spmd, %region_4.5_spmd} | conditional | flops 1612825600 | bytes 17732880 | solution.py:175
  54.9 0.7 constant_dynamic-slice_fusion
  56.8 0.1 compare_and_fusion
  56.9 0.6 gather_fusion
  57.4 0.1 bitcast_select_fusion
  57.5 0.0 copy-start.2
  57.5 7.6 %fusion.51 = bf16[128,128,128]{2,0,1:T(8,128)(2,1)} fusion(bf16[128,128,128]{2,1,0:T(8,128)(2,1)} %get-tuple-element.147, bf16[2,1,128,128]{3,2,0,1:T(8,128)(2,1)} %get-tuple-element.146, bf16[4,1,128,128]{3,2,0,1:T(8,128)(2,1)S(1)} %bitcast_select_fusion, s32[]{:T(128)} %bitcast.12, pred[]{:T(512)} %bitcast.9), kind=kOutput, calls=%fused_computation.42 | convolution fusion | flops 536887296 | bytes 8455168 | tf_op jit(solution)/shard_map/cond/branch_1_fun/xa,abp->xbp/dot_general | solution.py:104
  66.5 0.0 copy-done.2
  66.5 8.8 %fusion.60 = bf16[1,128,128]{1,2,0:T(8,128)(2,1)S(1)} fusion(bf16[128,128,128]{2,1,0:T(8,128)(2,1)} %get-tuple-element.147, bf16[128,128,128]{2,0,1:T(8,128)(2,1)} %fusion.51, bf16[2,1,128,128]{3,2,0,1:T(8,128)(2,1)S(1)} %copy-done.2, bf16[4,1,128,128]{3,2,0,1:T(8,128)(2,1)S(1)} %bitcast_select_fusion, s32[]{:T(128)} %bitcast.16, pred[]{:T(512)} %bitcast.15), kind=kOutput, calls=%fused_computation.47 | convolution fusion | flops 1075871744 | bytes 8486917 | tf_op jit(solution)/shard_map/cond/branch_1_fun/xyq,xyp->qp/dot_general | solution.py:110
  75.3 0.7 copy.18.x_ref
  76.0 26.8 %shard_map.58 = bf16[16,1,128,128]{3,2,1,0:T(8,128)(2,1)} custom-call(bf16[1,128,128]{2,1,0:T(8,128)(2,1)} %copy.18.x_ref), custom_call_target="tpu_custom_call" | custom-call | tf_op jit(solution)/shard_map/pallas_call | solution.py:88
  102.8 1.6 gather_fusion.1
  104.5 0.1 bitcast_select_fusion.1
  104.6 1.9 %collective-permute-start = (bf16[4,1,128,128]{3,2,0,1:T(8,128)(2,1)S(1)}, bf16[4,1,128,128]{3,2,0,1:T(8,128)(2,1)S(1)}, u32[]{:S(2)}, u32[]{:S(2)}) collective-permute-start(bf16[4,1,128,128]{3,2,0,1:T(8,128)(2,1)S(1)} %slice.35), channel_id=1, source_target_pairs={{16,0},{32,16},{48,32},{64,48},{80,64},{96,80},{112,96},{128,112},... | collective-permute-start | bytes 393224 | tf_op jit(solution)/shard_map/ppermute | solution.py:17
  106.5 2.4 %collective-permute-start.1 = (s32[16]{0:T(128)S(1)}, s32[16]{0:T(128)S(1)}, u32[]{:S(2)}, u32[]{:S(2)}) collective-permute-start(s32[16]{0:T(128)S(1)} %bitcast.142), channel_id=1, source_target_pairs={{496,0},{0,16},{16,32},{32,48},{48,64},{64,80},{80,96},{96,112},{1... | collective-permute-start | bytes 200 | tf_op jit(solution)/shard_map/ppermute | solution.py:17
  109.5 0.7 dynamic_slice.45
  112.0 4.4 %collective-permute-done.1 = s32[16]{0:T(128)S(1)} collective-permute-done((s32[16]{0:T(128)S(1)}, s32[16]{0:T(128)S(1)}, u32[]{:S(2)}, u32[]{:S(2)}) %collective-permute-start.1) | collective-permute-done | bytes 96 | tf_op jit(solution)/shard_map/ppermute | solution.py:17
  116.4 0.1 select_reduce_fusion
  116.5 0.7 dynamic_slice.47
  119.1 0.0 collective-permute-done
  119.1 0.0 copy-done.3
  119.1 54.4 %shard_map.59 = bf16[16,2,1,128,128]{4,3,2,1,0:T(8,128)(2,1)} custom-call(bf16[2,1,128,128]{3,2,1,0:T(8,128)(2,1)S(1)} %get-tuple-element.181.x_ref), custom_call_target="tpu_custom_call" | custom-call | tf_op jit(solution)/shard_map/pallas_call | solution.py:88
  173.5 1.4 fusion.81
  (7 shorter events, 0.1 us)
Async XLA Ops:
  2.4 51.5 %copy-start.5 = (s32[1,16]{1,0:T(1,128)S(1)}, s32[1,16]{1,0:T(1,128)}, u32[]{:S(2)}) copy-start(s32[1,16]{1,0:T(1,128)} %param.14) | copy-start | bytes 196
  2.4 52.2 %copy-start.4 = (s32[1,16]{1,0:T(1,128)S(1)}, s32[1,16]{1,0:T(1,128)}, u32[]{:S(2)}) copy-start(s32[1,16]{1,0:T(1,128)} %param.15) | copy-start | bytes 196
  54.7 64.4 %copy-start.3 = (bf16[1,1,1,128,128]{4,3,2,1,0:T(8,128)(2,1)S(1)}, bf16[1,1,1,128,128]{4,3,2,1,0:T(8,128)(2,1)}, u32[]{:S(2)}) copy-start(bf16[1,1,1,128,128]{4,3,2,1,0:T(8,128)(2,1)} %param.13) | copy-start | bytes 98308
  57.5 8.9 %copy-start.2 = (bf16[2,1,128,128]{3,2,0,1:T(8,128)(2,1)S(1)}, bf16[2,1,128,128]{3,2,0,1:T(8,128)(2,1)}, u32[]{:S(2)}) copy-start(bf16[2,1,128,128]{3,2,0,1:T(8,128)(2,1)} %get-tuple-element.146) | copy-start | bytes 196612 | tf_op jit(solution)/shard_map/cond
  104.6 14.5 %collective-permute-start = (bf16[4,1,128,128]{3,2,0,1:T(8,128)(2,1)S(1)}, bf16[4,1,128,128]{3,2,0,1:T(8,128)(2,1)S(1)}, u32[]{:S(2)}, u32[]{:S(2)}) collective-permute-start(bf16[4,1,128,128]{3,2,0,1:T(8,128)(2,1)S(1)} %slice.35), channel_id=1, source_target_pairs={{16,0},{32,16},{48,32},{64,48},{80,64},{96,80},{112,96},{128,112},... | collective-permute-start | bytes 393224 | tf_op jit(solution)/shard_map/ppermute | solution.py:17
  106.5 9.9 %collective-permute-start.1 = (s32[16]{0:T(128)S(1)}, s32[16]{0:T(128)S(1)}, u32[]{:S(2)}, u32[]{:S(2)}) collective-permute-start(s32[16]{0:T(128)S(1)} %bitcast.142), channel_id=1, source_target_pairs={{496,0},{0,16},{16,32},{32,48},{48,64},{64,80},{80,96},{96,112},{1... | collective-permute-start | bytes 200 | tf_op jit(solution)/shard_map/ppermute | solution.py:17

commit v7 on v6

--- a/solution.py
+++ b/solution.py
@@ -17,7 +17,7 @@
     return lax.ppermute(block, axis, route)
 
 
-def gather_kernel(n, groups, shift, x_ref, out_ref, send_sem, recv_sem, own_sem, sub_sem):
+def gather_kernel(n, groups, shift, pieces, x_ref, out_ref, send_sem, recv_sem, own_sem, sub_sem):
     me = lax.axis_index("node")
     group = lax.axis_index("sub")
     right = lax.rem(me + 1, n)
@@ -49,13 +49,16 @@
         own.start()
         first_src = x_ref
     ways = ((0, 1, right, n // 2), (1, -1, left, n - 1 - n // 2))
-
-    def hop(way, target, step, origin):
+    rows = x_ref.shape[-2] // pieces
+    lead = (slice(None),) * (len(x_ref.shape) - 2)
+
+    def hop(way, target, step, origin, piece):
+        part = lead + (pl.ds(piece * rows, rows), slice(None))
         return pltpu.make_async_remote_copy(
-            src_ref=first_src if step == 0 else out_ref.at[origin],
-            dst_ref=out_ref.at[origin],
-            send_sem=send_sem.at[way, step],
-            recv_sem=recv_sem.at[way, step],
+            src_ref=(first_src if step == 0 else out_ref.at[origin]).at[part],
+            dst_ref=out_ref.at[origin].at[part],
+            send_sem=send_sem.at[way, step, piece],
+            recv_sem=recv_sem.at[way, step, piece],
             device_id=(group, target),
             device_id_type=MESH,
         )
@@ -66,14 +69,16 @@
             if step >= steps:
                 continue
             origin = lax.rem(me - sign * step + 2 * n, n)
-            if step > 0:
-                hop(way, target, step - 1, origin).wait_recv()
-            copy = hop(way, target, step, origin)
-            copy.start()
-            sent.append(copy)
+            for piece in range(pieces):
+                if step > 0:
+                    hop(way, target, step - 1, origin, piece).wait_recv()
+                copy = hop(way, target, step, origin, piece)
+                copy.start()
+                sent.append(copy)
     for way, sign, target, steps in ways:
         origin = lax.rem(me - sign * steps + 2 * n, n)
-        hop(way, target, steps - 1, origin).wait_recv()
+        for piece in range(pieces):
+            hop(way, target, steps - 1, origin, piece).wait_recv()
     for copy in sent:
         copy.wait_send()
     if shift:
@@ -82,17 +87,17 @@
         own.wait()
 
 
-def node_gather(block, collective_id, shift=0):
+def node_gather(block, collective_id, shift=0, pieces=2):
     n = lax.axis_size("node")
     groups = lax.axis_size("sub")
     return pl.pallas_call(
-        functools.partial(gather_kernel, n, groups, shift),
+        functools.partial(gather_kernel, n, groups, shift, pieces),
         out_shape=jax.ShapeDtypeStruct((n,) + block.shape, block.dtype),
         in_specs=[pl.BlockSpec(memory_space=pltpu.VMEM)],
         out_specs=pl.BlockSpec(memory_space=pltpu.VMEM),
         scratch_shapes=[
-            pltpu.SemaphoreType.DMA((2, n // 2)),
-            pltpu.SemaphoreType.DMA((2, n // 2)),
+            pltpu.SemaphoreType.DMA((2, n // 2, pieces)),
+            pltpu.SemaphoreType.DMA((2, n // 2, pieces)),
             pltpu.SemaphoreType.DMA,
             pltpu.SemaphoreType.DMA((2,)),
         ],

time: 175 us -> 171 us (0.977)
  the two profiles are of different devices: /device:TPU:32 before, /device:TPU:24 now
where the time goes in v7:
time: 171 us; the launch traced here: 170 us
  Pallas kernels  130 us (76%)
  matrix products  16.3 us (10%)
  between operations  6.8 us (4%)
  local copies, waits for them, and re-layouts  6.19 us (4%)
  starting transfers between devices  4.33 us (3%)
  loops' own time  2.9 us (2%)
  other arithmetic  1.97 us (1%)
    pallas_call x3, Pallas kernels, node_gather(): pl.pallas_call(functools.partial(gather_kernel, n, groups, shift, pieces)...  130 us
    dot_general x1, matrix products, node_up(): jnp.einsum('xyq,xyp->qp', tensor_here, second, preferred_element_type=jnp...  8.78 us
    dot_general x1, matrix products, node_up(): jnp.einsum('xa,abp->xbp', left_env, tensor_here, preferred_element_type=j...  7.56 us
    ppermute x2, starting transfers between devices, from_behind(): return lax.ppermute(block, axis, route)  4.33 us
  transfers between devices with their start and end apart: 2, of which 1 were waited for; matrix products, arithmetic and copies ran while one was open for 1% of the time, Pallas kernels for 0%

profile of v7, /device:TPU:24, one launch (start us, length us, event | category | flops | bytes accessed | tf_op | source)
XLA Modules:
  0.0 170.1 jit_solution(4801654314083878808)
XLA Ops:
  0.0 1.2 constant_dynamic-slice_fusion.2
  2.4 0.0 copy-start.5
  2.4 0.0 copy-start.4
  2.5 50.0 %shard_map.57 = bf16[16,1,128,128]{3,2,1,0:T(8,128)(2,1)S(1)} custom-call(bf16[1,128,128]{2,1,0:T(8,128)(2,1)S(1)} %get-tuple-element.171.x_ref), custom_call_target="tpu_custom_call" | custom-call | tf_op jit(solution)/shard_map/pallas_call | solution.py:93
  53.0 0.0 copy-done.5
  53.1 0.1 select_reduce_fusion.1
  53.8 0.1 compare_and_fusion.1
  53.8 0.0 copy-done.4
  53.8 0.0 copy-start.3
  53.8 20.6 %conditional.4 = (bf16[1,128,128]{1,2,0:T(8,128)(2,1)S(1)}) conditional(s32[]{:T(128)} %convert_element_type.74, () %tuple.34, (s32[]{:T(128)}, s32[1,16]{1,0:T(1,128)S(1)}, s32[16]{0:T(128)S(1)}, bf16[16,1,128,128]{3,2,1,0:T(8,128)(2,1)S(1)}, bf16[2,1,128,128]{3,2,0,1:T(8,128)(2,1)}, /*index=5*/bf16[128,128,128]{2,1,0:T(8,128)(2,1)}) %tuple.60), branch_computations={%region_3.4_spmd, %region_4.5_spmd} | conditional | flops 1612825600 | bytes 17732880 | solution.py:180
  54.1 0.7 constant_dynamic-slice_fusion
  56.0 0.1 compare_and_fusion
  56.0 0.6 gather_fusion
  56.6 0.1 bitcast_select_fusion
  56.7 0.0 copy-start.2
  56.7 7.6 %fusion.51 = bf16[128,128,128]{2,0,1:T(8,128)(2,1)} fusion(bf16[128,128,128]{2,1,0:T(8,128)(2,1)} %get-tuple-element.147, bf16[2,1,128,128]{3,2,0,1:T(8,128)(2,1)} %get-tuple-element.146, bf16[4,1,128,128]{3,2,0,1:T(8,128)(2,1)S(1)} %bitcast_select_fusion, s32[]{:T(128)} %bitcast.12, pred[]{:T(512)} %bitcast.9), kind=kOutput, calls=%fused_computation.42 | convolution fusion | flops 536887296 | bytes 8455168 | tf_op jit(solution)/shard_map/cond/branch_1_fun/xa,abp->xbp/dot_general | solution.py:109
  65.7 0.0 copy-done.2
  65.7 8.8 %fusion.60 = bf16[1,128,128]{1,2,0:T(8,128)(2,1)S(1)} fusion(bf16[128,128,128]{2,1,0:T(8,128)(2,1)} %get-tuple-element.147, bf16[128,128,128]{2,0,1:T(8,128)(2,1)} %fusion.51, bf16[2,1,128,128]{3,2,0,1:T(8,128)(2,1)S(1)} %copy-done.2, bf16[4,1,128,128]{3,2,0,1:T(8,128)(2,1)S(1)} %bitcast_select_fusion, s32[]{:T(128)} %bitcast.16, pred[]{:T(512)} %bitcast.15), kind=kOutput, calls=%fused_computation.47 | convolution fusion | flops 1075871744 | bytes 8486917 | tf_op jit(solution)/shard_map/cond/branch_1_fun/xyq,xyp->qp/dot_general | solution.py:115
  74.5 0.7 copy.18.x_ref
  75.2 28.0 %shard_map.58 = bf16[16,1,128,128]{3,2,1,0:T(8,128)(2,1)} custom-call(bf16[1,128,128]{2,1,0:T(8,128)(2,1)} %copy.18.x_ref), custom_call_target="tpu_custom_call" | custom-call | tf_op jit(solution)/shard_map/pallas_call | solution.py:93
  103.2 1.6 gather_fusion.1
  104.9 0.1 bitcast_select_fusion.1
  105.0 1.9 %collective-permute-start = (bf16[4,1,128,128]{3,2,0,1:T(8,128)(2,1)S(1)}, bf16[4,1,128,128]{3,2,0,1:T(8,128)(2,1)S(1)}, u32[]{:S(2)}, u32[]{:S(2)}) collective-permute-start(bf16[4,1,128,128]{3,2,0,1:T(8,128)(2,1)S(1)} %slice.35), channel_id=1, source_target_pairs={{16,0},{32,16},{48,32},{64,48},{80,64},{96,80},{112,96},{128,112},... | collective-permute-start | bytes 393224 | tf_op jit(solution)/shard_map/ppermute | solution.py:17
  106.9 2.4 %collective-permute-start.1 = (s32[16]{0:T(128)S(1)}, s32[16]{0:T(128)S(1)}, u32[]{:S(2)}, u32[]{:S(2)}) collective-permute-start(s32[16]{0:T(128)S(1)} %bitcast.142), channel_id=1, source_target_pairs={{496,0},{0,16},{16,32},{32,48},{48,64},{64,80},{80,96},{96,112},{1... | collective-permute-start | bytes 200 | tf_op jit(solution)/shard_map/ppermute | solution.py:17
  109.9 0.7 dynamic_slice.45
  112.4 1.4 collective-permute-done.1
  113.9 0.1 select_reduce_fusion
  114.0 0.7 dynamic_slice.47
  116.5 0.0 collective-permute-done
  116.5 0.0 copy-done.3
  116.6 52.1 %shard_map.59 = bf16[16,2,1,128,128]{4,3,2,1,0:T(8,128)(2,1)} custom-call(bf16[2,1,128,128]{3,2,1,0:T(8,128)(2,1)S(1)} %get-tuple-element.181.x_ref), custom_call_target="tpu_custom_call" | custom-call | tf_op jit(solution)/shard_map/pallas_call | solution.py:93
  168.7 1.4 fusion.81
  (7 shorter events, 0.1 us)
Async XLA Ops:
  2.4 50.6 %copy-start.5 = (s32[1,16]{1,0:T(1,128)S(1)}, s32[1,16]{1,0:T(1,128)}, u32[]{:S(2)}) copy-start(s32[1,16]{1,0:T(1,128)} %param.14) | copy-start | bytes 196
  2.4 51.4 %copy-start.4 = (s32[1,16]{1,0:T(1,128)S(1)}, s32[1,16]{1,0:T(1,128)}, u32[]{:S(2)}) copy-start(s32[1,16]{1,0:T(1,128)} %param.15) | copy-start | bytes 196
  53.8 62.7 %copy-start.3 = (bf16[1,1,1,128,128]{4,3,2,1,0:T(8,128)(2,1)S(1)}, bf16[1,1,1,128,128]{4,3,2,1,0:T(8,128)(2,1)}, u32[]{:S(2)}) copy-start(bf16[1,1,1,128,128]{4,3,2,1,0:T(8,128)(2,1)} %param.13) | copy-start | bytes 98308
  56.7 8.9 %copy-start.2 = (bf16[2,1,128,128]{3,2,0,1:T(8,128)(2,1)S(1)}, bf16[2,1,128,128]{3,2,0,1:T(8,128)(2,1)}, u32[]{:S(2)}) copy-start(bf16[2,1,128,128]{3,2,0,1:T(8,128)(2,1)} %get-tuple-element.146) | copy-start | bytes 196612 | tf_op jit(solution)/shard_map/cond
  105.0 11.5 %collective-permute-start = (bf16[4,1,128,128]{3,2,0,1:T(8,128)(2,1)S(1)}, bf16[4,1,128,128]{3,2,0,1:T(8,128)(2,1)S(1)}, u32[]{:S(2)}, u32[]{:S(2)}) collective-permute-start(bf16[4,1,128,128]{3,2,0,1:T(8,128)(2,1)S(1)} %slice.35), channel_id=1, source_target_pairs={{16,0},{32,16},{48,32},{64,48},{80,64},{96,80},{112,96},{128,112},... | collective-permute-start | bytes 393224 | tf_op jit(solution)/shard_map/ppermute | solution.py:17
  106.9 7.0 %collective-permute-start.1 = (s32[16]{0:T(128)S(1)}, s32[16]{0:T(128)S(1)}, u32[]{:S(2)}, u32[]{:S(2)}) collective-permute-start(s32[16]{0:T(128)S(1)} %bitcast.142), channel_id=1, source_target_pairs={{496,0},{0,16},{16,32},{32,48},{48,64},{64,80},{80,96},{96,112},{1... | collective-permute-start | bytes 200 | tf_op jit(solution)/shard_map/ppermute | solution.py:17

commit v8 on v7

--- a/solution.py
+++ b/solution.py
@@ -178,12 +178,12 @@
         return jnp.stack([node_up(tensor_here, child_envs[0][0], child_envs[1][0])])
 
     mid_up = lax.cond(is_mid, mid_work, lambda: zero_envs)
-    mid_spots = role_spot[top_count : top_count + mid_count]
-    every_mid = node_gather(mid_up, 1)
-    mid_table = jnp.take(every_mid, mid_spots, axis=0)
+    next_roles = from_behind(group_roles, "sub", -1)
+    every_mid = node_gather(jnp.stack([mid_up, mid_up]), 1, -1)
     top_index = jnp.clip(my_role, 0, top_count - 1)
-    next_half = from_behind(mid_table[top_count:], "sub", -1)
-    right_envs = next_half[top_index]
+    mid_table = jnp.take(every_mid[:, 0], role_spot[top_count : top_count + mid_count], axis=0)
+    next_spots = placements(next_roles)[top_count + top_count : top_count + mid_count]
+    right_envs = jnp.take(every_mid[:, 1], next_spots, axis=0)[top_index]
 
     def top_work():
         left_env = mid_table[top_index]

time: 171 us -> 180 us (1.053)
  the two profiles are of different devices: /device:TPU:24 before, /device:TPU:32 now
where the time goes in v8:
time: 180 us; the launch traced here: 179 us
  Pallas kernels  135 us (75%)
  matrix products  16.3 us (9%)
  starting transfers between devices  8.47 us (5%)
  between operations  7.22 us (4%)
  local copies, waits for them, and re-layouts  5.51 us (3%)
  other arithmetic  3.31 us (2%)
  loops' own time  3.1 us (2%)
    pallas_call x3, Pallas kernels, node_gather(): pl.pallas_call(functools.partial(gather_kernel, n, groups, shift, pieces)...  135 us
    dot_general x1, matrix products, node_up(): jnp.einsum('xyq,xyp->qp', tensor_here, second, preferred_element_type=jnp...  8.79 us
    ppermute x2, starting transfers between devices, from_behind(): return lax.ppermute(block, axis, route)  8.47 us
    dot_general x1, matrix products, node_up(): jnp.einsum('xa,abp->xbp', left_env, tensor_here, preferred_element_type=j...  7.55 us
  transfers between devices with their start and end apart: 2, of which 0 were waited for; matrix products, arithmetic and copies ran while one was open for 13% of the time, Pallas kernels for 44%

profile of v8, /device:TPU:32, one launch (start us, length us, event | category | flops | bytes accessed | tf_op | source)
XLA Modules:
  0.0 179.0 jit_solution(10558993601794699690)
XLA Ops:
  0.0 6.5 %collective-permute-start = (s32[16]{0:T(128)}, s32[16]{0:T(128)S(1)}, u32[]{:S(2)}, u32[]{:S(2)}) collective-permute-start(s32[16]{0:T(128)} %bitcast.146), channel_id=1, source_target_pairs={{16,0},{32,16},{48,32},{64,48},{80,64},{96,80},{112,96},{128,112},... | collective-permute-start | bytes 200 | tf_op jit(solution)/shard_map/ppermute | solution.py:17
  6.6 1.9 %collective-permute-start.1 = (s32[16]{0:T(128)}, s32[16]{0:T(128)S(1)}, u32[]{:S(2)}, u32[]{:S(2)}) collective-permute-start(s32[16]{0:T(128)} %bitcast.147), channel_id=1, source_target_pairs={{496,0},{0,16},{16,32},{32,48},{48,64},{64,80},{80,96},{96,112},{1... | collective-permute-start | bytes 200 | tf_op jit(solution)/shard_map/ppermute | solution.py:17
  8.5 0.8 select_reduce_fusion.2
  9.3 1.2 constant_dynamic-slice_fusion.2
  13.1 0.1 compare_select_fusion.2
  13.8 0.6 dynamic_slice.45
  15.7 0.0 copy-start.4
  15.7 50.7 %shard_map.57 = bf16[16,1,128,128]{3,2,1,0:T(8,128)(2,1)} custom-call(bf16[1,128,128]{2,1,0:T(8,128)(2,1)S(1)} %get-tuple-element.198.x_ref), custom_call_target="tpu_custom_call" | custom-call | tf_op jit(solution)/shard_map/pallas_call | solution.py:93
  66.5 1.6 gather_fusion.1
  68.1 0.0 copy-done.4
  68.1 0.0 copy-start.3
  68.1 19.9 %conditional.4 = (bf16[1,128,128]{1,2,0:T(8,128)(2,1)S(1)}) conditional(s32[]{:T(128)} %convert_element_type.78, () %tuple.42, (s32[]{:T(128)}, s32[1,16]{1,0:T(1,128)S(1)}, s32[4]{0:T(128)S(1)}, bf16[2,1,128,128]{3,2,1,0:T(8,128)(2,1)}, bf16[128,128,128]{2,1,0:T(8,128)(2,1)}, /*index=5*/bf16[4,1,128,128]{3,2,0,1:T(8,128)(2,1)S(1)}, ...), branch_computations={%region_3.5_spmd, %region_4.6_spmd} | conditional | flops 1612824576 | bytes 17597700 | solution.py:180
  68.4 0.7 constant_dynamic-slice_fusion
  70.4 0.1 select_bitcast_fusion
  70.5 0.0 copy-start.2
  70.5 7.5 %fusion.24 = bf16[128,128,128]{2,0,1:T(8,128)(2,1)} fusion(bf16[128,128,128]{2,1,0:T(8,128)(2,1)} %get-tuple-element.165, bf16[2,1,128,128]{3,2,1,0:T(8,128)(2,1)} %get-tuple-element.164, bf16[4,1,128,128]{3,2,1,0:T(8,128)(2,1)S(1)} %select_bitcast_fusion, s32[]{:T(128)} %bitcast.10, pred[]{:T(512)} %bitcast.8), kind=kOutput, calls=%fused_computation.21 | convolution fusion | flops 536887296 | bytes 8455168 | tf_op jit(solution)/shard_map/cond/branch_1_fun/xa,abp->xbp/dot_general | solution.py:109
  79.2 0.0 copy-done.2
  79.2 8.8 %fusion.33 = bf16[1,128,128]{1,2,0:T(8,128)(2,1)S(1)} fusion(bf16[128,128,128]{2,1,0:T(8,128)(2,1)} %get-tuple-element.165, bf16[128,128,128]{2,0,1:T(8,128)(2,1)} %fusion.24, bf16[2,1,128,128]{3,2,1,0:T(8,128)(2,1)S(1)} %copy-done.2, bf16[4,1,128,128]{3,2,1,0:T(8,128)(2,1)S(1)} %select_bitcast_fusion, s32[]{:T(128)} %bitcast.14, pred[]{:T(512)} %bitcast.13), kind=kOutput, calls=%fused_computation.26 | convolution fusion | flops 1075871744 | bytes 8486917 | tf_op jit(solution)/shard_map/cond/branch_1_fun/xyq,xyp->qp/dot_general | solution.py:115
  88.0 0.1 copy.17
  88.1 0.6 pad_maximum_fusion.1.x_ref
  88.8 28.9 %shard_map.58 = bf16[16,2,1,128,128]{4,3,2,1,0:T(8,128)(2,1)S(1)} custom-call(bf16[2,1,128,128]{3,2,1,0:T(8,128)(2,1)} %pad_maximum_fusion.1.x_ref), custom_call_target="tpu_custom_call" | custom-call | tf_op jit(solution)/shard_map/pallas_call | solution.py:93
  118.4 0.0 collective-permute-done.1
  118.4 0.1 select_reduce_fusion
  118.5 0.6 dynamic_slice.47
  120.4 0.0 collective-permute-done
  120.4 0.1 select_reduce_fusion.1
  120.5 0.1 compare_select_fusion.1
  120.6 0.6 gather_fusion.2
  121.2 0.0 copy-done.3
  121.2 0.3 conditional.5
  121.5 55.4 %shard_map.59 = bf16[16,2,1,128,128]{4,3,2,1,0:T(8,128)(2,1)} custom-call(bf16[2,1,128,128]{3,2,1,0:T(8,128)(2,1)S(1)} %get-tuple-element.228.x_ref), custom_call_target="tpu_custom_call" | custom-call | tf_op jit(solution)/shard_map/pallas_call | solution.py:93
  177.6 1.4 fusion.90
  (9 shorter events, 0.1 us)
Async XLA Ops:
  0.0 120.4 %collective-permute-start = (s32[16]{0:T(128)}, s32[16]{0:T(128)S(1)}, u32[]{:S(2)}, u32[]{:S(2)}) collective-permute-start(s32[16]{0:T(128)} %bitcast.146), channel_id=1, source_target_pairs={{16,0},{32,16},{48,32},{64,48},{80,64},{96,80},{112,96},{128,112},... | collective-permute-start | bytes 200 | tf_op jit(solution)/shard_map/ppermute | solution.py:17
  6.6 111.8 %collective-permute-start.1 = (s32[16]{0:T(128)}, s32[16]{0:T(128)S(1)}, u32[]{:S(2)}, u32[]{:S(2)}) collective-permute-start(s32[16]{0:T(128)} %bitcast.147), channel_id=1, source_target_pairs={{496,0},{0,16},{16,32},{32,48},{48,64},{64,80},{80,96},{96,112},{1... | collective-permute-start | bytes 200 | tf_op jit(solution)/shard_map/ppermute | solution.py:17
  15.7 52.4 %copy-start.4 = (s32[1,16]{1,0:T(1,128)S(1)}, s32[1,16]{1,0:T(1,128)}, u32[]{:S(2)}) copy-start(s32[1,16]{1,0:T(1,128)} %param.17) | copy-start | bytes 196
  68.1 53.0 %copy-start.3 = (bf16[1,1,1,128,128]{4,3,2,1,0:T(8,128)(2,1)S(1)}, bf16[1,1,1,128,128]{4,3,2,1,0:T(8,128)(2,1)}, u32[]{:S(2)}) copy-start(bf16[1,1,1,128,128]{4,3,2,1,0:T(8,128)(2,1)} %param.15) | copy-start | bytes 98308
  70.5 8.7 %copy-start.2 = (bf16[2,1,128,128]{3,2,1,0:T(8,128)(2,1)S(1)}, bf16[2,1,128,128]{3,2,1,0:T(8,128)(2,1)}, u32[]{:S(2)}) copy-start(bf16[2,1,128,128]{3,2,1,0:T(8,128)(2,1)} %get-tuple-element.164) | copy-start | bytes 196612 | tf_op jit(solution)/shard_map/cond

commit v9 on v8

--- a/solution.py
+++ b/solution.py
@@ -17,7 +17,11 @@
     return lax.ppermute(block, axis, route)
 
 
-def gather_kernel(n, groups, shift, pieces, x_ref, out_ref, send_sem, recv_sem, own_sem, sub_sem):
+def gather_kernel(n, groups, shift, pieces, *refs):
+    if shift:
+        x_ref, roles_ref, out_ref, roles_out, send_sem, recv_sem, own_sem, sub_sem = refs
+    else:
+        x_ref, out_ref, send_sem, recv_sem, own_sem, sub_sem = refs
     me = lax.axis_index("node")
     group = lax.axis_index("sub")
     right = lax.rem(me + 1, n)
@@ -41,6 +45,15 @@
             device_id_type=MESH,
         )
         across.start()
+        roles_across = pltpu.make_async_remote_copy(
+            src_ref=roles_ref,
+            dst_ref=roles_out,
+            send_sem=sub_sem.at[2],
+            recv_sem=sub_sem.at[3],
+            device_id=peers[2],
+            device_id_type=MESH,
+        )
+        roles_across.start()
         own.wait()
         across.wait_recv()
         first_src = out_ref.at[me]
@@ -83,26 +96,31 @@
         copy.wait_send()
     if shift:
         across.wait_send()
+        roles_across.wait_send()
+        roles_across.wait_recv()
     else:
         own.wait()
 
 
-def node_gather(block, collective_id, shift=0, pieces=2):
+def node_gather(block, collective_id, shift=0, roles=None, pieces=2):
     n = lax.axis_size("node")
     groups = lax.axis_size("sub")
+    vmem = pl.BlockSpec(memory_space=pltpu.VMEM)
+    gathered = jax.ShapeDtypeStruct((n,) + block.shape, block.dtype)
+    operands = (block,) if roles is None else (block, roles)
     return pl.pallas_call(
         functools.partial(gather_kernel, n, groups, shift, pieces),
-        out_shape=jax.ShapeDtypeStruct((n,) + block.shape, block.dtype),
-        in_specs=[pl.BlockSpec(memory_space=pltpu.VMEM)],
-        out_specs=pl.BlockSpec(memory_space=pltpu.VMEM),
+        out_shape=gathered if roles is None else (gathered, jax.ShapeDtypeStruct(roles.shape, roles.dtype)),
+        in_specs=[vmem] * len(operands),
+        out_specs=vmem if roles is None else (vmem, vmem),
         scratch_shapes=[
             pltpu.SemaphoreType.DMA((2, n // 2, pieces)),
             pltpu.SemaphoreType.DMA((2, n // 2, pieces)),
             pltpu.SemaphoreType.DMA,
-            pltpu.SemaphoreType.DMA((2,)),
+            pltpu.SemaphoreType.DMA((4,)),
         ],
         compiler_params=pltpu.CompilerParams(collective_id=collective_id, has_side_effects=True),
-    )(block)
+    )(*operands)
 
 
 def node_up(tensor_here, left_env, right_env):
@@ -178,11 +196,10 @@
         return jnp.stack([node_up(tensor_here, child_envs[0][0], child_envs[1][0])])
 
     mid_up = lax.cond(is_mid, mid_work, lambda: zero_envs)
-    next_roles = from_behind(group_roles, "sub", -1)
-    every_mid = node_gather(jnp.stack([mid_up, mid_up]), 1, -1)
+    every_mid, next_roles = node_gather(jnp.stack([mid_up, mid_up]), 1, -1, role_map)
     top_index = jnp.clip(my_role, 0, top_count - 1)
     mid_table = jnp.take(every_mid[:, 0], role_spot[top_count : top_count + mid_count], axis=0)
-    next_spots = placements(next_roles)[top_count + top_count : top_count + mid_count]
+    next_spots = placements(next_roles[0])[top_count + top_count : top_count + mid_count]
     right_envs = jnp.take(every_mid[:, 1], next_spots, axis=0)[top_index]
 
     def top_work():
@@ -193,10 +210,9 @@
     top_down = lax.cond(
         is_top, top_work, lambda: jnp.zeros((2, TERMS, bond_size, bond_size), jnp.bfloat16)
     )
-    prev_roles = from_behind(group_roles, "sub", 1)
-    every_top = node_gather(top_down, 2, 1)
+    every_top, prev_roles = node_gather(top_down, 2, 1, role_map)
     own_field = every_top[role_spot[jnp.clip(mid_index, 0, top_count - 1)], 0]
-    other_field = every_top[placements(prev_roles)[jnp.clip(mid_index - top_count, 0, top_count - 1)], 1]
+    other_field = every_top[placements(prev_roles[0])[jnp.clip(mid_index - top_count, 0, top_count - 1)], 1]
     mid_field = jnp.where(mid_index < top_count, own_field, other_field)
     result = jnp.where(is_mid, mid_field, jnp.where(is_leaf, leaf_up, zero_envs))
     return result[None, None]

time: 180 us -> 173 us (0.961)
  the two profiles are of different devices: /device:TPU:32 before, /device:TPU:24 now
where the time goes in v9:
time: 173 us
  Pallas kernels  137 us (79%)
  matrix products  16.3 us (9%)
  between operations  7.3 us (4%)
  local copies, waits for them, and re-layouts  5.4 us (3%)
  other arithmetic  3.98 us (2%)
  loops' own time  2.79 us (2%)
    pallas_call x3, Pallas kernels, node_gather(): pl.pallas_call(functools.partial(gather_kernel, n, groups, shift, pieces)...  137 us
    dot_general x1, matrix products, node_up(): jnp.einsum('xyq,xyp->qp', tensor_here, second, preferred_element_type=jnp...  8.78 us
    dot_general x1, matrix products, node_up(): jnp.einsum('xa,abp->xbp', left_env, tensor_here, preferred_element_type=j...  7.55 us

profile of v9, /device:TPU:24, one launch (start us, length us, event | category | flops | bytes accessed | tf_op | source)
XLA Modules:
  0.0 172.9 jit_solution(13049058645548542690)
XLA Ops:
  0.0 1.2 constant_dynamic-slice_fusion.2
  1.9 0.0 copy-start.4
  1.9 0.0 copy-start.5
  1.9 50.9 %shard_map.57 = bf16[16,1,128,128]{3,2,1,0:T(8,128)(2,1)} custom-call(bf16[1,128,128]{2,1,0:T(8,128)(2,1)S(1)} %get-tuple-element.206.refs_0_), custom_call_target="tpu_custom_call" | custom-call | tf_op jit(solution)/shard_map/pallas_call | solution.py:111
  52.9 0.0 copy-done.4
  52.9 0.1 select_reduce_fusion.2
  53.0 0.1 compare_select_fusion.2
  53.1 1.6 gather_fusion.1
  56.7 0.0 copy-done.5
  56.7 0.0 copy-start.3
  56.7 19.5 %conditional.4 = (bf16[1,128,128]{1,2,0:T(8,128)(2,1)S(1)}) conditional(s32[]{:T(128)} %convert_element_type.78, () %tuple.42, (s32[]{:T(128)}, s32[1,16]{1,0:T(1,128)S(1)}, s32[4]{0:T(128)S(1)}, bf16[2,1,128,128]{3,2,1,0:T(8,128)(2,1)}, bf16[128,128,128]{2,1,0:T(8,128)(2,1)}, /*index=5*/bf16[4,1,128,128]{3,2,0,1:T(8,128)(2,1)S(1)}, ...), branch_computations={%region_3.5_spmd, %region_4.6_spmd} | conditional | flops 1612824576 | bytes 17597700 | solution.py:198
  56.9 0.6 constant_dynamic-slice_fusion
  58.7 0.1 select_bitcast_fusion
  58.7 0.0 copy-start.2
  58.8 7.5 %fusion.24 = bf16[128,128,128]{2,0,1:T(8,128)(2,1)} fusion(bf16[128,128,128]{2,1,0:T(8,128)(2,1)} %get-tuple-element.165, bf16[2,1,128,128]{3,2,1,0:T(8,128)(2,1)} %get-tuple-element.164, bf16[4,1,128,128]{3,2,1,0:T(8,128)(2,1)S(1)} %select_bitcast_fusion, s32[]{:T(128)} %bitcast.10, pred[]{:T(512)} %bitcast.8), kind=kOutput, calls=%fused_computation.21 | convolution fusion | flops 536887296 | bytes 8455168 | tf_op jit(solution)/shard_map/cond/branch_1_fun/xa,abp->xbp/dot_general | solution.py:127
  67.4 0.0 copy-done.2
  67.4 8.8 %fusion.33 = bf16[1,128,128]{1,2,0:T(8,128)(2,1)S(1)} fusion(bf16[128,128,128]{2,1,0:T(8,128)(2,1)} %get-tuple-element.165, bf16[128,128,128]{2,0,1:T(8,128)(2,1)} %fusion.24, bf16[2,1,128,128]{3,2,1,0:T(8,128)(2,1)S(1)} %copy-done.2, bf16[4,1,128,128]{3,2,1,0:T(8,128)(2,1)S(1)} %select_bitcast_fusion, s32[]{:T(128)} %bitcast.14, pred[]{:T(512)} %bitcast.13), kind=kOutput, calls=%fused_computation.26 | convolution fusion | flops 1075871744 | bytes 8486917 | tf_op jit(solution)/shard_map/cond/branch_1_fun/xyq,xyp->qp/dot_general | solution.py:133
  76.2 0.1 copy.17
  76.4 0.6 pad_maximum_fusion.1.refs_0_
  77.0 30.4 %shard_map.58 = (bf16[16,2,1,128,128]{4,3,2,1,0:T(8,128)(2,1)S(1)}, s32[1,16]{1,0:T(1,128)}) custom-call(bf16[2,1,128,128]{3,2,1,0:T(8,128)(2,1)} %pad_maximum_fusion.1.refs_0_, s32[1,16]{1,0:T(1,128)} %refs_1_.3), custom_call_target="tpu_custom_call" | custom-call | tf_op jit(solution)/shard_map/pallas_call | solution.py:111
  107.4 0.8 select_reduce_fusion.1
  108.2 0.1 compare_select_fusion.1
  108.3 0.6 gather_fusion.2
  109.5 0.0 copy-done.3
  109.5 0.3 conditional.5
  109.8 55.8 %shard_map.59 = (bf16[16,2,1,128,128]{4,3,2,1,0:T(8,128)(2,1)}, s32[1,16]{1,0:T(1,128)}) custom-call(bf16[2,1,128,128]{3,2,1,0:T(8,128)(2,1)S(1)} %get-tuple-element.236.refs_0_, s32[1,16]{1,0:T(1,128)} %refs_1_.3), custom_call_target="tpu_custom_call" | custom-call | tf_op jit(solution)/shard_map/pallas_call | solution.py:111
  165.7 0.8 select_reduce_fusion
  166.4 0.6 dynamic_slice.47
  169.0 0.6 dynamic_slice.45
  171.5 1.4 fusion.90
  (9 shorter events, 0.1 us)
Async XLA Ops:
  1.9 51.0 %copy-start.4 = (s32[1,16]{1,0:T(1,128)S(1)}, s32[1,16]{1,0:T(1,128)}, u32[]{:S(2)}) copy-start(s32[1,16]{1,0:T(1,128)} %refs_1_.3) | copy-start | bytes 196
  1.9 54.8 %copy-start.5 = (s32[1,16]{1,0:T(1,128)S(1)}, s32[1,16]{1,0:T(1,128)}, u32[]{:S(2)}) copy-start(s32[1,16]{1,0:T(1,128)} %param.17) | copy-start | bytes 196
  56.7 52.8 %copy-start.3 = (bf16[1,1,1,128,128]{4,3,2,1,0:T(8,128)(2,1)S(1)}, bf16[1,1,1,128,128]{4,3,2,1,0:T(8,128)(2,1)}, u32[]{:S(2)}) copy-start(bf16[1,1,1,128,128]{4,3,2,1,0:T(8,128)(2,1)} %param.15) | copy-start | bytes 98308
  58.7 8.7 %copy-start.2 = (bf16[2,1,128,128]{3,2,1,0:T(8,128)(2,1)S(1)}, bf16[2,1,128,128]{3,2,1,0:T(8,128)(2,1)}, u32[]{:S(2)}) copy-start(bf16[2,1,128,128]{3,2,1,0:T(8,128)(2,1)} %get-tuple-element.164) | copy-start | bytes 196612 | tf_op jit(solution)/shard_map/cond

commit v10 on v9

--- a/solution.py
+++ b/solution.py
@@ -17,8 +17,8 @@
     return lax.ppermute(block, axis, route)
 
 
-def gather_kernel(n, groups, shift, pieces, *refs):
-    if shift:
+def gather_kernel(n, groups, shift, pieces, with_roles, *refs):
+    if with_roles:
         x_ref, roles_ref, out_ref, roles_out, send_sem, recv_sem, own_sem, sub_sem = refs
     else:
         x_ref, out_ref, send_sem, recv_sem, own_sem, sub_sem = refs
@@ -45,15 +45,19 @@
             device_id_type=MESH,
         )
         across.start()
-        roles_across = pltpu.make_async_remote_copy(
-            src_ref=roles_ref,
-            dst_ref=roles_out,
-            send_sem=sub_sem.at[2],
-            recv_sem=sub_sem.at[3],
-            device_id=peers[2],
-            device_id_type=MESH,
-        )
-        roles_across.start()
+        roles_across = [
+            pltpu.make_async_remote_copy(
+                src_ref=roles_ref,
+                dst_ref=roles_out.at[side],
+                send_sem=sub_sem.at[2 + 2 * side],
+                recv_sem=sub_sem.at[3 + 2 * side],
+                device_id=peers[2 + side],
+                device_id_type=MESH,
+            )
+            for side in range(2 if with_roles else 0)
+        ]
+        for copy in roles_across:
+            copy.start()
         own.wait()
         across.wait_recv()
         first_src = out_ref.at[me]
@@ -96,8 +100,9 @@
         copy.wait_send()
     if shift:
         across.wait_send()
-        roles_across.wait_send()
-        roles_across.wait_recv()
+        for copy in roles_across:
+            copy.wait_send()
+            copy.wait_recv()
     else:
         own.wait()
 
@@ -109,15 +114,15 @@
     gathered = jax.ShapeDtypeStruct((n,) + block.shape, block.dtype)
     operands = (block,) if roles is None else (block, roles)
     return pl.pallas_call(
-        functools.partial(gather_kernel, n, groups, shift, pieces),
-        out_shape=gathered if roles is None else (gathered, jax.ShapeDtypeStruct(roles.shape, roles.dtype)),
+        functools.partial(gather_kernel, n, groups, shift, pieces, roles is not None),
+        out_shape=gathered if roles is None else (gathered, jax.ShapeDtypeStruct((2,) + roles.shape, roles.dtype)),
         in_specs=[vmem] * len(operands),
         out_specs=vmem if roles is None else (vmem, vmem),
         scratch_shapes=[
             pltpu.SemaphoreType.DMA((2, n // 2, pieces)),
             pltpu.SemaphoreType.DMA((2, n // 2, pieces)),
             pltpu.SemaphoreType.DMA,
-            pltpu.SemaphoreType.DMA((4,)),
+            pltpu.SemaphoreType.DMA((6,)),
         ],
         compiler_params=pltpu.CompilerParams(collective_id=collective_id, has_side_effects=True),
     )(*operands)
@@ -196,7 +201,9 @@
         return jnp.stack([node_up(tensor_here, child_envs[0][0], child_envs[1][0])])
 
     mid_up = lax.cond(is_mid, mid_work, lambda: zero_envs)
-    every_mid, next_roles = node_gather(jnp.stack([mid_up, mid_up]), 1, -1, role_map)
+    every_mid, near_roles = node_gather(jnp.stack([mid_up, mid_up]), 1, -1, role_map)
+    next_roles = near_roles[0]
+    prev_roles = near_roles[1]
     top_index = jnp.clip(my_role, 0, top_count - 1)
     mid_table = jnp.take(every_mid[:, 0], role_spot[top_count : top_count + mid_count], axis=0)
     next_spots = placements(next_roles[0])[top_count + top_count : top_count + mid_count]
@@ -210,7 +217,7 @@
     top_down = lax.cond(
         is_top, top_work, lambda: jnp.zeros((2, TERMS, bond_size, bond_size), jnp.bfloat16)
     )
-    every_top, prev_roles = node_gather(top_down, 2, 1, role_map)
+    every_top = node_gather(top_down, 2, 1)
     own_field = every_top[role_spot[jnp.clip(mid_index, 0, top_count - 1)], 0]
     other_field = every_top[placements(prev_roles[0])[jnp.clip(mid_index - top_count, 0, top_count - 1)], 1]
     mid_field = jnp.where(mid_index < top_count, own_field, other_field)

time: 173 us -> 173 us (level); the launches traced: 173 us -> 171 us
  Pallas kernels: 137 us -> 134 us
  matrix products: 16.3 us -> 18.2 us
    pallas_call x3, Pallas kernels: 137 us -> 134 us  [node_gather(): pl.pallas_call(functools.partial(gather_kernel, n, groups, shift, pieces,...]
    another operation x1, loops' own time: 2.49 us -> 0.2 us  [local(): mid_up = lax.cond(is_mid, mid_work, lambda: zero_envs)]
    dot_general x2 -> x5, matrix products: 16.3 us -> 18.2 us  [the longest x1 6.56 us: node_down(): jnp.einsum('xyq,xa->ayq', tensor_here, left_env, preferred_element_type=j...]
where the time goes in v10:
time: 173 us; the launch traced here: 171 us
  Pallas kernels  134 us (77%)
  matrix products  18.2 us (11%)
  between operations  7.4 us (4%)
  local copies, waits for them, and re-layouts  6.78 us (4%)
  other arithmetic  2.65 us (2%)
    pallas_call x3, Pallas kernels, node_gather(): pl.pallas_call(functools.partial(gather_kernel, n, groups, shift, pieces,...  134 us
    dot_general x1, matrix products, node_down(): jnp.einsum('xyq,xa->ayq', tensor_here, left_env, preferred_element_type=j...  6.56 us
    dot_general x1, matrix products, node_down(): jnp.einsum('xbq,abq->xa', right_part, weighted, preferred_element_type=jn...  4.94 us
    dot_general x1, matrix products, node_down(): jnp.einsum('ayq,abq->yb', left_part, weighted, preferred_element_type=jnp...  4.13 us

profile of v10, /device:TPU:24, one launch (start us, length us, event | category | flops | bytes accessed | tf_op | source)
XLA Modules:
  0.0 170.6 jit_solution(4196807983509918444)
XLA Ops:
  0.0 1.2 constant_dynamic-slice_fusion.2
  1.9 0.0 copy-start.5
  1.9 0.0 copy-start.4
  1.9 50.7 %shard_map.57 = bf16[16,1,128,128]{3,2,1,0:T(8,128)(2,1)} custom-call(bf16[1,128,128]{2,1,0:T(8,128)(2,1)S(1)} %get-tuple-element.202.refs_0_), custom_call_target="tpu_custom_call" | custom-call | tf_op jit(solution)/shard_map/pallas_call | solution.py:116
  52.6 0.0 copy-done.5
  52.6 0.1 select_reduce_fusion.2
  52.7 0.1 compare_select_fusion.2
  52.8 1.6 gather_fusion.1
  56.4 0.0 copy-done.4
  56.4 0.0 copy-start.3
  56.5 0.2 conditional.4
  56.7 0.1 copy.17
  56.8 0.6 pad_maximum_fusion.1.refs_0_
  57.4 50.8 %shard_map.58 = (bf16[16,2,1,128,128]{4,3,2,1,0:T(8,128)(2,1)S(1)}, s32[2,1,16]{2,1,0:T(1,128)}) custom-call(bf16[2,1,128,128]{3,2,1,0:T(8,128)(2,1)} %pad_maximum_fusion.1.refs_0_, s32[1,16]{1,0:T(1,128)} %refs_1_.1), custom_call_target="tpu_custom_call" | custom-call | tf_op jit(solution)/shard_map/pallas_call | solution.py:116
  108.3 0.6 slice_bitcast_fusion.2
  108.9 0.1 select_reduce_fusion
  109.0 0.7 dynamic_slice.47
  111.7 0.1 compare_select_fusion.1
  111.9 0.6 gather_fusion.2
  113.1 0.0 copy-done.3
  113.1 20.9 %conditional.5 = (bf16[2,1,128,128]{3,2,1,0:T(8,128)(2,1)S(1)}) conditional(s32[]{:T(128)} %convert_element_type.77, () %tuple.41, (s32[]{:T(128)}, s32[4]{0:T(128)S(1)}, bf16[128,128,128]{2,1,0:T(8,128)(2,1)}, bf16[1,1,1,128,128]{4,3,2,1,0:T(8,128)(2,1)S(1)}, s32[16]{0:T(128)S(1)}, /*index=5*/bf16[16,2,1,128,128]{4,3,2,1,0:T(8,128)(2,1)S(1)}, ...), branch_computations={%region_6.8_spmd, %region_7.9_spmd} | conditional | flops 2686600192 | bytes 60985616 | solution.py:217
  114.0 0.1 compare_and_fusion.2
  114.1 0.6 dynamic-slice.3
  114.8 0.6 gather_fusion
  115.4 0.0 copy-start
  115.4 6.6 %fusion.58 = bf16[128,128,128]{2,0,1:T(8,128)(2,1)S(1)} fusion(bf16[128,128,128]{2,1,0:T(8,128)(2,1)} %get-tuple-element.168, bf16[8,1,128,128]{3,2,0,1:T(8,128)(2,1)S(1)} %bitcast.146, s32[]{:T(128)S(6)} %min.12, pred[1]{0:T(512)(128)(4,1)} %dynamic-slice.3), kind=kOutput, calls=%fused_computation.48 | convolution fusion | flops 536887296 | bytes 8421381 | tf_op jit(solution)/shard_map/cond/branch_1_fun/xyq,xa->ayq/dot_general | solution.py:150
  122.0 0.0 copy-done
  122.0 1.3 convolution_convert_fusion
  123.3 4.1 %fusion.73 = bf16[1,1,128,128]{3,2,1,0:T(8,128)(2,1)S(1)} fusion(bf16[128,128,128]{2,1,0:T(8,128)(2,1)S(1)} %convolution_convert_fusion, bf16[128,128,128]{2,0,1:T(8,128)(2,1)S(1)} %fusion.58), kind=kOutput, calls=%fused_computation.56 | convolution fusion | flops 536887296 | bytes 8421376 | tf_op jit(solution)/shard_map/cond/branch_1_fun/ayq,abq->yb/dot_general | solution.py:156
  127.4 0.1 select_bitcast_fusion.1
  127.5 1.3 fusion.82
  128.8 4.9 %fusion.74 = bf16[1,1,128,128]{3,2,1,0:T(8,128)(2,1)S(1)} fusion(bf16[128,128,128]{2,1,0:T(8,128)(2,1)S(1)} %convolution_convert_fusion, bf16[128,128,128]{2,0,1:T(8,128)(2,1)S(1)} %fusion.82), kind=kOutput, calls=%fused_computation.57 | convolution fusion | flops 536887296 | bytes 8421376 | tf_op jit(solution)/shard_map/cond/branch_1_fun/xbq,abq->xa/dot_general | solution.py:153
  134.0 32.6 %shard_map.59 = bf16[16,2,1,128,128]{4,3,2,1,0:T(8,128)(2,1)} custom-call(bf16[2,1,128,128]{3,2,1,0:T(8,128)(2,1)S(1)} %get-tuple-element.236.refs_0_), custom_call_target="tpu_custom_call" | custom-call | tf_op jit(solution)/shard_map/pallas_call | solution.py:116
  166.6 0.6 dynamic_slice.45
  169.2 1.4 fusion.90
  (12 shorter events, 0.2 us)
Async XLA Ops:
  1.9 50.7 %copy-start.5 = (s32[1,16]{1,0:T(1,128)S(1)}, s32[1,16]{1,0:T(1,128)}, u32[]{:S(2)}) copy-start(s32[1,16]{1,0:T(1,128)} %refs_1_.1) | copy-start | bytes 196
  1.9 54.5 %copy-start.4 = (s32[1,16]{1,0:T(1,128)S(1)}, s32[1,16]{1,0:T(1,128)}, u32[]{:S(2)}) copy-start(s32[1,16]{1,0:T(1,128)} %param.17) | copy-start | bytes 196
  56.4 56.6 %copy-start.3 = (bf16[1,1,1,128,128]{4,3,2,1,0:T(8,128)(2,1)S(1)}, bf16[1,1,1,128,128]{4,3,2,1,0:T(8,128)(2,1)}, u32[]{:S(2)}) copy-start(bf16[1,1,1,128,128]{4,3,2,1,0:T(8,128)(2,1)} %param.15) | copy-start | bytes 98308
  115.4 6.6 %copy-start = (bf16[128,128,128]{2,1,0:T(8,128)(2,1)S(1)}, bf16[128,128,128]{2,1,0:T(8,128)(2,1)}, u32[]{:S(2)}) copy-start(bf16[128,128,128]{2,1,0:T(8,128)(2,1)} %get-tuple-element.168) | copy-start | bytes 12582916 | tf_op jit(solution)/shard_map/cond

commit v11 on v10

--- a/solution.py
+++ b/solution.py
@@ -165,6 +165,11 @@
     return jnp.sum(jnp.where(group_roles[None, :] == spots[:, None], spots[None, :], 0), axis=1)
 
 
+def pick(table, hit):
+    hit = hit.reshape(hit.shape + (1,) * (table.ndim - 1))
+    return jnp.sum(jnp.where(hit, table.astype(jnp.float32), 0.0), axis=0).astype(table.dtype)
+
+
 def local(node_tensor, outer_env, upper_env, role_map, child_slots):
     tensor_here = node_tensor[0, 0]
     outer_envs = outer_env[0, 0]
@@ -205,21 +210,19 @@
     next_roles = near_roles[0]
     prev_roles = near_roles[1]
     top_index = jnp.clip(my_role, 0, top_count - 1)
-    mid_table = jnp.take(every_mid[:, 0], role_spot[top_count : top_count + mid_count], axis=0)
-    next_spots = placements(next_roles[0])[top_count + top_count : top_count + mid_count]
-    right_envs = jnp.take(every_mid[:, 1], next_spots, axis=0)[top_index]
+    left_envs = pick(every_mid[:, 0], group_roles == top_count + top_index)
+    right_envs = pick(every_mid[:, 1], next_roles[0] == top_count + top_count + top_index)
 
     def top_work():
-        left_env = mid_table[top_index]
-        results = [node_down(tensor_here, left_env[0], right_envs[0], upper_envs[0])]
+        results = [node_down(tensor_here, left_envs[t], right_envs[t], upper_envs[t]) for t in range(TERMS)]
         return jnp.stack([jnp.stack([r[0] for r in results]), jnp.stack([r[1] for r in results])])
 
     top_down = lax.cond(
         is_top, top_work, lambda: jnp.zeros((2, TERMS, bond_size, bond_size), jnp.bfloat16)
     )
     every_top = node_gather(top_down, 2, 1)
-    own_field = every_top[role_spot[jnp.clip(mid_index, 0, top_count - 1)], 0]
-    other_field = every_top[placements(prev_roles[0])[jnp.clip(mid_index - top_count, 0, top_count - 1)], 1]
+    own_field = pick(every_top[:, 0], group_roles == jnp.clip(mid_index, 0, top_count - 1))
+    other_field = pick(every_top[:, 1], prev_roles[0] == jnp.clip(mid_index - top_count, 0, top_count - 1))
     mid_field = jnp.where(mid_index < top_count, own_field, other_field)
     result = jnp.where(is_mid, mid_field, jnp.where(is_leaf, leaf_up, zero_envs))
     return result[None, None]

time: 173 us -> 161 us (0.931)
  local copies, waits for them, and re-layouts: 6.78 us -> 2.72 us
  between operations: 7.4 us -> 3.42 us
  Pallas kernels: 134 us -> 131 us
  matrix products: 18.2 us -> 16.3 us
    pallas_call x3, Pallas kernels: 134 us -> 131 us  [node_gather(): pl.pallas_call(functools.partial(gather_kernel, n, groups, shift, pieces,...]
    another operation x1, loops' own time: 0.2 us -> 2.88 us  [local(): mid_up = lax.cond(is_mid, mid_work, lambda: zero_envs)]
    dot_general x5 -> x2, matrix products: 18.2 us -> 16.3 us  [the longest x1 8.79 us: node_up(): jnp.einsum('xyq,xyp->qp', tensor_here, second, preferred_element_type=jnp...]
where the time goes in v11:
time: 161 us; the launch traced here: 160 us
  Pallas kernels  131 us (81%)
  matrix products  16.3 us (10%)
  between operations  3.42 us (2%)
  loops' own time  3.18 us (2%)
  other arithmetic  3.04 us (2%)
  local copies, waits for them, and re-layouts  2.72 us (2%)
    pallas_call x3, Pallas kernels, node_gather(): pl.pallas_call(functools.partial(gather_kernel, n, groups, shift, pieces,...  131 us
    dot_general x1, matrix products, node_up(): jnp.einsum('xyq,xyp->qp', tensor_here, second, preferred_element_type=jnp...  8.79 us
    dot_general x1, matrix products, node_up(): jnp.einsum('xa,abp->xbp', left_env, tensor_here, preferred_element_type=j...  7.54 us

profile of v11, /device:TPU:24, one launch (start us, length us, event | category | flops | bytes accessed | tf_op | source)
XLA Modules:
  0.0 159.6 jit_solution(4511403625949305132)
XLA Ops:
  0.0 1.2 constant_dynamic-slice_fusion.2
  1.9 0.0 copy-start.4
  1.9 0.0 copy-start.5
  1.9 48.8 %shard_map.57 = bf16[16,1,128,128]{3,2,1,0:T(8,128)(2,1)S(1)} custom-call(bf16[1,128,128]{2,1,0:T(8,128)(2,1)S(1)} %get-tuple-element.231.refs_0_), custom_call_target="tpu_custom_call" | custom-call | tf_op jit(solution)/shard_map/pallas_call | solution.py:116
  52.8 0.0 copy-done.4
  52.8 0.0 copy-done.5
  52.8 0.0 copy-start.3
  52.8 20.7 %conditional.4 = (bf16[1,128,128]{1,2,0:T(8,128)(2,1)S(1)}) conditional(s32[]{:T(128)} %convert_element_type.176, () %tuple.41, (s32[]{:T(128)}, s32[1,16]{1,0:T(1,128)S(1)}, s32[16]{0:T(128)S(1)}, s32[16,16]{1,0:T(8,128)S(1)}, s32[16,16]{1,0:T(8,128)S(1)}, /*index=5*/bf16[16,1,128,128]{3,2,1,0:T(8,128)(2,1)S(1)}, bf16[2,1,128,128]{3,2,0,1:T(8,128)(2,1)}, ...), branch_computations={%region_2.3_spmd, %region_3.5_spmd} | conditional | flops 1612826368 | bytes 17735056 | solution.py:208
  53.0 0.7 constant_dynamic-slice_fusion
  54.9 0.1 select_reduce_fusion
  55.1 0.1 compare_and_fusion
  55.2 0.6 gather_fusion
  55.7 0.1 bitcast_select_fusion
  55.8 0.0 copy-start.2
  55.8 7.5 %fusion.51 = bf16[128,128,128]{2,0,1:T(8,128)(2,1)} fusion(bf16[128,128,128]{2,1,0:T(8,128)(2,1)} %get-tuple-element.213, bf16[2,1,128,128]{3,2,0,1:T(8,128)(2,1)} %get-tuple-element.212, bf16[4,1,128,128]{3,2,0,1:T(8,128)(2,1)S(1)} %bitcast_select_fusion, s32[]{:T(128)} %bitcast.12, pred[]{:T(512)} %bitcast.9), kind=kOutput, calls=%fused_computation.47 | convolution fusion | flops 536887296 | bytes 8455168 | tf_op jit(solution)/shard_map/cond/branch_1_fun/xa,abp->xbp/dot_general | solution.py:132
  64.7 0.0 copy-done.2
  64.7 8.8 %fusion.60 = bf16[1,128,128]{1,2,0:T(8,128)(2,1)S(1)} fusion(bf16[128,128,128]{2,1,0:T(8,128)(2,1)} %get-tuple-element.213, bf16[128,128,128]{2,0,1:T(8,128)(2,1)} %fusion.51, bf16[2,1,128,128]{3,2,0,1:T(8,128)(2,1)S(1)} %copy-done.2, bf16[4,1,128,128]{3,2,0,1:T(8,128)(2,1)S(1)} %bitcast_select_fusion, s32[]{:T(128)} %bitcast.16, pred[]{:T(512)} %bitcast.15), kind=kOutput, calls=%fused_computation.52 | convolution fusion | flops 1075871744 | bytes 8486917 | tf_op jit(solution)/shard_map/cond/branch_1_fun/xyq,xyp->qp/dot_general | solution.py:138
  73.5 0.1 copy.13
  73.7 0.6 pad_maximum_fusion.1.refs_0_
  74.3 30.3 %shard_map.58 = (bf16[16,2,1,128,128]{4,3,2,1,0:T(8,128)(2,1)S(1)}, s32[2,1,16]{2,1,0:T(1,128)S(1)}) custom-call(bf16[2,1,128,128]{3,2,1,0:T(8,128)(2,1)} %pad_maximum_fusion.1.refs_0_, s32[1,16]{1,0:T(1,128)S(1)} %copy-done.4), custom_call_target="tpu_custom_call" | custom-call | tf_op jit(solution)/shard_map/pallas_call | solution.py:116
  104.6 0.1 broadcast_in_dim.76
  105.4 0.0 copy-done.3
  105.4 0.3 conditional.5
  105.7 51.8 %shard_map.59 = bf16[16,2,1,128,128]{4,3,2,1,0:T(8,128)(2,1)} custom-call(bf16[2,1,128,128]{3,2,1,0:T(8,128)(2,1)S(1)} %get-tuple-element.243.refs_0_), custom_call_target="tpu_custom_call" | custom-call | tf_op jit(solution)/shard_map/pallas_call | solution.py:116
  157.5 1.5 fusion.82
  159.0 0.6 fusion.83
  (8 shorter events, 0.1 us)
Async XLA Ops:
  1.9 50.9 %copy-start.4 = (s32[1,16]{1,0:T(1,128)S(1)}, s32[1,16]{1,0:T(1,128)}, u32[]{:S(2)}) copy-start(s32[1,16]{1,0:T(1,128)} %refs_1_.1) | copy-start | bytes 196
  1.9 50.9 %copy-start.5 = (s32[1,16]{1,0:T(1,128)S(1)}, s32[1,16]{1,0:T(1,128)}, u32[]{:S(2)}) copy-start(s32[1,16]{1,0:T(1,128)} %param.15) | copy-start | bytes 196
  52.8 52.6 %copy-start.3 = (bf16[1,1,1,128,128]{4,3,2,1,0:T(8,128)(2,1)S(1)}, bf16[1,1,1,128,128]{4,3,2,1,0:T(8,128)(2,1)}, u32[]{:S(2)}) copy-start(bf16[1,1,1,128,128]{4,3,2,1,0:T(8,128)(2,1)} %param.13) | copy-start | bytes 98308
  55.8 8.9 %copy-start.2 = (bf16[2,1,128,128]{3,2,0,1:T(8,128)(2,1)S(1)}, bf16[2,1,128,128]{3,2,0,1:T(8,128)(2,1)}, u32[]{:S(2)}) copy-start(bf16[2,1,128,128]{3,2,0,1:T(8,128)(2,1)} %get-tuple-element.212) | copy-start | bytes 196612 | tf_op jit(solution)/shard_map/cond

commit v12 on v11

--- a/solution.py
+++ b/solution.py
@@ -107,7 +107,7 @@
         own.wait()
 
 
-def node_gather(block, collective_id, shift=0, roles=None, pieces=2):
+def node_gather(block, collective_id, shift=0, roles=None, pieces=4):
     n = lax.axis_size("node")
     groups = lax.axis_size("sub")
     vmem = pl.BlockSpec(memory_space=pltpu.VMEM)
@@ -192,16 +192,14 @@
         return jnp.stack([node_up(tensor_here, outer_envs[0, 0], outer_envs[1, 0])])
 
     leaf_up = lax.cond(is_leaf, leaf_work, lambda: zero_envs)
-    leaf_spots = role_spot[top_count + mid_count :]
     every_leaf = node_gather(leaf_up, 0)
-    leaf_table = jnp.take(every_leaf, leaf_spots, axis=0)
     mid_index = jnp.clip(my_role - top_count, 0, mid_count - 1)
 
     def mid_work():
         child_envs = []
         for branch in range(2):
             slot_link = child_links[2 * mid_index + branch]
-            leaf_pick = leaf_table[jnp.maximum(slot_link, 0)]
+            leaf_pick = pick(every_leaf, group_roles == top_count + mid_count + jnp.maximum(slot_link, 0))
             child_envs.append(jnp.where(slot_link >= 0, leaf_pick, outer_envs[branch]))
         return jnp.stack([node_up(tensor_here, child_envs[0][0], child_envs[1][0])])
 

time: 161 us -> 159 us (0.988)
  no operation moved by 1% of the time
where the time goes in v12:
time: 159 us; the launch traced here: 158 us
  Pallas kernels  130 us (82%)
  matrix products  16.3 us (10%)
  between operations  3.4 us (2%)
  other arithmetic  3.03 us (2%)
  loops' own time  2.81 us (2%)
  local copies, waits for them, and re-layouts  2.07 us (1%)
    pallas_call x3, Pallas kernels, node_gather(): pl.pallas_call(functools.partial(gather_kernel, n, groups, shift, pieces,...  130 us
    dot_general x1, matrix products, node_up(): jnp.einsum('xyq,xyp->qp', tensor_here, second, preferred_element_type=jnp...  8.78 us
    dot_general x1, matrix products, node_up(): jnp.einsum('xa,abp->xbp', left_env, tensor_here, preferred_element_type=j...  7.54 us

profile of v12, /device:TPU:24, one launch (start us, length us, event | category | flops | bytes accessed | tf_op | source)
XLA Modules:
  0.0 157.9 jit_solution(8873135535353494730)
XLA Ops:
  0.0 1.2 constant_dynamic-slice_fusion.2
  1.9 0.0 copy-start.4
  1.9 0.0 copy-start.5
  1.9 49.3 %shard_map.57 = bf16[16,1,128,128]{3,2,1,0:T(8,128)(2,1)S(1)} custom-call(bf16[1,128,128]{2,1,0:T(8,128)(2,1)S(1)} %get-tuple-element.131.refs_0_), custom_call_target="tpu_custom_call" | custom-call | tf_op jit(solution)/shard_map/pallas_call | solution.py:116
  53.2 0.0 copy-done.4
  53.2 0.0 copy-done.5
  53.2 0.0 copy-start.3
  53.2 19.7 %conditional.4 = (bf16[1,128,128]{1,2,0:T(8,128)(2,1)S(1)}) conditional(s32[]{:T(128)} %convert_element_type.183, () %tuple.27, (s32[]{:T(128)}, s32[1,16]{1,0:T(1,128)S(1)}, s32[1,16]{1,0:T(1,128)S(1)}, bf16[16,1,128,128]{3,2,1,0:T(8,128)(2,1)S(1)}, bf16[2,1,128,128]{3,2,1,0:T(8,128)(2,1)}, /*index=5*/bf16[128,128,128]{2,1,0:T(8,128)(2,1)}) %tuple.53), branch_computations={%region_2.3_spmd, %region_3.6_spmd} | conditional | flops 1614036992 | bytes 17793892 | solution.py:206
  53.4 0.6 constant_dynamic-slice_fusion.1
  55.1 0.3 fusion.37
  56.0 0.0 copy-start.2
  56.0 7.5 %fusion.24 = bf16[128,128,128]{2,0,1:T(8,128)(2,1)} fusion(bf16[128,128,128]{2,1,0:T(8,128)(2,1)} %get-tuple-element.115, bf16[2,1,128,128]{3,2,1,0:T(8,128)(2,1)} %get-tuple-element.114, bf16[128,128]{1,0:T(8,128)(2,1)S(1)} %get-tuple-element.133, pred[]{:T(512)} %bitcast.8), kind=kOutput, calls=%fused_computation.18 | convolution fusion | flops 536887296 | bytes 8454656 | tf_op jit(solution)/shard_map/cond/branch_1_fun/xa,abp->xbp/dot_general | solution.py:132
  64.1 0.0 copy-done.2
  64.1 8.8 %fusion.33 = bf16[1,128,128]{1,2,0:T(8,128)(2,1)S(1)} fusion(bf16[128,128,128]{2,1,0:T(8,128)(2,1)} %get-tuple-element.115, bf16[128,128,128]{2,0,1:T(8,128)(2,1)} %fusion.24, bf16[2,1,128,128]{3,2,1,0:T(8,128)(2,1)S(1)} %copy-done.2, bf16[128,128]{1,0:T(8,128)(2,1)S(1)} %get-tuple-element.132, pred[]{:T(512)} %bitcast.13), kind=kOutput, calls=%fused_computation.25 | convolution fusion | flops 1075871744 | bytes 8486913 | tf_op jit(solution)/shard_map/cond/branch_1_fun/xyq,xyp->qp/dot_general | solution.py:138
  72.9 0.1 copy.12
  73.0 0.6 pad_maximum_fusion.1.refs_0_
  73.6 30.5 %shard_map.58 = (bf16[16,2,1,128,128]{4,3,2,1,0:T(8,128)(2,1)S(1)}, s32[2,1,16]{2,1,0:T(1,128)S(1)}) custom-call(bf16[2,1,128,128]{3,2,1,0:T(8,128)(2,1)} %pad_maximum_fusion.1.refs_0_, s32[1,16]{1,0:T(1,128)S(1)} %copy-done.4), custom_call_target="tpu_custom_call" | custom-call | tf_op jit(solution)/shard_map/pallas_call | solution.py:116
  104.1 0.1 broadcast_in_dim.57
  104.9 0.0 copy-done.3
  104.9 0.3 conditional.5
  105.2 50.5 %shard_map.59 = bf16[16,2,1,128,128]{4,3,2,1,0:T(8,128)(2,1)} custom-call(bf16[2,1,128,128]{3,2,1,0:T(8,128)(2,1)S(1)} %get-tuple-element.145.refs_0_), custom_call_target="tpu_custom_call" | custom-call | tf_op jit(solution)/shard_map/pallas_call | solution.py:116
  155.7 1.5 fusion.84
  157.2 0.6 fusion.85
  (6 shorter events, 0.1 us)
Async XLA Ops:
  1.9 51.3 %copy-start.4 = (s32[1,16]{1,0:T(1,128)S(1)}, s32[1,16]{1,0:T(1,128)}, u32[]{:S(2)}) copy-start(s32[1,16]{1,0:T(1,128)} %refs_1_.1) | copy-start | bytes 196
  1.9 51.3 %copy-start.5 = (s32[1,16]{1,0:T(1,128)S(1)}, s32[1,16]{1,0:T(1,128)}, u32[]{:S(2)}) copy-start(s32[1,16]{1,0:T(1,128)} %param.15) | copy-start | bytes 196
  53.2 51.7 %copy-start.3 = (bf16[1,1,1,128,128]{4,3,2,1,0:T(8,128)(2,1)S(1)}, bf16[1,1,1,128,128]{4,3,2,1,0:T(8,128)(2,1)}, u32[]{:S(2)}) copy-start(bf16[1,1,1,128,128]{4,3,2,1,0:T(8,128)(2,1)} %param.13) | copy-start | bytes 98308
  56.0 8.1 %copy-start.2 = (bf16[2,1,128,128]{3,2,1,0:T(8,128)(2,1)S(1)}, bf16[2,1,128,128]{3,2,1,0:T(8,128)(2,1)}, u32[]{:S(2)}) copy-start(bf16[2,1,128,128]{3,2,1,0:T(8,128)(2,1)} %get-tuple-element.114) | copy-start | bytes 196612 | tf_op jit(solution)/shard_map/cond

commit v13 on v12

--- a/solution.py
+++ b/solution.py
@@ -107,7 +107,7 @@
         own.wait()
 
 
-def node_gather(block, collective_id, shift=0, roles=None, pieces=4):
+def node_gather(block, collective_id, shift=0, roles=None, pieces=8):
     n = lax.axis_size("node")
     groups = lax.axis_size("sub")
     vmem = pl.BlockSpec(memory_space=pltpu.VMEM)

time: 159 us -> 161 us (1.013)
  Pallas kernels: 130 us -> 135 us
  loops' own time: 2.81 us -> 0.51 us
    pallas_call x3, Pallas kernels: 130 us -> 135 us  [node_gather(): pl.pallas_call(functools.partial(gather_kernel, n, groups, shift, pieces,...]
    another operation x1, loops' own time: 2.51 us -> 0.2 us  [local(): mid_up = lax.cond(is_mid, mid_work, lambda: zero_envs)]
where the time goes in v13:
time: 161 us; the launch traced here: 160 us
  Pallas kernels  135 us (84%)
  matrix products  16.5 us (10%)
  between operations  3.4 us (2%)
  other arithmetic  2.76 us (2%)
    pallas_call x3, Pallas kernels, node_gather(): pl.pallas_call(functools.partial(gather_kernel, n, groups, shift, pieces,...  135 us
    dot_general x1, matrix products, node_up(): jnp.einsum('xyq,xyp->qp', tensor_here, second, preferred_element_type=jnp...  8.89 us
    dot_general x1, matrix products, node_up(): jnp.einsum('xa,abp->xbp', left_env, tensor_here, preferred_element_type=j...  7.6 us

profile of v13, /device:TPU:24, one launch (start us, length us, event | category | flops | bytes accessed | tf_op | source)
XLA Modules:
  0.0 159.8 jit_solution(3950702508318636986)
XLA Ops:
  0.0 1.2 constant_dynamic-slice_fusion.2
  1.9 0.0 copy-start.4
  1.9 0.0 copy-start.5
  1.9 16.6 %conditional.3 = (bf16[1,128,128]{2,1,0:T(8,128)(2,1)S(1)}) conditional(s32[]{:T(128)} %convert_element_type.184, () %tuple.28, (bf16[2,1,128,128]{3,2,1,0:T(8,128)(2,1)}, bf16[128,128,128]{2,1,0:T(8,128)(2,1)}) %tuple.48), branch_computations={%region_0.0_spmd, %region_1.0_spmd} | conditional | flops 1612726272 | bytes 17203236 | solution.py:194
  1.9 0.0 copy-start.1
  1.9 7.6 %fusion.3 = bf16[128,128,128]{2,0,1:T(8,128)(2,1)} fusion(bf16[128,128,128]{2,1,0:T(8,128)(2,1)} %get-tuple-element.109, bf16[2,1,128,128]{3,2,1,0:T(8,128)(2,1)} %get-tuple-element.108), kind=kOutput, calls=%fused_computation.4 | convolution fusion | flops 536870912 | bytes 8421376 | tf_op jit(solution)/shard_map/cond/branch_1_fun/xa,abp->xbp/dot_general | solution.py:132
  9.5 0.0 copy-done.1
  9.5 8.9 %fusion.12 = bf16[1,128,128]{1,2,0:T(8,128)(2,1)S(1)} fusion(bf16[128,128,128]{2,1,0:T(8,128)(2,1)} %get-tuple-element.109, bf16[128,128,128]{2,0,1:T(8,128)(2,1)} %fusion.3, bf16[2,1,128,128]{3,2,1,0:T(8,128)(2,1)S(1)} %copy-done.1), kind=kOutput, calls=%fused_computation.9 | convolution fusion | flops 1075855360 | bytes 8454144 | tf_op jit(solution)/shard_map/cond/branch_1_fun/xyq,xyp->qp/dot_general | solution.py:138
  18.4 0.1 copy.23
  18.6 33.4 %shard_map.57 = bf16[16,1,128,128]{3,2,1,0:T(8,128)(2,1)S(1)} custom-call(bf16[1,128,128]{2,1,0:T(8,128)(2,1)S(1)} %get-tuple-element.131.refs_0_), custom_call_target="tpu_custom_call" | custom-call | tf_op jit(solution)/shard_map/pallas_call | solution.py:116
  53.9 0.0 copy-done.4
  53.9 0.0 copy-done.5
  53.9 0.0 copy-start.3
  54.0 0.2 conditional.4
  54.2 0.1 copy.12
  54.3 0.6 pad_maximum_fusion.1.refs_0_
  54.9 51.3 %shard_map.58 = (bf16[16,2,1,128,128]{4,3,2,1,0:T(8,128)(2,1)S(1)}, s32[2,1,16]{2,1,0:T(1,128)S(1)}) custom-call(bf16[2,1,128,128]{3,2,1,0:T(8,128)(2,1)} %pad_maximum_fusion.1.refs_0_, s32[1,16]{1,0:T(1,128)S(1)} %copy-done.4), custom_call_target="tpu_custom_call" | custom-call | tf_op jit(solution)/shard_map/pallas_call | solution.py:116
  106.2 0.1 broadcast_in_dim.57
  106.9 0.0 copy-done.3
  107.0 0.3 conditional.5
  107.3 50.4 %shard_map.59 = bf16[16,2,1,128,128]{4,3,2,1,0:T(8,128)(2,1)} custom-call(bf16[2,1,128,128]{3,2,1,0:T(8,128)(2,1)S(1)} %get-tuple-element.145.refs_0_), custom_call_target="tpu_custom_call" | custom-call | tf_op jit(solution)/shard_map/pallas_call | solution.py:116
  157.7 1.5 fusion.84
  159.2 0.6 fusion.85
  (4 shorter events, 0.0 us)
Async XLA Ops:
  1.9 52.0 %copy-start.4 = (s32[1,16]{1,0:T(1,128)S(1)}, s32[1,16]{1,0:T(1,128)}, u32[]{:S(2)}) copy-start(s32[1,16]{1,0:T(1,128)} %refs_1_.1) | copy-start | bytes 196
  1.9 52.0 %copy-start.5 = (s32[1,16]{1,0:T(1,128)S(1)}, s32[1,16]{1,0:T(1,128)}, u32[]{:S(2)}) copy-start(s32[1,16]{1,0:T(1,128)} %param.15) | copy-start | bytes 196
  1.9 7.6 %copy-start.1 = (bf16[2,1,128,128]{3,2,1,0:T(8,128)(2,1)S(1)}, bf16[2,1,128,128]{3,2,1,0:T(8,128)(2,1)}, u32[]{:S(2)}) copy-start(bf16[2,1,128,128]{3,2,1,0:T(8,128)(2,1)} %get-tuple-element.108) | copy-start | bytes 196612 | tf_op jit(solution)/shard_map/cond
  53.9 53.0 %copy-start.3 = (bf16[1,1,1,128,128]{4,3,2,1,0:T(8,128)(2,1)S(1)}, bf16[1,1,1,128,128]{4,3,2,1,0:T(8,128)(2,1)}, u32[]{:S(2)}) copy-start(bf16[1,1,1,128,128]{4,3,2,1,0:T(8,128)(2,1)} %param.13) | copy-start | bytes 98308

commit v14 on v12

--- a/solution.py
+++ b/solution.py
@@ -58,53 +58,63 @@
         ]
         for copy in roles_across:
             copy.start()
-        own.wait()
-        across.wait_recv()
-        first_src = out_ref.at[me]
     else:
         own = pltpu.make_async_copy(x_ref, out_ref.at[me], own_sem)
         own.start()
-        first_src = x_ref
     ways = ((0, 1, right, n // 2), (1, -1, left, n - 1 - n // 2))
     rows = x_ref.shape[-2] // pieces
-    lead = (slice(None),) * (len(x_ref.shape) - 2)
-
-    def hop(way, target, step, origin, piece):
-        part = lead + (pl.ds(piece * rows, rows), slice(None))
+    slots = (0, 1) if shift else (None,)
+    middle = (slice(None),) * (len(x_ref.shape) - 2 - (1 if shift else 0))
+    parts = [(slot, chunk) for slot in slots for chunk in range(pieces)]
+
+    def hop(way, target, step, origin, index):
+        slot, chunk = parts[index]
+        part = ((slot,) if shift else ()) + middle + (pl.ds(chunk * rows, rows), slice(None))
+        if step == 0:
+            source = out_ref.at[me] if slot == 1 else x_ref
+        else:
+            source = out_ref.at[origin]
         return pltpu.make_async_remote_copy(
-            src_ref=(first_src if step == 0 else out_ref.at[origin]).at[part],
+            src_ref=source.at[part],
             dst_ref=out_ref.at[origin].at[part],
-            send_sem=send_sem.at[way, step, piece],
-            recv_sem=recv_sem.at[way, step, piece],
+            send_sem=send_sem.at[way, step, index],
+            recv_sem=recv_sem.at[way, step, index],
             device_id=(group, target),
             device_id_type=MESH,
         )
 
     sent = []
-    for step in range(n // 2):
+    for slot in slots:
+        if slot == 1:
+            across.wait_recv()
+        for way, sign, target, steps in ways:
+            for index in range(len(parts)):
+                if parts[index][0] == slot:
+                    copy = hop(way, target, 0, me, index)
+                    copy.start()
+                    sent.append(copy)
+    for step in range(1, n // 2):
         for way, sign, target, steps in ways:
             if step >= steps:
                 continue
             origin = lax.rem(me - sign * step + 2 * n, n)
-            for piece in range(pieces):
-                if step > 0:
-                    hop(way, target, step - 1, origin, piece).wait_recv()
-                copy = hop(way, target, step, origin, piece)
+            for index in range(len(parts)):
+                hop(way, target, step - 1, origin, index).wait_recv()
+                copy = hop(way, target, step, origin, index)
                 copy.start()
                 sent.append(copy)
     for way, sign, target, steps in ways:
         origin = lax.rem(me - sign * steps + 2 * n, n)
-        for piece in range(pieces):
-            hop(way, target, steps - 1, origin, piece).wait_recv()
+        for index in range(len(parts)):
+            hop(way, target, steps - 1, origin, index).wait_recv()
     for copy in sent:
         copy.wait_send()
+    own.wait()
     if shift:
         across.wait_send()
         for copy in roles_across:
             copy.wait_send()
             copy.wait_recv()
-    else:
-        own.wait()
 
 
 def node_gather(block, collective_id, shift=0, roles=None, pieces=4):
@@ -119,8 +129,8 @@
         in_specs=[vmem] * len(operands),
         out_specs=vmem if roles is None else (vmem, vmem),
         scratch_shapes=[
-            pltpu.SemaphoreType.DMA((2, n // 2, pieces)),
-            pltpu.SemaphoreType.DMA((2, n // 2, pieces)),
+            pltpu.SemaphoreType.DMA((2, n // 2, pieces * (2 if shift else 1))),
+            pltpu.SemaphoreType.DMA((2, n // 2, pieces * (2 if shift else 1))),
             pltpu.SemaphoreType.DMA,
             pltpu.SemaphoreType.DMA((6,)),
         ],

time: 159 us -> 161 us (1.013)
  no operation moved by 1% of the time
where the time goes in v14:
time: 161 us; the launch traced here: 159 us
  Pallas kernels  131 us (81%)
  matrix products  16.3 us (10%)
  between operations  3.4 us (2%)
  other arithmetic  3.03 us (2%)
  loops' own time  2.81 us (2%)
  local copies, waits for them, and re-layouts  2.07 us (1%)
    pallas_call x3, Pallas kernels, node_gather(): pl.pallas_call(functools.partial(gather_kernel, n, groups, shift, pieces,...  131 us
    dot_general x1, matrix products, node_up(): jnp.einsum('xyq,xyp->qp', tensor_here, second, preferred_element_type=jnp...  8.78 us
    dot_general x1, matrix products, node_up(): jnp.einsum('xa,abp->xbp', left_env, tensor_here, preferred_element_type=j...  7.54 us

profile of v14, /device:TPU:24, one launch (start us, length us, event | category | flops | bytes accessed | tf_op | source)
XLA Modules:
  0.0 158.9 jit_solution(5459979604376907977)
XLA Ops:
  0.0 1.2 constant_dynamic-slice_fusion.2
  1.9 0.0 copy-start.4
  1.9 0.0 copy-start.5
  1.9 50.3 %shard_map.57 = bf16[16,1,128,128]{3,2,1,0:T(8,128)(2,1)S(1)} custom-call(bf16[1,128,128]{2,1,0:T(8,128)(2,1)S(1)} %get-tuple-element.131.refs_0_), custom_call_target="tpu_custom_call" | custom-call | tf_op jit(solution)/shard_map/pallas_call | solution.py:126
  54.2 0.0 copy-done.4
  54.2 0.0 copy-done.5
  54.2 0.0 copy-start.3
  54.2 19.7 %conditional.4 = (bf16[1,128,128]{1,2,0:T(8,128)(2,1)S(1)}) conditional(s32[]{:T(128)} %convert_element_type.183, () %tuple.27, (s32[]{:T(128)}, s32[1,16]{1,0:T(1,128)S(1)}, s32[1,16]{1,0:T(1,128)S(1)}, bf16[16,1,128,128]{3,2,1,0:T(8,128)(2,1)S(1)}, bf16[2,1,128,128]{3,2,1,0:T(8,128)(2,1)}, /*index=5*/bf16[128,128,128]{2,1,0:T(8,128)(2,1)}) %tuple.53), branch_computations={%region_2.3_spmd, %region_3.6_spmd} | conditional | flops 1614036992 | bytes 17793892 | solution.py:216
  54.4 0.6 constant_dynamic-slice_fusion.1
  56.2 0.3 fusion.37
  57.0 0.0 copy-start.2
  57.0 7.5 %fusion.24 = bf16[128,128,128]{2,0,1:T(8,128)(2,1)} fusion(bf16[128,128,128]{2,1,0:T(8,128)(2,1)} %get-tuple-element.115, bf16[2,1,128,128]{3,2,1,0:T(8,128)(2,1)} %get-tuple-element.114, bf16[128,128]{1,0:T(8,128)(2,1)S(1)} %get-tuple-element.133, pred[]{:T(512)} %bitcast.8), kind=kOutput, calls=%fused_computation.18 | convolution fusion | flops 536887296 | bytes 8454656 | tf_op jit(solution)/shard_map/cond/branch_1_fun/xa,abp->xbp/dot_general | solution.py:142
  65.1 0.0 copy-done.2
  65.1 8.8 %fusion.33 = bf16[1,128,128]{1,2,0:T(8,128)(2,1)S(1)} fusion(bf16[128,128,128]{2,1,0:T(8,128)(2,1)} %get-tuple-element.115, bf16[128,128,128]{2,0,1:T(8,128)(2,1)} %fusion.24, bf16[2,1,128,128]{3,2,1,0:T(8,128)(2,1)S(1)} %copy-done.2, bf16[128,128]{1,0:T(8,128)(2,1)S(1)} %get-tuple-element.132, pred[]{:T(512)} %bitcast.13), kind=kOutput, calls=%fused_computation.25 | convolution fusion | flops 1075871744 | bytes 8486913 | tf_op jit(solution)/shard_map/cond/branch_1_fun/xyq,xyp->qp/dot_general | solution.py:148
  73.9 0.1 copy.12
  74.1 0.6 pad_maximum_fusion.1.refs_0_
  74.7 29.9 %shard_map.58 = (bf16[16,2,1,128,128]{4,3,2,1,0:T(8,128)(2,1)S(1)}, s32[2,1,16]{2,1,0:T(1,128)S(1)}) custom-call(bf16[2,1,128,128]{3,2,1,0:T(8,128)(2,1)} %pad_maximum_fusion.1.refs_0_, s32[1,16]{1,0:T(1,128)S(1)} %copy-done.4), custom_call_target="tpu_custom_call" | custom-call | tf_op jit(solution)/shard_map/pallas_call | solution.py:126
  104.6 0.1 broadcast_in_dim.57
  105.4 0.0 copy-done.3
  105.4 0.3 conditional.5
  105.7 51.0 %shard_map.59 = bf16[16,2,1,128,128]{4,3,2,1,0:T(8,128)(2,1)} custom-call(bf16[2,1,128,128]{3,2,1,0:T(8,128)(2,1)S(1)} %get-tuple-element.145.refs_0_), custom_call_target="tpu_custom_call" | custom-call | tf_op jit(solution)/shard_map/pallas_call | solution.py:126
  156.8 1.5 fusion.84
  158.3 0.6 fusion.85
  (6 shorter events, 0.1 us)
Async XLA Ops:
  1.9 52.3 %copy-start.4 = (s32[1,16]{1,0:T(1,128)S(1)}, s32[1,16]{1,0:T(1,128)}, u32[]{:S(2)}) copy-start(s32[1,16]{1,0:T(1,128)} %refs_1_.1) | copy-start | bytes 196
  1.9 52.3 %copy-start.5 = (s32[1,16]{1,0:T(1,128)S(1)}, s32[1,16]{1,0:T(1,128)}, u32[]{:S(2)}) copy-start(s32[1,16]{1,0:T(1,128)} %param.15) | copy-start | bytes 196
  54.2 51.2 %copy-start.3 = (bf16[1,1,1,128,128]{4,3,2,1,0:T(8,128)(2,1)S(1)}, bf16[1,1,1,128,128]{4,3,2,1,0:T(8,128)(2,1)}, u32[]{:S(2)}) copy-start(bf16[1,1,1,128,128]{4,3,2,1,0:T(8,128)(2,1)} %param.13) | copy-start | bytes 98308
  57.0 8.1 %copy-start.2 = (bf16[2,1,128,128]{3,2,1,0:T(8,128)(2,1)S(1)}, bf16[2,1,128,128]{3,2,1,0:T(8,128)(2,1)}, u32[]{:S(2)}) copy-start(bf16[2,1,128,128]{3,2,1,0:T(8,128)(2,1)} %get-tuple-element.114) | copy-start | bytes 196612 | tf_op jit(solution)/shard_map/cond

commit v15 on v14

--- a/solution.py
+++ b/solution.py
@@ -214,7 +214,7 @@
         return jnp.stack([node_up(tensor_here, child_envs[0][0], child_envs[1][0])])
 
     mid_up = lax.cond(is_mid, mid_work, lambda: zero_envs)
-    every_mid, near_roles = node_gather(jnp.stack([mid_up, mid_up]), 1, -1, role_map)
+    every_mid, near_roles = node_gather(jnp.stack([mid_up, mid_up]), 1, -1, role_map, pieces=2)
     next_roles = near_roles[0]
     prev_roles = near_roles[1]
     top_index = jnp.clip(my_role, 0, top_count - 1)
@@ -228,7 +228,7 @@
     top_down = lax.cond(
         is_top, top_work, lambda: jnp.zeros((2, TERMS, bond_size, bond_size), jnp.bfloat16)
     )
-    every_top = node_gather(top_down, 2, 1)
+    every_top = node_gather(top_down, 2, 1, pieces=2)
     own_field = pick(every_top[:, 0], group_roles == jnp.clip(mid_index, 0, top_count - 1))
     other_field = pick(every_top[:, 1], prev_roles[0] == jnp.clip(mid_index - top_count, 0, top_count - 1))
     mid_field = jnp.where(mid_index < top_count, own_field, other_field)

time: 161 us -> 158 us (0.981)
  loops' own time: 2.81 us -> 0.51 us
  Pallas kernels: 131 us -> 133 us
    another operation x1, loops' own time: 2.51 us -> 0.2 us  [local(): mid_up = lax.cond(is_mid, mid_work, lambda: zero_envs)]
where the time goes in v15:
time: 158 us; the launch traced here: 157 us
  Pallas kernels  133 us (84%)
  matrix products  16.5 us (10%)
  between operations  3.4 us (2%)
  other arithmetic  2.76 us (2%)
  local copies, waits for them, and re-layouts  1.6 us (1%)
    pallas_call x3, Pallas kernels, node_gather(): pl.pallas_call(functools.partial(gather_kernel, n, groups, shift, pieces,...  133 us
    dot_general x1, matrix products, node_up(): jnp.einsum('xyq,xyp->qp', tensor_here, second, preferred_element_type=jnp...  8.89 us
    dot_general x1, matrix products, node_up(): jnp.einsum('xa,abp->xbp', left_env, tensor_here, preferred_element_type=j...  7.6 us

profile of v15, /device:TPU:24, one launch (start us, length us, event | category | flops | bytes accessed | tf_op | source)
XLA Modules:
  0.0 157.4 jit_solution(6639991685446745639)
XLA Ops:
  0.0 1.2 constant_dynamic-slice_fusion.2
  1.9 0.0 copy-start.4
  1.9 0.0 copy-start.5
  1.9 16.6 %conditional.3 = (bf16[1,128,128]{2,1,0:T(8,128)(2,1)S(1)}) conditional(s32[]{:T(128)} %convert_element_type.184, () %tuple.28, (bf16[2,1,128,128]{3,2,1,0:T(8,128)(2,1)}, bf16[128,128,128]{2,1,0:T(8,128)(2,1)}) %tuple.48), branch_computations={%region_0.0_spmd, %region_1.0_spmd} | conditional | flops 1612726272 | bytes 17203236 | solution.py:204
  1.9 0.0 copy-start.1
  1.9 7.6 %fusion.3 = bf16[128,128,128]{2,0,1:T(8,128)(2,1)} fusion(bf16[128,128,128]{2,1,0:T(8,128)(2,1)} %get-tuple-element.109, bf16[2,1,128,128]{3,2,1,0:T(8,128)(2,1)} %get-tuple-element.108), kind=kOutput, calls=%fused_computation.4 | convolution fusion | flops 536870912 | bytes 8421376 | tf_op jit(solution)/shard_map/cond/branch_1_fun/xa,abp->xbp/dot_general | solution.py:142
  9.5 0.0 copy-done.1
  9.5 8.9 %fusion.12 = bf16[1,128,128]{1,2,0:T(8,128)(2,1)S(1)} fusion(bf16[128,128,128]{2,1,0:T(8,128)(2,1)} %get-tuple-element.109, bf16[128,128,128]{2,0,1:T(8,128)(2,1)} %fusion.3, bf16[2,1,128,128]{3,2,1,0:T(8,128)(2,1)S(1)} %copy-done.1), kind=kOutput, calls=%fused_computation.9 | convolution fusion | flops 1075855360 | bytes 8454144 | tf_op jit(solution)/shard_map/cond/branch_1_fun/xyq,xyp->qp/dot_general | solution.py:148
  18.4 0.1 copy.23
  18.6 31.3 %shard_map.57 = bf16[16,1,128,128]{3,2,1,0:T(8,128)(2,1)S(1)} custom-call(bf16[1,128,128]{2,1,0:T(8,128)(2,1)S(1)} %get-tuple-element.131.refs_0_), custom_call_target="tpu_custom_call" | custom-call | tf_op jit(solution)/shard_map/pallas_call | solution.py:126
  51.9 0.0 copy-done.4
  51.9 0.0 copy-done.5
  51.9 0.0 copy-start.3
  51.9 0.2 conditional.4
  52.1 0.1 copy.12
  52.2 0.6 pad_maximum_fusion.1.refs_0_
  52.9 51.4 %shard_map.58 = (bf16[16,2,1,128,128]{4,3,2,1,0:T(8,128)(2,1)S(1)}, s32[2,1,16]{2,1,0:T(1,128)S(1)}) custom-call(bf16[2,1,128,128]{3,2,1,0:T(8,128)(2,1)} %pad_maximum_fusion.1.refs_0_, s32[1,16]{1,0:T(1,128)S(1)} %copy-done.4), custom_call_target="tpu_custom_call" | custom-call | tf_op jit(solution)/shard_map/pallas_call | solution.py:126
  104.3 0.1 broadcast_in_dim.57
  105.1 0.0 copy-done.3
  105.1 0.3 conditional.5
  105.4 49.9 %shard_map.59 = bf16[16,2,1,128,128]{4,3,2,1,0:T(8,128)(2,1)} custom-call(bf16[2,1,128,128]{3,2,1,0:T(8,128)(2,1)S(1)} %get-tuple-element.145.refs_0_), custom_call_target="tpu_custom_call" | custom-call | tf_op jit(solution)/shard_map/pallas_call | solution.py:126
  155.3 1.5 fusion.84
  156.8 0.6 fusion.85
  (4 shorter events, 0.0 us)
Async XLA Ops:
  1.9 50.0 %copy-start.4 = (s32[1,16]{1,0:T(1,128)S(1)}, s32[1,16]{1,0:T(1,128)}, u32[]{:S(2)}) copy-start(s32[1,16]{1,0:T(1,128)} %refs_1_.1) | copy-start | bytes 196
  1.9 50.0 %copy-start.5 = (s32[1,16]{1,0:T(1,128)S(1)}, s32[1,16]{1,0:T(1,128)}, u32[]{:S(2)}) copy-start(s32[1,16]{1,0:T(1,128)} %param.15) | copy-start | bytes 196
  1.9 7.6 %copy-start.1 = (bf16[2,1,128,128]{3,2,1,0:T(8,128)(2,1)S(1)}, bf16[2,1,128,128]{3,2,1,0:T(8,128)(2,1)}, u32[]{:S(2)}) copy-start(bf16[2,1,128,128]{3,2,1,0:T(8,128)(2,1)} %get-tuple-element.108) | copy-start | bytes 196612 | tf_op jit(solution)/shard_map/cond
  51.9 53.2 %copy-start.3 = (bf16[1,1,1,128,128]{4,3,2,1,0:T(8,128)(2,1)S(1)}, bf16[1,1,1,128,128]{4,3,2,1,0:T(8,128)(2,1)}, u32[]{:S(2)}) copy-start(bf16[1,1,1,128,128]{4,3,2,1,0:T(8,128)(2,1)} %param.13) | copy-start | bytes 98308

commit v16 on v15

--- a/solution.py
+++ b/solution.py
@@ -202,7 +202,7 @@
         return jnp.stack([node_up(tensor_here, outer_envs[0, 0], outer_envs[1, 0])])
 
     leaf_up = lax.cond(is_leaf, leaf_work, lambda: zero_envs)
-    every_leaf = node_gather(leaf_up, 0)
+    every_leaf = node_gather(leaf_up, 0, pieces=2)
     mid_index = jnp.clip(my_role - top_count, 0, mid_count - 1)
 
     def mid_work():

time: 158 us -> 158 us (level)
  no operation moved by 1% of the time
where the time goes in v16:
time: 158 us
  Pallas kernels  133 us (84%)
  matrix products  16.5 us (10%)
  between operations  3.4 us (2%)
  other arithmetic  2.76 us (2%)
  local copies, waits for them, and re-layouts  1.6 us (1%)
    pallas_call x3, Pallas kernels, node_gather(): pl.pallas_call(functools.partial(gather_kernel, n, groups, shift, pieces,...  133 us
    dot_general x1, matrix products, node_up(): jnp.einsum('xyq,xyp->qp', tensor_here, second, preferred_element_type=jnp...  8.89 us
    dot_general x1, matrix products, node_up(): jnp.einsum('xa,abp->xbp', left_env, tensor_here, preferred_element_type=j...  7.6 us

profile of v16, /device:TPU:24, one launch (start us, length us, event | category | flops | bytes accessed | tf_op | source)
XLA Modules:
  0.0 157.9 jit_solution(9881136240358729920)
XLA Ops:
  0.0 1.2 constant_dynamic-slice_fusion.2
  1.9 0.0 copy-start.4
  1.9 0.0 copy-start.5
  1.9 16.6 %conditional.3 = (bf16[1,128,128]{2,1,0:T(8,128)(2,1)S(1)}) conditional(s32[]{:T(128)} %convert_element_type.184, () %tuple.28, (bf16[2,1,128,128]{3,2,1,0:T(8,128)(2,1)}, bf16[128,128,128]{2,1,0:T(8,128)(2,1)}) %tuple.48), branch_computations={%region_0.0_spmd, %region_1.0_spmd} | conditional | flops 1612726272 | bytes 17203236 | solution.py:204
  1.9 0.0 copy-start.1
  1.9 7.6 %fusion.3 = bf16[128,128,128]{2,0,1:T(8,128)(2,1)} fusion(bf16[128,128,128]{2,1,0:T(8,128)(2,1)} %get-tuple-element.109, bf16[2,1,128,128]{3,2,1,0:T(8,128)(2,1)} %get-tuple-element.108), kind=kOutput, calls=%fused_computation.4 | convolution fusion | flops 536870912 | bytes 8421376 | tf_op jit(solution)/shard_map/cond/branch_1_fun/xa,abp->xbp/dot_general | solution.py:142
  9.5 0.0 copy-done.1
  9.5 8.9 %fusion.12 = bf16[1,128,128]{1,2,0:T(8,128)(2,1)S(1)} fusion(bf16[128,128,128]{2,1,0:T(8,128)(2,1)} %get-tuple-element.109, bf16[128,128,128]{2,0,1:T(8,128)(2,1)} %fusion.3, bf16[2,1,128,128]{3,2,1,0:T(8,128)(2,1)S(1)} %copy-done.1), kind=kOutput, calls=%fused_computation.9 | convolution fusion | flops 1075855360 | bytes 8454144 | tf_op jit(solution)/shard_map/cond/branch_1_fun/xyq,xyp->qp/dot_general | solution.py:148
  18.4 0.1 copy.23
  18.6 32.4 %shard_map.57 = bf16[16,1,128,128]{3,2,1,0:T(8,128)(2,1)S(1)} custom-call(bf16[1,128,128]{2,1,0:T(8,128)(2,1)S(1)} %get-tuple-element.131.refs_0_), custom_call_target="tpu_custom_call" | custom-call | tf_op jit(solution)/shard_map/pallas_call | solution.py:126
  53.0 0.0 copy-done.4
  53.0 0.0 copy-done.5
  53.0 0.0 copy-start.3
  53.0 0.2 conditional.4
  53.2 0.1 copy.12
  53.3 0.6 pad_maximum_fusion.1.refs_0_
  53.9 50.9 %shard_map.58 = (bf16[16,2,1,128,128]{4,3,2,1,0:T(8,128)(2,1)S(1)}, s32[2,1,16]{2,1,0:T(1,128)S(1)}) custom-call(bf16[2,1,128,128]{3,2,1,0:T(8,128)(2,1)} %pad_maximum_fusion.1.refs_0_, s32[1,16]{1,0:T(1,128)S(1)} %copy-done.4), custom_call_target="tpu_custom_call" | custom-call | tf_op jit(solution)/shard_map/pallas_call | solution.py:126
  104.9 0.1 broadcast_in_dim.57
  105.7 0.0 copy-done.3
  105.7 0.3 conditional.5
  106.0 49.8 %shard_map.59 = bf16[16,2,1,128,128]{4,3,2,1,0:T(8,128)(2,1)} custom-call(bf16[2,1,128,128]{3,2,1,0:T(8,128)(2,1)S(1)} %get-tuple-element.145.refs_0_), custom_call_target="tpu_custom_call" | custom-call | tf_op jit(solution)/shard_map/pallas_call | solution.py:126
  155.8 1.5 fusion.84
  157.3 0.6 fusion.85
  (4 shorter events, 0.0 us)
Async XLA Ops:
  1.9 51.1 %copy-start.4 = (s32[1,16]{1,0:T(1,128)S(1)}, s32[1,16]{1,0:T(1,128)}, u32[]{:S(2)}) copy-start(s32[1,16]{1,0:T(1,128)} %refs_1_.1) | copy-start | bytes 196
  1.9 51.1 %copy-start.5 = (s32[1,16]{1,0:T(1,128)S(1)}, s32[1,16]{1,0:T(1,128)}, u32[]{:S(2)}) copy-start(s32[1,16]{1,0:T(1,128)} %param.15) | copy-start | bytes 196
  1.9 7.6 %copy-start.1 = (bf16[2,1,128,128]{3,2,1,0:T(8,128)(2,1)S(1)}, bf16[2,1,128,128]{3,2,1,0:T(8,128)(2,1)}, u32[]{:S(2)}) copy-start(bf16[2,1,128,128]{3,2,1,0:T(8,128)(2,1)} %get-tuple-element.108) | copy-start | bytes 196612 | tf_op jit(solution)/shard_map/cond
  53.0 52.7 %copy-start.3 = (bf16[1,1,1,128,128]{4,3,2,1,0:T(8,128)(2,1)S(1)}, bf16[1,1,1,128,128]{4,3,2,1,0:T(8,128)(2,1)}, u32[]{:S(2)}) copy-start(bf16[1,1,1,128,128]{4,3,2,1,0:T(8,128)(2,1)} %param.13) | copy-start | bytes 98308

commit v17 on v16

--- a/solution.py
+++ b/solution.py
@@ -140,9 +140,9 @@
 
 def node_up(tensor_here, left_env, right_env):
     first = jnp.einsum(
-        "xa,abp->xbp", left_env, tensor_here, preferred_element_type=jnp.float32
-    ).astype(jnp.bfloat16)
-    second = jnp.einsum("yb,xbp->xyp", right_env, first, preferred_element_type=jnp.float32).astype(
+        "abp,yb->ayp", tensor_here, right_env, preferred_element_type=jnp.float32
+    ).astype(jnp.bfloat16)
+    second = jnp.einsum("xa,ayp->xyp", left_env, first, preferred_element_type=jnp.float32).astype(
         jnp.bfloat16
     )
     return jnp.einsum(

time: 158 us -> 172 us (1.089)
  local copies, waits for them, and re-layouts: 1.6 us -> 9.01 us
  Pallas kernels: 133 us -> 139 us
  matrix products: 16.5 us -> 13.5 us
  loops' own time: 0.51 us -> 2.95 us
    dot_general x0 -> x1, local copies, waits for them, and re-layouts: none -> 6.91 us  [node_up(): jnp.einsum('xa,ayp->xyp', left_env, first, preferred_element_type=jnp.flo...]
    pallas_call x3, Pallas kernels: 133 us -> 139 us  [node_gather(): pl.pallas_call(functools.partial(gather_kernel, n, groups, shift, pieces,...]
    dot_general x1, matrix products: 8.89 us -> 4.71 us  [node_up(): jnp.einsum('xyq,xyp->qp', tensor_here, second, preferred_element_type=jnp...]
    another operation x1, loops' own time: 0.2 us -> 2.48 us  [local(): mid_up = lax.cond(is_mid, mid_work, lambda: zero_envs)]
    dot_general x1 -> x2, matrix products: 7.6 us -> 8.78 us  [the longest x1 5.3 us: node_up(): jnp.einsum('xa,ayp->xyp', left_env, first, preferred_element_type=jnp.flo...]
where the time goes in v17:
time: 172 us; the launch traced here: 171 us
  Pallas kernels  139 us (81%)
  matrix products  13.5 us (8%)
  local copies, waits for them, and re-layouts  9.01 us (5%)
  between operations  3.4 us (2%)
  other arithmetic  3.03 us (2%)
  loops' own time  2.95 us (2%)
    pallas_call x3, Pallas kernels, node_gather(): pl.pallas_call(functools.partial(gather_kernel, n, groups, shift, pieces,...  139 us
    dot_general x1, local copies, waits for them, and re-layouts, node_up(): jnp.einsum('xa,ayp->xyp', left_env, first, preferred_element_type=jnp.flo...  6.91 us
    dot_general x1, matrix products, node_up(): jnp.einsum('xa,ayp->xyp', left_env, first, preferred_element_type=jnp.flo...  5.3 us
    dot_general x1, matrix products, node_up(): jnp.einsum('xyq,xyp->qp', tensor_here, second, preferred_element_type=jnp...  4.71 us
    dot_general x1, matrix products, node_up(): jnp.einsum('abp,yb->ayp', tensor_here, right_env, preferred_element_type=...  3.48 us

profile of v17, /device:TPU:24, one launch (start us, length us, event | category | flops | bytes accessed | tf_op | source)
XLA Modules:
  0.0 170.7 jit_solution(12333305358418797972)
XLA Ops:
  0.0 1.2 constant_dynamic-slice_fusion.2
  1.9 0.0 copy-start.4
  1.9 0.0 copy-start.5
  1.9 0.2 conditional.3
  2.1 59.3 %shard_map.57 = bf16[16,1,128,128]{3,2,1,0:T(8,128)(2,1)S(1)} custom-call(bf16[1,128,128]{2,1,0:T(8,128)(2,1)S(1)} %get-tuple-element.131.refs_0_), custom_call_target="tpu_custom_call" | custom-call | tf_op jit(solution)/shard_map/pallas_call | solution.py:126
  63.4 0.0 copy-done.4
  63.4 0.0 copy-done.5
  63.4 0.0 copy-start.3
  63.4 23.8 %conditional.4 = (bf16[1,128,128]{1,2,0:T(8,128)(2,1)S(1)}) conditional(s32[]{:T(128)} %convert_element_type.186, () %tuple.27, (s32[]{:T(128)}, s32[1,16]{1,0:T(1,128)S(1)}, s32[1,16]{1,0:T(1,128)S(1)}, bf16[16,1,128,128]{3,2,1,0:T(8,128)(2,1)S(1)}, bf16[2,1,128,128]{3,2,1,0:T(8,128)(2,1)}, /*index=5*/bf16[128,128,128]{2,1,0:T(8,128)(2,1)}) %tuple.53), branch_computations={%region_2.3_spmd, %region_3.6_spmd} | conditional | flops 1611939840 | bytes 34571108 | solution.py:216
  63.4 0.6 constant_dynamic-slice_fusion
  65.3 0.3 fusion.34
  66.2 0.0 copy-start.2
  66.2 3.5 %fusion.36 = bf16[128,128,128]{2,0,1:T(8,128)(2,1)S(1)} fusion(bf16[128,128,128]{2,1,0:T(8,128)(2,1)} %get-tuple-element.115, bf16[2,1,128,128]{3,2,1,0:T(8,128)(2,1)} %get-tuple-element.114, bf16[128,128]{1,0:T(8,128)(2,1)S(1)} %get-tuple-element.133, pred[]{:T(512)} %bitcast.14), kind=kOutput, calls=%fused_computation.26 | convolution fusion | flops 536887296 | bytes 8454656 | tf_op jit(solution)/shard_map/cond/branch_1_fun/abp,yb->ayp/dot_general | solution.py:142
  70.2 0.0 copy-done.2
  70.2 5.3 %fusion.21 = bf16[128,128,128]{2,0,1:T(8,128)(2,1)} fusion(bf16[128,128,128]{2,0,1:T(8,128)(2,1)S(1)} %fusion.36, bf16[2,1,128,128]{3,2,1,0:T(8,128)(2,1)S(1)} %copy-done.2, bf16[128,128]{1,0:T(8,128)(2,1)S(1)} %get-tuple-element.132, pred[]{:T(512)} %bitcast.9), kind=kOutput, calls=%fused_computation.16 | convolution fusion | flops 536887296 | bytes 8454145 | tf_op jit(solution)/shard_map/cond/branch_1_fun/xa,ayp->xyp/dot_general | solution.py:145
  75.5 6.9 %copy.18 = bf16[128,128,128]{1,2,0:T(8,128)(2,1)} copy(bf16[128,128,128]{2,0,1:T(8,128)(2,1)} %fusion.21) | data formatting | bytes 8388608 | tf_op jit(solution)/shard_map/cond/branch_1_fun/xa,ayp->xyp/dot_general | solution.py:145
  82.5 4.7 %fusion.31 = bf16[1,128,128]{1,2,0:T(8,128)(2,1)S(1)} fusion(bf16[128,128,128]{2,1,0:T(8,128)(2,1)} %get-tuple-element.115, bf16[128,128,128]{1,2,0:T(8,128)(2,1)} %copy.18), kind=kOutput, calls=%fused_computation.23 | convolution fusion | flops 536887296 | bytes 8421376 | tf_op jit(solution)/shard_map/cond/branch_1_fun/xyq,xyp->qp/dot_general | solution.py:148
  87.2 0.1 copy.12
  87.3 0.6 pad_maximum_fusion.1.refs_0_
  87.9 30.0 %shard_map.58 = (bf16[16,2,1,128,128]{4,3,2,1,0:T(8,128)(2,1)S(1)}, s32[2,1,16]{2,1,0:T(1,128)S(1)}) custom-call(bf16[2,1,128,128]{3,2,1,0:T(8,128)(2,1)} %pad_maximum_fusion.1.refs_0_, s32[1,16]{1,0:T(1,128)S(1)} %copy-done.4), custom_call_target="tpu_custom_call" | custom-call | tf_op jit(solution)/shard_map/pallas_call | solution.py:126
  117.9 0.1 broadcast_in_dim.57
  118.6 0.0 copy-done.3
  118.7 0.3 conditional.5
  118.9 49.6 %shard_map.59 = bf16[16,2,1,128,128]{4,3,2,1,0:T(8,128)(2,1)} custom-call(bf16[2,1,128,128]{3,2,1,0:T(8,128)(2,1)S(1)} %get-tuple-element.145.refs_0_), custom_call_target="tpu_custom_call" | custom-call | tf_op jit(solution)/shard_map/pallas_call | solution.py:126
  168.6 1.5 fusion.79
  170.1 0.6 fusion.80
  (5 shorter events, 0.0 us)
Async XLA Ops:
  1.9 61.5 %copy-start.4 = (s32[1,16]{1,0:T(1,128)S(1)}, s32[1,16]{1,0:T(1,128)}, u32[]{:S(2)}) copy-start(s32[1,16]{1,0:T(1,128)} %refs_1_.1) | copy-start | bytes 196
  1.9 61.5 %copy-start.5 = (s32[1,16]{1,0:T(1,128)S(1)}, s32[1,16]{1,0:T(1,128)}, u32[]{:S(2)}) copy-start(s32[1,16]{1,0:T(1,128)} %param.15) | copy-start | bytes 196
  63.4 55.3 %copy-start.3 = (bf16[1,1,1,128,128]{4,3,2,1,0:T(8,128)(2,1)S(1)}, bf16[1,1,1,128,128]{4,3,2,1,0:T(8,128)(2,1)}, u32[]{:S(2)}) copy-start(bf16[1,1,1,128,128]{4,3,2,1,0:T(8,128)(2,1)} %param.13) | copy-start | bytes 98308
  66.2 4.1 %copy-start.2 = (bf16[2,1,128,128]{3,2,1,0:T(8,128)(2,1)S(1)}, bf16[2,1,128,128]{3,2,1,0:T(8,128)(2,1)}, u32[]{:S(2)}) copy-start(bf16[2,1,128,128]{3,2,1,0:T(8,128)(2,1)} %get-tuple-element.114) | copy-start | bytes 196612 | tf_op jit(solution)/shard_map/cond

commit v18 on v16

--- a/solution.py
+++ b/solution.py
@@ -229,10 +229,11 @@
         is_top, top_work, lambda: jnp.zeros((2, TERMS, bond_size, bond_size), jnp.bfloat16)
     )
     every_top = node_gather(top_down, 2, 1, pieces=2)
-    own_field = pick(every_top[:, 0], group_roles == jnp.clip(mid_index, 0, top_count - 1))
-    other_field = pick(every_top[:, 1], prev_roles[0] == jnp.clip(mid_index - top_count, 0, top_count - 1))
-    mid_field = jnp.where(mid_index < top_count, own_field, other_field)
-    result = jnp.where(is_mid, mid_field, jnp.where(is_leaf, leaf_up, zero_envs))
+    own_hit = jnp.logical_and(mid_index < top_count, group_roles == mid_index)
+    other_hit = jnp.logical_and(mid_index >= top_count, prev_roles[0] == mid_index - top_count)
+    hits = jnp.logical_and(is_mid, jnp.stack([own_hit, other_hit], axis=1))
+    mid_field = pick(every_top.reshape((-1,) + every_top.shape[2:]), hits.reshape(-1))
+    result = jnp.where(is_leaf, leaf_up, mid_field)
     return result[None, None]
 
 

time: 158 us -> 159 us (level)
  Pallas kernels: 133 us -> 130 us
  other arithmetic: 2.76 us -> 5.51 us
  loops' own time: 0.51 us -> 2.87 us
    pallas_call x3, Pallas kernels: 133 us -> 130 us  [node_gather(): pl.pallas_call(functools.partial(gather_kernel, n, groups, shift, pieces,...]
    another operation x1, loops' own time: 0.2 us -> 2.58 us  [local(): mid_up = lax.cond(is_mid, mid_work, lambda: zero_envs)]
where the time goes in v18:
time: 159 us
  Pallas kernels  130 us (82%)
  matrix products  16.3 us (10%)
  other arithmetic  5.51 us (3%)
  between operations  3.26 us (2%)
  loops' own time  2.87 us (2%)
    pallas_call x3, Pallas kernels, node_gather(): pl.pallas_call(functools.partial(gather_kernel, n, groups, shift, pieces,...  130 us
    dot_general x1, matrix products, node_up(): jnp.einsum('xyq,xyp->qp', tensor_here, second, preferred_element_type=jnp...  8.78 us
    dot_general x1, matrix products, node_up(): jnp.einsum('xa,abp->xbp', left_env, tensor_here, preferred_element_type=j...  7.54 us

profile of v18, /device:TPU:24, one launch (start us, length us, event | category | flops | bytes accessed | tf_op | source)
XLA Modules:
  0.0 158.9 jit_solution(17429790894406009664)
XLA Ops:
  0.0 1.2 fusion.84
  4.4 0.7 and_bitcast_fusion.1
  5.1 0.0 copy-start.4
  5.1 0.0 copy-start.5
  5.1 50.0 %shard_map.58 = bf16[16,1,128,128]{3,2,1,0:T(8,128)(2,1)S(1)} custom-call(bf16[1,128,128]{2,1,0:T(8,128)(2,1)S(1)} %get-tuple-element.149.refs_0_), custom_call_target="tpu_custom_call" | custom-call | tf_op jit(solution)/shard_map/pallas_call | solution.py:126
  55.1 0.0 copy-done.4
  55.1 0.0 copy-done.5
  55.1 0.0 copy-start.3
  55.2 19.8 %conditional.4 = (bf16[1,128,128]{1,2,0:T(8,128)(2,1)S(1)}) conditional(s32[]{:T(128)} %convert_element_type.154, () %tuple.28, (s32[]{:T(128)}, s32[1,16]{1,0:T(1,128)S(1)}, s32[1,16]{1,0:T(1,128)S(1)}, bf16[16,1,128,128]{3,2,1,0:T(8,128)(2,1)S(1)}, bf16[2,1,128,128]{3,2,1,0:T(8,128)(2,1)}, /*index=5*/bf16[128,128,128]{2,1,0:T(8,128)(2,1)}) %tuple.56), branch_computations={%region_2.3_spmd, %region_3.6_spmd} | conditional | flops 1614036992 | bytes 17793892 | solution.py:216
  55.4 0.6 constant_dynamic-slice_fusion.1
  58.4 0.3 fusion.37
  58.6 0.0 copy-start.2
  58.6 7.5 %fusion.24 = bf16[128,128,128]{2,0,1:T(8,128)(2,1)} fusion(bf16[128,128,128]{2,1,0:T(8,128)(2,1)} %get-tuple-element.111, bf16[2,1,128,128]{3,2,1,0:T(8,128)(2,1)} %get-tuple-element.110, bf16[128,128]{1,0:T(8,128)(2,1)S(1)} %get-tuple-element.151, pred[]{:T(512)} %bitcast.8), kind=kOutput, calls=%fused_computation.18 | convolution fusion | flops 536887296 | bytes 8454656 | tf_op jit(solution)/shard_map/cond/branch_1_fun/xa,abp->xbp/dot_general | solution.py:142
  66.2 0.0 copy-done.2
  66.2 8.8 %fusion.33 = bf16[1,128,128]{1,2,0:T(8,128)(2,1)S(1)} fusion(bf16[128,128,128]{2,1,0:T(8,128)(2,1)} %get-tuple-element.111, bf16[128,128,128]{2,0,1:T(8,128)(2,1)} %fusion.24, bf16[2,1,128,128]{3,2,1,0:T(8,128)(2,1)S(1)} %copy-done.2, bf16[128,128]{1,0:T(8,128)(2,1)S(1)} %get-tuple-element.150, pred[]{:T(512)} %bitcast.13), kind=kOutput, calls=%fused_computation.25 | convolution fusion | flops 1075871744 | bytes 8486913 | tf_op jit(solution)/shard_map/cond/branch_1_fun/xyq,xyp->qp/dot_general | solution.py:148
  75.0 0.1 copy.18
  75.1 0.6 pad_maximum_fusion.1.refs_0_
  75.7 29.0 %shard_map.59 = (bf16[16,2,1,128,128]{4,3,2,1,0:T(8,128)(2,1)S(1)}, s32[2,1,16]{2,1,0:T(1,128)S(1)}) custom-call(bf16[2,1,128,128]{3,2,1,0:T(8,128)(2,1)} %pad_maximum_fusion.1.refs_0_, s32[1,16]{1,0:T(1,128)S(1)} %copy-done.4), custom_call_target="tpu_custom_call" | custom-call | tf_op jit(solution)/shard_map/pallas_call | solution.py:126
  104.8 0.0 copy-done.3
  104.8 0.3 conditional.5
  105.1 0.1 copy.19
  105.2 51.1 %shard_map.60 = bf16[16,2,1,128,128]{4,3,2,1,0:T(8,128)(2,1)} custom-call(bf16[2,1,128,128]{3,2,1,0:T(8,128)(2,1)S(1)} %get-tuple-element.163.refs_0_), custom_call_target="tpu_custom_call" | custom-call | tf_op jit(solution)/shard_map/pallas_call | solution.py:126
  156.2 1.5 select_reduce_fusion
  157.7 1.2 fusion.83
  (6 shorter events, 0.1 us)
Async XLA Ops:
  5.1 50.1 %copy-start.4 = (s32[1,16]{1,0:T(1,128)S(1)}, s32[1,16]{1,0:T(1,128)}, u32[]{:S(2)}) copy-start(s32[1,16]{1,0:T(1,128)} %refs_1_.1) | copy-start | bytes 196
  5.1 50.1 %copy-start.5 = (s32[1,16]{1,0:T(1,128)S(1)}, s32[1,16]{1,0:T(1,128)}, u32[]{:S(2)}) copy-start(s32[1,16]{1,0:T(1,128)} %param.15) | copy-start | bytes 196
  55.1 49.6 %copy-start.3 = (bf16[1,1,1,128,128]{4,3,2,1,0:T(8,128)(2,1)S(1)}, bf16[1,1,1,128,128]{4,3,2,1,0:T(8,128)(2,1)}, u32[]{:S(2)}) copy-start(bf16[1,1,1,128,128]{4,3,2,1,0:T(8,128)(2,1)} %param.13) | copy-start | bytes 98308
  58.6 7.6 %copy-start.2 = (bf16[2,1,128,128]{3,2,1,0:T(8,128)(2,1)S(1)}, bf16[2,1,128,128]{3,2,1,0:T(8,128)(2,1)}, u32[]{:S(2)}) copy-start(bf16[2,1,128,128]{3,2,1,0:T(8,128)(2,1)} %get-tuple-element.110) | copy-start | bytes 196612 | tf_op jit(solution)/shard_map/cond

commit v19 on v16

--- a/solution.py
+++ b/solution.py
@@ -214,7 +214,7 @@
         return jnp.stack([node_up(tensor_here, child_envs[0][0], child_envs[1][0])])
 
     mid_up = lax.cond(is_mid, mid_work, lambda: zero_envs)
-    every_mid, near_roles = node_gather(jnp.stack([mid_up, mid_up]), 1, -1, role_map, pieces=2)
+    every_mid, near_roles = node_gather(jnp.stack([mid_up, mid_up]), 1, -1, role_map, pieces=1)
     next_roles = near_roles[0]
     prev_roles = near_roles[1]
     top_index = jnp.clip(my_role, 0, top_count - 1)
@@ -228,7 +228,7 @@
     top_down = lax.cond(
         is_top, top_work, lambda: jnp.zeros((2, TERMS, bond_size, bond_size), jnp.bfloat16)
     )
-    every_top = node_gather(top_down, 2, 1, pieces=2)
+    every_top = node_gather(top_down, 2, 1, pieces=1)
     own_field = pick(every_top[:, 0], group_roles == jnp.clip(mid_index, 0, top_count - 1))
     other_field = pick(every_top[:, 1], prev_roles[0] == jnp.clip(mid_index - top_count, 0, top_count - 1))
     mid_field = jnp.where(mid_index < top_count, own_field, other_field)

time: 158 us -> 159 us (level)
  Pallas kernels: 133 us -> 130 us
  loops' own time: 0.51 us -> 2.81 us
    pallas_call x3, Pallas kernels: 133 us -> 130 us  [node_gather(): pl.pallas_call(functools.partial(gather_kernel, n, groups, shift, pieces,...]
    another operation x1, loops' own time: 0.2 us -> 2.51 us  [local(): mid_up = lax.cond(is_mid, mid_work, lambda: zero_envs)]
where the time goes in v19:
time: 159 us; the launch traced here: 158 us
  Pallas kernels  130 us (82%)
  matrix products  16.3 us (10%)
  between operations  3.4 us (2%)
  other arithmetic  3.03 us (2%)
  loops' own time  2.81 us (2%)
  local copies, waits for them, and re-layouts  2.07 us (1%)
    pallas_call x3, Pallas kernels, node_gather(): pl.pallas_call(functools.partial(gather_kernel, n, groups, shift, pieces,...  130 us
    dot_general x1, matrix products, node_up(): jnp.einsum('xyq,xyp->qp', tensor_here, second, preferred_element_type=jnp...  8.78 us
    dot_general x1, matrix products, node_up(): jnp.einsum('xa,abp->xbp', left_env, tensor_here, preferred_element_type=j...  7.54 us

profile of v19, /device:TPU:24, one launch (start us, length us, event | category | flops | bytes accessed | tf_op | source)
XLA Modules:
  0.0 157.5 jit_solution(10910508920925877523)
XLA Ops:
  0.0 1.2 constant_dynamic-slice_fusion.2
  1.9 0.0 copy-start.4
  1.9 0.0 copy-start.5
  1.9 50.2 %shard_map.57 = bf16[16,1,128,128]{3,2,1,0:T(8,128)(2,1)S(1)} custom-call(bf16[1,128,128]{2,1,0:T(8,128)(2,1)S(1)} %get-tuple-element.131.refs_0_), custom_call_target="tpu_custom_call" | custom-call | tf_op jit(solution)/shard_map/pallas_call | solution.py:126
  54.1 0.0 copy-done.4
  54.1 0.0 copy-done.5
  54.1 0.0 copy-start.3
  54.1 19.7 %conditional.4 = (bf16[1,128,128]{1,2,0:T(8,128)(2,1)S(1)}) conditional(s32[]{:T(128)} %convert_element_type.183, () %tuple.27, (s32[]{:T(128)}, s32[1,16]{1,0:T(1,128)S(1)}, s32[1,16]{1,0:T(1,128)S(1)}, bf16[16,1,128,128]{3,2,1,0:T(8,128)(2,1)S(1)}, bf16[2,1,128,128]{3,2,1,0:T(8,128)(2,1)}, /*index=5*/bf16[128,128,128]{2,1,0:T(8,128)(2,1)}) %tuple.53), branch_computations={%region_2.3_spmd, %region_3.6_spmd} | conditional | flops 1614036992 | bytes 17793892 | solution.py:216
  54.3 0.6 constant_dynamic-slice_fusion.1
  56.1 0.3 fusion.37
  56.9 0.0 copy-start.2
  56.9 7.5 %fusion.24 = bf16[128,128,128]{2,0,1:T(8,128)(2,1)} fusion(bf16[128,128,128]{2,1,0:T(8,128)(2,1)} %get-tuple-element.115, bf16[2,1,128,128]{3,2,1,0:T(8,128)(2,1)} %get-tuple-element.114, bf16[128,128]{1,0:T(8,128)(2,1)S(1)} %get-tuple-element.133, pred[]{:T(512)} %bitcast.8), kind=kOutput, calls=%fused_computation.18 | convolution fusion | flops 536887296 | bytes 8454656 | tf_op jit(solution)/shard_map/cond/branch_1_fun/xa,abp->xbp/dot_general | solution.py:142
  65.0 0.0 copy-done.2
  65.0 8.8 %fusion.33 = bf16[1,128,128]{1,2,0:T(8,128)(2,1)S(1)} fusion(bf16[128,128,128]{2,1,0:T(8,128)(2,1)} %get-tuple-element.115, bf16[128,128,128]{2,0,1:T(8,128)(2,1)} %fusion.24, bf16[2,1,128,128]{3,2,1,0:T(8,128)(2,1)S(1)} %copy-done.2, bf16[128,128]{1,0:T(8,128)(2,1)S(1)} %get-tuple-element.132, pred[]{:T(512)} %bitcast.13), kind=kOutput, calls=%fused_computation.25 | convolution fusion | flops 1075871744 | bytes 8486913 | tf_op jit(solution)/shard_map/cond/branch_1_fun/xyq,xyp->qp/dot_general | solution.py:148
  73.8 0.1 copy.12
  74.0 0.6 pad_maximum_fusion.1.refs_0_
  74.6 29.9 %shard_map.58 = (bf16[16,2,1,128,128]{4,3,2,1,0:T(8,128)(2,1)S(1)}, s32[2,1,16]{2,1,0:T(1,128)S(1)}) custom-call(bf16[2,1,128,128]{3,2,1,0:T(8,128)(2,1)} %pad_maximum_fusion.1.refs_0_, s32[1,16]{1,0:T(1,128)S(1)} %copy-done.4), custom_call_target="tpu_custom_call" | custom-call | tf_op jit(solution)/shard_map/pallas_call | solution.py:126
  104.5 0.1 broadcast_in_dim.57
  105.3 0.0 copy-done.3
  105.3 0.3 conditional.5
  105.6 49.8 %shard_map.59 = bf16[16,2,1,128,128]{4,3,2,1,0:T(8,128)(2,1)} custom-call(bf16[2,1,128,128]{3,2,1,0:T(8,128)(2,1)S(1)} %get-tuple-element.145.refs_0_), custom_call_target="tpu_custom_call" | custom-call | tf_op jit(solution)/shard_map/pallas_call | solution.py:126
  155.4 1.5 fusion.84
  156.9 0.6 fusion.85
  (6 shorter events, 0.1 us)
Async XLA Ops:
  1.9 52.2 %copy-start.4 = (s32[1,16]{1,0:T(1,128)S(1)}, s32[1,16]{1,0:T(1,128)}, u32[]{:S(2)}) copy-start(s32[1,16]{1,0:T(1,128)} %refs_1_.1) | copy-start | bytes 196
  1.9 52.2 %copy-start.5 = (s32[1,16]{1,0:T(1,128)S(1)}, s32[1,16]{1,0:T(1,128)}, u32[]{:S(2)}) copy-start(s32[1,16]{1,0:T(1,128)} %param.15) | copy-start | bytes 196
  54.1 51.1 %copy-start.3 = (bf16[1,1,1,128,128]{4,3,2,1,0:T(8,128)(2,1)S(1)}, bf16[1,1,1,128,128]{4,3,2,1,0:T(8,128)(2,1)}, u32[]{:S(2)}) copy-start(bf16[1,1,1,128,128]{4,3,2,1,0:T(8,128)(2,1)} %param.13) | copy-start | bytes 98308
  56.9 8.1 %copy-start.2 = (bf16[2,1,128,128]{3,2,1,0:T(8,128)(2,1)S(1)}, bf16[2,1,128,128]{3,2,1,0:T(8,128)(2,1)}, u32[]{:S(2)}) copy-start(bf16[2,1,128,128]{3,2,1,0:T(8,128)(2,1)} %get-tuple-element.114) | copy-start | bytes 196612 | tf_op jit(solution)/shard_map/cond

commit v20 on v16

--- a/solution.py
+++ b/solution.py
@@ -202,7 +202,7 @@
         return jnp.stack([node_up(tensor_here, outer_envs[0, 0], outer_envs[1, 0])])
 
     leaf_up = lax.cond(is_leaf, leaf_work, lambda: zero_envs)
-    every_leaf = node_gather(leaf_up, 0, pieces=2)
+    every_leaf = node_gather(leaf_up, 0, pieces=1)
     mid_index = jnp.clip(my_role - top_count, 0, mid_count - 1)
 
     def mid_work():

time: 158 us -> 159 us (level)
  Pallas kernels: 133 us -> 131 us
    pallas_call x3, Pallas kernels: 133 us -> 131 us  [node_gather(): pl.pallas_call(functools.partial(gather_kernel, n, groups, shift, pieces,...]
    dot_general x2 -> x5, matrix products: 16.5 us -> 17.3 us  [the longest x1 4.65 us: node_down(): jnp.einsum('xbq,abq->xa', right_part, weighted, preferred_element_type=jn...]
where the time goes in v20:
time: 159 us; the launch traced here: 158 us
  Pallas kernels  131 us (82%)
  matrix products  17.3 us (11%)
  between operations  3.4 us (2%)
  other arithmetic  3.09 us (2%)
    pallas_call x3, Pallas kernels, node_gather(): pl.pallas_call(functools.partial(gather_kernel, n, groups, shift, pieces,...  131 us
    dot_general x1, matrix products, node_down(): jnp.einsum('xbq,abq->xa', right_part, weighted, preferred_element_type=jn...  4.65 us
    dot_general x1, matrix products, node_down(): jnp.einsum('ayq,abq->yb', left_part, weighted, preferred_element_type=jnp...  4.41 us
    dot_general x1, matrix products, node_down(): jnp.einsum('xyq,yb->xbq', tensor_here, right_env, preferred_element_type=...  3.61 us
    dot_general x1, matrix products, node_down(): jnp.einsum('xyq,xa->ayq', tensor_here, left_env, preferred_element_type=j...  3.39 us

profile of v20, /device:TPU:24, one launch (start us, length us, event | category | flops | bytes accessed | tf_op | source)
XLA Modules:
  0.0 158.0 jit_solution(5444891711950788036)
XLA Ops:
  0.0 1.2 constant_dynamic-slice_fusion.2
  1.9 0.0 copy-start.4
  1.9 0.0 copy-start.5
  1.9 48.7 %shard_map.57 = bf16[16,1,128,128]{3,2,1,0:T(8,128)(2,1)S(1)} custom-call(bf16[1,128,128]{2,1,0:T(8,128)(2,1)S(1)} %get-tuple-element.131.refs_0_), custom_call_target="tpu_custom_call" | custom-call | tf_op jit(solution)/shard_map/pallas_call | solution.py:126
  52.6 0.0 copy-done.4
  52.6 0.0 copy-done.5
  52.7 0.0 copy-start.3
  52.7 0.2 conditional.4
  52.9 0.1 copy.12
  53.0 0.6 pad_maximum_fusion.1.refs_0_
  53.6 50.7 %shard_map.58 = (bf16[16,2,1,128,128]{4,3,2,1,0:T(8,128)(2,1)S(1)}, s32[2,1,16]{2,1,0:T(1,128)S(1)}) custom-call(bf16[2,1,128,128]{3,2,1,0:T(8,128)(2,1)} %pad_maximum_fusion.1.refs_0_, s32[1,16]{1,0:T(1,128)S(1)} %copy-done.4), custom_call_target="tpu_custom_call" | custom-call | tf_op jit(solution)/shard_map/pallas_call | solution.py:126
  104.4 0.1 broadcast_in_dim.57
  105.1 0.0 copy-done.3
  105.2 18.9 %conditional.5 = (bf16[2,1,128,128]{3,2,1,0:T(8,128)(2,1)S(1)}) conditional(s32[]{:T(128)} %convert_element_type.182, () %tuple.26, (s32[2,1,16]{2,1,0:T(1,128)S(1)}, s32[]{:T(128)}, bf16[16,2,1,128,128]{4,3,2,1,0:T(8,128)(2,1)S(1)}, f32[16,1,128,128]{3,2,0,1:T(8,128)S(1)}, bf16[128,128,128]{2,1,0:T(8,128)(2,1)}, ...), branch_computations={%region_6.7_spmd, %region_7.10_spmd} | conditional | flops 2688057344 | bytes 61178140 | solution.py:228
  106.1 0.3 fusion.76
  106.4 0.0 copy-start
  106.5 3.6 %fusion.79 = bf16[128,128,128]{2,0,1:T(8,128)(2,1)S(1)} fusion(bf16[128,128,128]{2,1,0:T(8,128)(2,1)} %get-tuple-element.120, bf16[128,128]{1,0:T(8,128)(2,1)S(1)} %get-tuple-element.134), kind=kOutput, calls=%fused_computation.66 | convolution fusion | flops 536870912 | bytes 8421376 | tf_op jit(solution)/shard_map/cond/branch_1_fun/xyq,yb->xbq/dot_general | solution.py:157
  110.1 0.0 copy-done
  110.1 1.3 convolution_convert_fusion
  111.3 4.6 %fusion.70 = bf16[1,1,128,128]{3,2,1,0:T(8,128)(2,1)S(1)} fusion(bf16[128,128,128]{2,1,0:T(8,128)(2,1)S(1)} %convolution_convert_fusion, bf16[128,128,128]{2,0,1:T(8,128)(2,1)S(1)} %fusion.79), kind=kOutput, calls=%fused_computation.56 | convolution fusion | flops 536887296 | bytes 8421376 | tf_op jit(solution)/shard_map/cond/branch_1_fun/xbq,abq->xa/dot_general | solution.py:163
  116.0 3.4 %fusion.54 = bf16[128,128,128]{2,0,1:T(8,128)(2,1)S(1)} fusion(bf16[128,128,128]{2,1,0:T(8,128)(2,1)S(1)} %copy-done, bf16[128,128]{1,0:T(8,128)(2,1)S(1)} %get-tuple-element.135), kind=kOutput, calls=%fused_computation.47 | convolution fusion | flops 536870912 | bytes 8421376 | tf_op jit(solution)/shard_map/cond/branch_1_fun/xyq,xa->ayq/dot_general | solution.py:160
  119.4 4.4 %fusion.69 = bf16[1,1,128,128]{3,2,1,0:T(8,128)(2,1)S(1)} fusion(bf16[128,128,128]{2,1,0:T(8,128)(2,1)S(1)} %convolution_convert_fusion, bf16[128,128,128]{2,0,1:T(8,128)(2,1)S(1)} %fusion.54), kind=kOutput, calls=%fused_computation.55 | convolution fusion | flops 536887296 | bytes 8421376 | tf_op jit(solution)/shard_map/cond/branch_1_fun/ayq,abq->yb/dot_general | solution.py:166
  124.1 31.7 %shard_map.59 = bf16[16,2,1,128,128]{4,3,2,1,0:T(8,128)(2,1)} custom-call(bf16[2,1,128,128]{3,2,1,0:T(8,128)(2,1)S(1)} %get-tuple-element.145.refs_0_), custom_call_target="tpu_custom_call" | custom-call | tf_op jit(solution)/shard_map/pallas_call | solution.py:126
  155.8 1.5 fusion.84
  157.3 0.6 fusion.85
  (8 shorter events, 0.1 us)
Async XLA Ops:
  1.9 50.8 %copy-start.4 = (s32[1,16]{1,0:T(1,128)S(1)}, s32[1,16]{1,0:T(1,128)}, u32[]{:S(2)}) copy-start(s32[1,16]{1,0:T(1,128)} %refs_1_.1) | copy-start | bytes 196
  1.9 50.7 %copy-start.5 = (s32[1,16]{1,0:T(1,128)S(1)}, s32[1,16]{1,0:T(1,128)}, u32[]{:S(2)}) copy-start(s32[1,16]{1,0:T(1,128)} %param.15) | copy-start | bytes 196
  52.7 52.5 %copy-start.3 = (bf16[1,1,1,128,128]{4,3,2,1,0:T(8,128)(2,1)S(1)}, bf16[1,1,1,128,128]{4,3,2,1,0:T(8,128)(2,1)}, u32[]{:S(2)}) copy-start(bf16[1,1,1,128,128]{4,3,2,1,0:T(8,128)(2,1)} %param.13) | copy-start | bytes 98308
  106.4 3.6 %copy-start = (bf16[128,128,128]{2,1,0:T(8,128)(2,1)S(1)}, bf16[128,128,128]{2,1,0:T(8,128)(2,1)}, u32[]{:S(2)}) copy-start(bf16[128,128,128]{2,1,0:T(8,128)(2,1)} %get-tuple-element.120) | copy-start | bytes 12582916 | tf_op jit(solution)/shard_map/cond

commit v21 on v16

--- a/solution.py
+++ b/solution.py
@@ -134,7 +134,7 @@
             pltpu.SemaphoreType.DMA,
             pltpu.SemaphoreType.DMA((6,)),
         ],
-        compiler_params=pltpu.CompilerParams(collective_id=collective_id, has_side_effects=True),
+        compiler_params=pltpu.CompilerParams(collective_id=collective_id),
     )(*operands)
 
 

time: 158 us -> 158 us (level)
  Pallas kernels: 133 us -> 131 us
    pallas_call x3, Pallas kernels: 133 us -> 131 us  [node_gather(): pl.pallas_call(functools.partial(gather_kernel, n, groups, shift, pieces,...]
    dot_general x2 -> x5, matrix products: 16.5 us -> 17.3 us  [the longest x1 4.65 us: node_down(): jnp.einsum('xbq,abq->xa', right_part, weighted, preferred_element_type=jn...]
where the time goes in v21:
time: 158 us; the launch traced here: 157 us
  Pallas kernels  131 us (83%)
  matrix products  17.3 us (11%)
  between operations  3.4 us (2%)
  other arithmetic  3.09 us (2%)
    pallas_call x3, Pallas kernels, node_gather(): pl.pallas_call(functools.partial(gather_kernel, n, groups, shift, pieces,...  131 us
    dot_general x1, matrix products, node_down(): jnp.einsum('xbq,abq->xa', right_part, weighted, preferred_element_type=jn...  4.65 us
    dot_general x1, matrix products, node_down(): jnp.einsum('ayq,abq->yb', left_part, weighted, preferred_element_type=jnp...  4.41 us
    dot_general x1, matrix products, node_down(): jnp.einsum('xyq,yb->xbq', tensor_here, right_env, preferred_element_type=...  3.61 us
    dot_general x1, matrix products, node_down(): jnp.einsum('xyq,xa->ayq', tensor_here, left_env, preferred_element_type=j...  3.39 us

profile of v21, /device:TPU:24, one launch (start us, length us, event | category | flops | bytes accessed | tf_op | source)
XLA Modules:
  0.0 157.3 jit_solution(9881136240358729920)
XLA Ops:
  0.0 1.2 constant_dynamic-slice_fusion.2
  1.9 0.0 copy-start.4
  1.9 0.0 copy-start.5
  1.9 50.1 %shard_map.57 = bf16[16,1,128,128]{3,2,1,0:T(8,128)(2,1)S(1)} custom-call(bf16[1,128,128]{2,1,0:T(8,128)(2,1)S(1)} %get-tuple-element.131.refs_0_), custom_call_target="tpu_custom_call" | custom-call | tf_op jit(solution)/shard_map/pallas_call | solution.py:126
  54.0 0.0 copy-done.4
  54.0 0.0 copy-done.5
  54.1 0.0 copy-start.3
  54.1 0.2 conditional.4
  54.3 0.1 copy.12
  54.4 0.6 pad_maximum_fusion.1.refs_0_
  55.0 49.6 %shard_map.58 = (bf16[16,2,1,128,128]{4,3,2,1,0:T(8,128)(2,1)S(1)}, s32[2,1,16]{2,1,0:T(1,128)S(1)}) custom-call(bf16[2,1,128,128]{3,2,1,0:T(8,128)(2,1)} %pad_maximum_fusion.1.refs_0_, s32[1,16]{1,0:T(1,128)S(1)} %copy-done.4), custom_call_target="tpu_custom_call" | custom-call | tf_op jit(solution)/shard_map/pallas_call | solution.py:126
  104.7 0.1 broadcast_in_dim.57
  105.4 0.0 copy-done.3
  105.4 18.9 %conditional.5 = (bf16[2,1,128,128]{3,2,1,0:T(8,128)(2,1)S(1)}) conditional(s32[]{:T(128)} %convert_element_type.182, () %tuple.26, (s32[2,1,16]{2,1,0:T(1,128)S(1)}, s32[]{:T(128)}, bf16[16,2,1,128,128]{4,3,2,1,0:T(8,128)(2,1)S(1)}, f32[16,1,128,128]{3,2,0,1:T(8,128)S(1)}, bf16[128,128,128]{2,1,0:T(8,128)(2,1)}, ...), branch_computations={%region_6.7_spmd, %region_7.10_spmd} | conditional | flops 2688057344 | bytes 61178140 | solution.py:228
  106.4 0.3 fusion.76
  106.7 0.0 copy-start
  106.7 3.6 %fusion.79 = bf16[128,128,128]{2,0,1:T(8,128)(2,1)S(1)} fusion(bf16[128,128,128]{2,1,0:T(8,128)(2,1)} %get-tuple-element.120, bf16[128,128]{1,0:T(8,128)(2,1)S(1)} %get-tuple-element.134), kind=kOutput, calls=%fused_computation.66 | convolution fusion | flops 536870912 | bytes 8421376 | tf_op jit(solution)/shard_map/cond/branch_1_fun/xyq,yb->xbq/dot_general | solution.py:157
  110.3 0.0 copy-done
  110.3 1.3 convolution_convert_fusion
  111.6 4.6 %fusion.70 = bf16[1,1,128,128]{3,2,1,0:T(8,128)(2,1)S(1)} fusion(bf16[128,128,128]{2,1,0:T(8,128)(2,1)S(1)} %convolution_convert_fusion, bf16[128,128,128]{2,0,1:T(8,128)(2,1)S(1)} %fusion.79), kind=kOutput, calls=%fused_computation.56 | convolution fusion | flops 536887296 | bytes 8421376 | tf_op jit(solution)/shard_map/cond/branch_1_fun/xbq,abq->xa/dot_general | solution.py:163
  116.3 3.4 %fusion.54 = bf16[128,128,128]{2,0,1:T(8,128)(2,1)S(1)} fusion(bf16[128,128,128]{2,1,0:T(8,128)(2,1)S(1)} %copy-done, bf16[128,128]{1,0:T(8,128)(2,1)S(1)} %get-tuple-element.135), kind=kOutput, calls=%fused_computation.47 | convolution fusion | flops 536870912 | bytes 8421376 | tf_op jit(solution)/shard_map/cond/branch_1_fun/xyq,xa->ayq/dot_general | solution.py:160
  119.7 4.4 %fusion.69 = bf16[1,1,128,128]{3,2,1,0:T(8,128)(2,1)S(1)} fusion(bf16[128,128,128]{2,1,0:T(8,128)(2,1)S(1)} %convolution_convert_fusion, bf16[128,128,128]{2,0,1:T(8,128)(2,1)S(1)} %fusion.54), kind=kOutput, calls=%fused_computation.55 | convolution fusion | flops 536887296 | bytes 8421376 | tf_op jit(solution)/shard_map/cond/branch_1_fun/ayq,abq->yb/dot_general | solution.py:166
  124.4 30.8 %shard_map.59 = bf16[16,2,1,128,128]{4,3,2,1,0:T(8,128)(2,1)} custom-call(bf16[2,1,128,128]{3,2,1,0:T(8,128)(2,1)S(1)} %get-tuple-element.145.refs_0_), custom_call_target="tpu_custom_call" | custom-call | tf_op jit(solution)/shard_map/pallas_call | solution.py:126
  155.2 1.5 fusion.84
  156.7 0.6 fusion.85
  (8 shorter events, 0.1 us)
Async XLA Ops:
  1.9 52.2 %copy-start.4 = (s32[1,16]{1,0:T(1,128)S(1)}, s32[1,16]{1,0:T(1,128)}, u32[]{:S(2)}) copy-start(s32[1,16]{1,0:T(1,128)} %refs_1_.1) | copy-start | bytes 196
  1.9 52.1 %copy-start.5 = (s32[1,16]{1,0:T(1,128)S(1)}, s32[1,16]{1,0:T(1,128)}, u32[]{:S(2)}) copy-start(s32[1,16]{1,0:T(1,128)} %param.15) | copy-start | bytes 196
  54.1 51.4 %copy-start.3 = (bf16[1,1,1,128,128]{4,3,2,1,0:T(8,128)(2,1)S(1)}, bf16[1,1,1,128,128]{4,3,2,1,0:T(8,128)(2,1)}, u32[]{:S(2)}) copy-start(bf16[1,1,1,128,128]{4,3,2,1,0:T(8,128)(2,1)} %param.13) | copy-start | bytes 98308
  106.7 3.6 %copy-start = (bf16[128,128,128]{2,1,0:T(8,128)(2,1)S(1)}, bf16[128,128,128]{2,1,0:T(8,128)(2,1)}, u32[]{:S(2)}) copy-start(bf16[128,128,128]{2,1,0:T(8,128)(2,1)} %get-tuple-element.120) | copy-start | bytes 12582916 | tf_op jit(solution)/shard_map/cond
